TPU v7x, 512 devices: a whole 4x8x8 slice. The times are simulated.
512 devices in a mesh: chan: 16 (over x_lo, y), ctx: 32 (over z, x_hi, core).
Axes of the slice: x: 4 (x_hi: 2, x_lo: 2; x = x_hi * 2 + x_lo), y: 8, z: 8, core: 2. Of those that a mesh axis runs over, the one named last changes fastest.
Arguments:
- gate_stream: bfloat16 [8192, 4096], P('ctx', 'chan'), may hold values from -6 to 6
- key_stream: bfloat16 [8192, 4096], P('ctx', 'chan'), may hold values from -6 to 6
- value_stream: bfloat16 [8192, 4096], P('ctx', 'chan'), may hold values from -6 to 6
- residues: float32 [16, 4096], P(None, 'chan'), may hold values from -4 to 4
- decay_rates: float32 [16, 4096], P(None, 'chan'), may hold values from 2.4414062e-06 to 0.05
- out_weight: bfloat16 [4096, 4096], P('chan'), may hold values from -0.125 to 0.125
Outputs:
- projected: bfloat16 [8192, 4096], P('ctx', 'chan')
All inputs are finite; a program needn't handle non-finite values.
Results may differ from a plain program's by a relative error of at most 0.006.
Values sent between devices are 32-bit elements; how exact they have to be, the bound alone decides.
No kernel may reach another device: no remote copies, remote signals or barrier semaphores. Data moves between devices by JAX's collectives and lax.ppermute only.
A program may use at most 64 MiB of HBM per device.

v0:
```python
import math

import jax
import jax.numpy as jnp
from jax import lax
from jax.sharding import PartitionSpec as P

HIGH = lax.Precision.HIGHEST
TWO_PI = 2.0 * math.pi


def swapped(block, axis, distance):
    count = lax.axis_size(axis)
    route = []
    for low in range(count):
        high = low | 1 << distance
        if high != low and high < count:
            route += [(low, high), (high, low)]
    return lax.ppermute(block, axis, route)


def unit_circle(numer, denom):
    angle = TWO_PI * numer.astype(jnp.float32) / denom
    return (jnp.cos(angle), jnp.sin(angle))


def times(ar, ai, br, bi):
    return (ar * br - ai * bi, ar * bi + ai * br)


def dft_matrix(length, inverse):
    index = jnp.arange(length, dtype=jnp.int32)
    cosine, sine = unit_circle(index[:, None] * index[None, :] % length, length)
    if inverse:
        top = jnp.concatenate([cosine, sine], axis=1)
        bottom = jnp.concatenate([-sine, cosine], axis=1)
    else:
        top = jnp.concatenate([cosine, -sine], axis=1)
        bottom = jnp.concatenate([sine, cosine], axis=1)
    return jnp.concatenate([top, bottom], axis=0)


def along_time(real_part, imag_part, matrix):
    rows = real_part.shape[-1]
    stacked = jnp.concatenate([real_part, imag_part], axis=-1)
    result = jnp.dot(stacked, matrix, precision=HIGH)
    return (result[..., :rows], result[..., rows:])


def filter_terms(residues, decay_rates, length):
    lam = jnp.exp(-decay_rates)
    one_less = -jnp.expm1(-decay_rates)
    base = residues * jnp.sqrt(-jnp.expm1(-2.0 * decay_rates))
    tail = jnp.exp(-decay_rates * length)
    return (base, lam, one_less, tail)


def response(freq, total, filt):
    base, lam, one_less, tail = filt
    wrapped = freq % total
    cosine, sine = unit_circle(wrapped, total)
    half_sine = jnp.sin(math.pi * wrapped.astype(jnp.float32) / total)
    parity_sign = 1.0 - 2.0 * (wrapped % 2).astype(jnp.float32)
    resp_r = 0.0
    resp_i = 0.0
    for mode in range(base.shape[0]):
        numer = base[mode] * (1.0 - tail[mode] * parity_sign)
        den_r = one_less[mode] + 2.0 * lam[mode] * half_sine * half_sine
        den_i = lam[mode] * sine
        norm_sq = den_r * den_r + den_i * den_i
        resp_r = resp_r + numer * den_r / norm_sq
        resp_i = resp_i - numer * den_i / norm_sq
    return (resp_r, resp_i)


def spectral(spec_r, spec_i, q_index, filt, big_p, rows):
    total = 2 * big_p * rows
    fsel = jnp.arange(2, dtype=jnp.int32).reshape((2,) + (1,) * (spec_r.ndim - 1))
    freq = 2 * q_index + fsel
    pos = jnp.arange(rows, dtype=jnp.int32)
    cosine, sine = unit_circle(pos * freq % total, total)
    tw_r, tw_i = times(spec_r, spec_i, cosine, -sine)
    full_r, full_i = along_time(tw_r, tw_i, dft_matrix(rows, False))
    resp_r, resp_i = response(freq + 2 * big_p * pos, total, filt)
    prod_r, prod_i = times(full_r, full_i, resp_r, resp_i)
    back_r, back_i = along_time(prod_r, prod_i, dft_matrix(rows, True))
    return times(back_r, back_i, cosine, sine)


def pre_twiddle(mixed, p_index, big_p, shape_f):
    fsel = jnp.arange(2, dtype=jnp.int32).reshape(shape_f)
    cosine, sine = unit_circle(p_index * fsel % (2 * big_p), 2 * big_p)
    return (mixed * cosine, -mixed * sine)


def post_twiddle(spec_r, spec_i, p_index, big_p, rows, shape_f):
    fsel = jnp.arange(2, dtype=jnp.int32).reshape(shape_f)
    cosine, sine = unit_circle(p_index * fsel % (2 * big_p), 2 * big_p)
    return jnp.sum(cosine * spec_r - sine * spec_i, axis=0) / (2.0 * big_p * rows)


def reverse_bits(device, bits):
    result = jnp.zeros_like(device)
    for bit in range(bits):
        result = result | (device >> bit & 1) << bits - 1 - bit
    return result


def butterfly_forward(real_part, imag_part, device, bits):
    for bit in range(bits - 1, -1, -1):
        half = 1 << bit
        place = device % (2 * half)
        upper = place >= half
        other_r, other_i = swapped((real_part, imag_part), "ctx", bit)
        cosine, sine = unit_circle(jnp.where(upper, place - half, 0), 2 * half)
        tw_r, tw_i = times(other_r - real_part, other_i - imag_part, cosine, -sine)
        real_part = jnp.where(upper, tw_r, real_part + other_r)
        imag_part = jnp.where(upper, tw_i, imag_part + other_i)
    return (real_part, imag_part)


def butterfly_inverse(real_part, imag_part, device, bits):
    for bit in range(bits):
        half = 1 << bit
        place = device % (2 * half)
        upper = place >= half
        cosine, sine = unit_circle(jnp.where(upper, place - half, 0), 2 * half)
        tw_r, tw_i = times(real_part, imag_part, cosine, sine)
        send_r = jnp.where(upper, tw_r, real_part)
        send_i = jnp.where(upper, tw_i, imag_part)
        other_r, other_i = swapped((send_r, send_i), "ctx", bit)
        real_part = jnp.where(upper, other_r - tw_r, real_part + other_r)
        imag_part = jnp.where(upper, other_i - tw_i, imag_part + other_i)
    return (real_part, imag_part)


def on_device(gate_stream, key_stream, value_stream, residues, decay_rates, out_weight):
    big_p = lax.axis_size("ctx")
    bits = big_p.bit_length() - 1
    rows = key_stream.shape[0]
    length = float(big_p * rows)
    device = lax.axis_index("ctx")
    mixed = jnp.transpose(key_stream.astype(jnp.float32) * value_stream.astype(jnp.float32))
    base, lam, one_less, tail = filter_terms(residues, decay_rates, length)
    filt = (base[:, :, None], lam[:, :, None], one_less[:, :, None], tail[:, :, None])
    z_r, z_i = pre_twiddle(mixed, device, big_p, (2, 1, 1))
    y_r, y_i = butterfly_forward(z_r, z_i, device, bits)
    q_index = reverse_bits(device, bits)
    u_r, u_i = spectral(y_r, y_i, q_index, filt, big_p, rows)
    v_r, v_i = butterfly_inverse(u_r, u_i, device, bits)
    conv_t = post_twiddle(v_r, v_i, device, big_p, rows, (2, 1, 1))
    conv_rows = jnp.transpose(conv_t)
    gated = (gate_stream.astype(jnp.float32) * conv_rows).astype(jnp.bfloat16)
    partial_terms = jnp.dot(gated, out_weight, preferred_element_type=jnp.float32)
    return lax.psum_scatter(partial_terms, "chan", scatter_dimension=1, tiled=True).astype(
        jnp.bfloat16
    )


def solution(mesh):
    return jax.shard_map(
        on_device,
        mesh=mesh,
        in_specs=(
            P("ctx", "chan"),
            P("ctx", "chan"),
            P("ctx", "chan"),
            P(None, "chan"),
            P(None, "chan"),
            P("chan", None),
        ),
        out_specs=P("ctx", "chan"),
        check_vma=False,
    )
```

profile of v0, /device:TPU:4, one launch (start us, length us, event | category | flops | bytes accessed | tf_op | source)
XLA Modules:
  0.0 447.3 jit_solution(1021400048351862410)
XLA Ops:
  6.6 1.1 multiply_bitcast_fusion
  7.9 0.9 broadcast_multiply_fusion.1
  8.8 10.9 %collective-permute-start = (f32[2,256,256]{2,1,0:T(8,128)}, f32[2,256,256]{2,1,0:T(8,128)S(1)}, u32[]{:S(2)}, u32[]{:S(2)}) collective-permute-start(f32[2,256,256]{2,1,0:T(8,128)} %broadcast_multiply_fusion.1), channel_id=1, source_target_pairs={{0,16},{16,0},{1,17},{17,1},{2,18},{18,2},{3,19},{19,3},{4,20},{20... | collective-permute-start | bytes 1572872 | tf_op jit(solution)/shard_map/ppermute | solution.py:19
  19.8 1.0 fusion.108
  20.9 0.9 broadcast_multiply_fusion
  21.8 1.9 collective-permute-start.1
  24.7 8.1 %collective-permute-done = f32[2,256,256]{2,1,0:T(8,128)S(1)} collective-permute-done((f32[2,256,256]{2,1,0:T(8,128)}, f32[2,256,256]{2,1,0:T(8,128)S(1)}, u32[]{:S(2)}, u32[]{:S(2)}) %collective-permute-start) | collective-permute-done | bytes 524320 | tf_op jit(solution)/shard_map/ppermute | solution.py:19
  32.8 10.6 %collective-permute-done.1 = f32[2,256,256]{2,1,0:T(8,128)} collective-permute-done((f32[2,256,256]{2,1,0:T(8,128)}, f32[2,256,256]{2,1,0:T(8,128)}, u32[]{:S(2)}, u32[]{:S(2)}) %collective-permute-start.1) | collective-permute-done | bytes 524320 | tf_op jit(solution)/shard_map/ppermute | solution.py:19
  43.4 1.4 add_select_fusion.16
  44.7 26.6 %collective-permute-start.2 = (f32[2,256,256]{2,1,0:T(8,128)S(1)}, f32[2,256,256]{2,1,0:T(8,128)S(1)}, u32[]{:S(2)}, u32[]{:S(2)}) collective-permute-start(f32[2,256,256]{2,1,0:T(8,128)S(1)} %get-tuple-element.33), channel_id=1, source_target_pairs={{0,8},{8,0},{1,9},{9,1},{2,10},{10,2},{3,11},{11,3},{4,12},{12,4},... | collective-permute-start | bytes 1572872 | tf_op jit(solution)/shard_map/ppermute | solution.py:19
  71.4 1.9 collective-permute-start.3
  73.3 1.0 fusion.86
  74.4 32.2 %collective-permute-done.2 = f32[2,256,256]{2,1,0:T(8,128)S(1)} collective-permute-done((f32[2,256,256]{2,1,0:T(8,128)S(1)}, f32[2,256,256]{2,1,0:T(8,128)S(1)}, u32[]{:S(2)}, u32[]{:S(2)}) %collective-permute-start.2) | collective-permute-done | bytes 524320 | tf_op jit(solution)/shard_map/ppermute | solution.py:19
  106.5 10.5 %collective-permute-done.3 = f32[2,256,256]{2,1,0:T(8,128)S(1)} collective-permute-done((f32[2,256,256]{2,1,0:T(8,128)S(1)}, f32[2,256,256]{2,1,0:T(8,128)S(1)}, u32[]{:S(2)}, u32[]{:S(2)}) %collective-permute-start.3) | collective-permute-done | bytes 524320 | tf_op jit(solution)/shard_map/ppermute | solution.py:19
  117.1 0.2 add_select_fusion.14
  117.3 1.9 collective-permute-start.4
  119.2 3.9 collective-permute-start.5
  123.2 10.9 %collective-permute-done.4 = f32[2,256,256]{2,1,0:T(8,128)S(1)} collective-permute-done((f32[2,256,256]{2,1,0:T(8,128)S(1)}, f32[2,256,256]{2,1,0:T(8,128)S(1)}, u32[]{:S(2)}, u32[]{:S(2)}) %collective-permute-start.4) | collective-permute-done | bytes 524320 | tf_op jit(solution)/shard_map/ppermute | solution.py:19
  134.1 9.6 %collective-permute-done.5 = f32[2,256,256]{2,1,0:T(8,128)S(1)} collective-permute-done((f32[2,256,256]{2,1,0:T(8,128)S(1)}, f32[2,256,256]{2,1,0:T(8,128)S(1)}, u32[]{:S(2)}, u32[]{:S(2)}) %collective-permute-start.5) | collective-permute-done | bytes 524320 | tf_op jit(solution)/shard_map/ppermute | solution.py:19
  143.7 0.2 add_select_fusion.12
  143.9 2.4 collective-permute-start.6
  146.3 4.9 %collective-permute-start.7 = (f32[2,256,256]{2,1,0:T(8,128)S(1)}, f32[2,256,256]{2,1,0:T(8,128)S(1)}, u32[]{:S(2)}, u32[]{:S(2)}) collective-permute-start(f32[2,256,256]{2,1,0:T(8,128)S(1)} %get-tuple-element.28), channel_id=1, source_target_pairs={{0,2},{2,0},{1,3},{3,1},{4,6},{6,4},{5,7},{7,5},{8,10},{10,8},{9,1... | collective-permute-start | bytes 1572872 | tf_op jit(solution)/shard_map/ppermute | solution.py:19
  151.3 0.2 fusion.94
  151.5 10.7 %collective-permute-done.6 = f32[2,256,256]{2,1,0:T(8,128)S(1)} collective-permute-done((f32[2,256,256]{2,1,0:T(8,128)S(1)}, f32[2,256,256]{2,1,0:T(8,128)S(1)}, u32[]{:S(2)}, u32[]{:S(2)}) %collective-permute-start.6) | collective-permute-done | bytes 524320 | tf_op jit(solution)/shard_map/ppermute | solution.py:19
  162.2 8.7 %collective-permute-done.7 = f32[2,256,256]{2,1,0:T(8,128)S(1)} collective-permute-done((f32[2,256,256]{2,1,0:T(8,128)S(1)}, f32[2,256,256]{2,1,0:T(8,128)S(1)}, u32[]{:S(2)}, u32[]{:S(2)}) %collective-permute-start.7) | collective-permute-done | bytes 524320 | tf_op jit(solution)/shard_map/ppermute | solution.py:19
  170.9 0.2 add_select_fusion.10
  171.1 1.9 collective-permute-start.8
  173.0 2.6 collective-permute-start.9
  175.6 1.0 fusion.88
  176.7 0.3 collective-permute-done.9
  176.9 0.3 multiply_subtract_fusion.7
  177.3 1.9 fusion.2
  179.2 5.3 %multiply_subtract_fusion.6 = (f32[2,256,256]{2,1,0:T(8,128)S(1)}, f32[2,256,256]{2,1,0:T(8,128)S(1)}, f32[2,256,256]{2,1,0:T(8,128)S(1)}) fusion(f32[2,256,512]{2,1,0:T(8,128)S(1)} %fusion.2, f32[256]{0:T(256)S(1)} %get-tuple-element.110, f32[256]{0:T(256)S(1)} %bitcast.145, f32[256]{0:T(256)S(1)} %bitcast.83, f32[256]{0:T(256)S(1)} %bitcast.129, ...), kind=kLoop, calls=%fused_computation.132 | loop fusion | flops 33816576 | bytes 2709504 | tf_op jit(solution)/shard_map/sub | solution.py:28
  184.5 0.1 multiply_add_fusion.6
  184.6 1.9 fusion.6
  186.5 0.2 fusion.75
  186.8 2.3 collective-permute-start.11
  189.0 2.0 collective-permute-start.10
  191.1 1.7 collective-permute-done.10
  192.9 0.3 fusion.74
  193.2 2.4 collective-permute-start.13
  195.6 4.9 %collective-permute-start.12 = (f32[2,256,256]{2,1,0:T(8,128)S(1)}, f32[2,256,256]{2,1,0:T(8,128)S(1)}, u32[]{:S(2)}, u32[]{:S(2)}) collective-permute-start(f32[2,256,256]{2,1,0:T(8,128)S(1)} %get-tuple-element.14), channel_id=1, source_target_pairs={{0,2},{2,0},{1,3},{3,1},{4,6},{6,4},{5,7},{7,5},{8,10},{10,8},{9,1... | collective-permute-start | bytes 1572872 | tf_op jit(solution)/shard_map/ppermute | solution.py:19
  200.6 10.8 %collective-permute-done.13 = f32[2,256,256]{2,1,0:T(8,128)S(1)} collective-permute-done((f32[2,256,256]{2,1,0:T(8,128)S(1)}, f32[2,256,256]{2,1,0:T(8,128)S(1)}, u32[]{:S(2)}, u32[]{:S(2)}) %collective-permute-start.13) | collective-permute-done | bytes 524320 | tf_op jit(solution)/shard_map/ppermute | solution.py:19
  211.4 10.4 %collective-permute-done.12 = f32[2,256,256]{2,1,0:T(8,128)S(1)} collective-permute-done((f32[2,256,256]{2,1,0:T(8,128)S(1)}, f32[2,256,256]{2,1,0:T(8,128)S(1)}, u32[]{:S(2)}, u32[]{:S(2)}) %collective-permute-start.12) | collective-permute-done | bytes 524320 | tf_op jit(solution)/shard_map/ppermute | solution.py:19
  221.8 0.3 fusion.72
  222.2 2.5 collective-permute-start.15
  224.7 3.3 collective-permute-start.14
  228.0 10.9 %collective-permute-done.15 = f32[2,256,256]{2,1,0:T(8,128)S(1)} collective-permute-done((f32[2,256,256]{2,1,0:T(8,128)S(1)}, f32[2,256,256]{2,1,0:T(8,128)S(1)}, u32[]{:S(2)}, u32[]{:S(2)}) %collective-permute-start.15) | collective-permute-done | bytes 524320 | tf_op jit(solution)/shard_map/ppermute | solution.py:19
  238.9 9.5 %collective-permute-done.14 = f32[2,256,256]{2,1,0:T(8,128)S(1)} collective-permute-done((f32[2,256,256]{2,1,0:T(8,128)S(1)}, f32[2,256,256]{2,1,0:T(8,128)S(1)}, u32[]{:S(2)}, u32[]{:S(2)}) %collective-permute-start.14) | collective-permute-done | bytes 524320 | tf_op jit(solution)/shard_map/ppermute | solution.py:19
  248.4 0.3 fusion.70
  248.8 1.9 collective-permute-start.17
  250.7 5.0 %collective-permute-start.16 = (f32[2,256,256]{2,1,0:T(8,128)S(1)}, f32[2,256,256]{2,1,0:T(8,128)S(1)}, u32[]{:S(2)}, u32[]{:S(2)}) collective-permute-start(f32[2,256,256]{2,1,0:T(8,128)S(1)} %get-tuple-element.8), channel_id=1, source_target_pairs={{0,8},{8,0},{1,9},{9,1},{2,10},{10,2},{3,11},{11,3},{4,12},{12,4},... | collective-permute-start | bytes 1572872 | tf_op jit(solution)/shard_map/ppermute | solution.py:19
  255.7 30.7 %collective-permute-done.17 = f32[2,256,256]{2,1,0:T(8,128)S(1)} collective-permute-done((f32[2,256,256]{2,1,0:T(8,128)S(1)}, f32[2,256,256]{2,1,0:T(8,128)S(1)}, u32[]{:S(2)}, u32[]{:S(2)}) %collective-permute-start.17) | collective-permute-done | bytes 524320 | tf_op jit(solution)/shard_map/ppermute | solution.py:19
  286.4 11.1 %collective-permute-done.16 = f32[2,256,256]{2,1,0:T(8,128)S(1)} collective-permute-done((f32[2,256,256]{2,1,0:T(8,128)S(1)}, f32[2,256,256]{2,1,0:T(8,128)S(1)}, u32[]{:S(2)}, u32[]{:S(2)}) %collective-permute-start.16) | collective-permute-done | bytes 524320 | tf_op jit(solution)/shard_map/ppermute | solution.py:19
  297.5 1.1 fusion.68
  298.6 0.9 fusion.66
  299.5 7.7 %collective-permute-start.19 = (f32[2,256,256]{2,1,0:T(8,128)}, f32[2,256,256]{2,1,0:T(8,128)}, u32[]{:S(2)}, u32[]{:S(2)}) collective-permute-start(f32[2,256,256]{2,1,0:T(8,128)} %fusion.66), channel_id=1, source_target_pairs={{0,16},{16,0},{1,17},{17,1},{2,18},{18,2},{3,19},{19,3},{4,20},{20... | collective-permute-start | bytes 1572872 | tf_op jit(solution)/shard_map/ppermute | solution.py:19
  307.2 2.0 collective-permute-start.18
  309.4 27.0 %collective-permute-done.19 = f32[2,256,256]{2,1,0:T(8,128)} collective-permute-done((f32[2,256,256]{2,1,0:T(8,128)}, f32[2,256,256]{2,1,0:T(8,128)}, u32[]{:S(2)}, u32[]{:S(2)}) %collective-permute-start.19) | collective-permute-done | bytes 524320 | tf_op jit(solution)/shard_map/ppermute | solution.py:19
  336.3 17.4 %collective-permute-done.18 = f32[2,256,256]{2,1,0:T(8,128)} collective-permute-done((f32[2,256,256]{2,1,0:T(8,128)}, f32[2,256,256]{2,1,0:T(8,128)}, u32[]{:S(2)}, u32[]{:S(2)}) %collective-permute-start.18) | collective-permute-done | bytes 524320 | tf_op jit(solution)/shard_map/ppermute | solution.py:19
  353.8 1.5 subtract_reduce_fusion
  355.3 2.7 fusion.83
  358.0 80.8 %reduce-scatter.2.cloned.1.call-done = f32[256,256]{1,0:T(8,128)} async-done(((f32[256,4096]{1,0:T(8,128)}), f32[256,256]{1,0:T(8,128)}) %reduce-scatter.2.cloned.1.call-update) | async-done | bytes 262160 | tf_op jit(solution)/shard_map/reduce_scatter | solution.py:155
  438.9 1.6 convert_element_type.113
  (37 shorter events, 1.0 us)
Async XLA Ops:
  6.5 348.7 %copy-start = (bf16[256,4096]{1,0:T(8,128)(2,1)S(1)}, bf16[256,4096]{1,0:T(8,128)(2,1)}, u32[]{:S(2)}) copy-start(bf16[256,4096]{1,0:T(8,128)(2,1)} %param.11) | copy-start | bytes 6291460
  6.5 17.2 %copy-start.3 = (f32[16,256]{1,0:T(8,128)S(1)}, f32[16,256]{1,0:T(8,128)}, u32[]{:S(2)}) copy-start(f32[16,256]{1,0:T(8,128)} %param.10) | copy-start | bytes 49156
  6.5 17.2 %copy-start.2 = (f32[16,256]{1,0:T(8,128)S(1)}, f32[16,256]{1,0:T(8,128)}, u32[]{:S(2)}) copy-start(f32[16,256]{1,0:T(8,128)} %param.9) | copy-start | bytes 49156
  6.5 432.3 %reduce-scatter.2.cloned.1.call-start = ((), (), s32[]{:S(2)}) async-start(), calls=%async_computation.1 | async-start | bytes 4456448 | tf_op jit(solution)/shard_map/reduce_scatter | solution.py:155
  8.8 24.0 %collective-permute-start = (f32[2,256,256]{2,1,0:T(8,128)}, f32[2,256,256]{2,1,0:T(8,128)S(1)}, u32[]{:S(2)}, u32[]{:S(2)}) collective-permute-start(f32[2,256,256]{2,1,0:T(8,128)} %broadcast_multiply_fusion.1), channel_id=1, source_target_pairs={{0,16},{16,0},{1,17},{17,1},{2,18},{18,2},{3,19},{19,3},{4,20},{20... | collective-permute-start | bytes 1572872 | tf_op jit(solution)/shard_map/ppermute | solution.py:19
  21.8 21.6 %collective-permute-start.1 = (f32[2,256,256]{2,1,0:T(8,128)}, f32[2,256,256]{2,1,0:T(8,128)}, u32[]{:S(2)}, u32[]{:S(2)}) collective-permute-start(f32[2,256,256]{2,1,0:T(8,128)} %broadcast_multiply_fusion), channel_id=1, source_target_pairs={{0,16},{16,0},{1,17},{17,1},{2,18},{18,2},{3,19},{19,3},{4,20},{20... | collective-permute-start | bytes 1572872 | tf_op jit(solution)/shard_map/ppermute | solution.py:19
  44.7 61.8 %collective-permute-start.2 = (f32[2,256,256]{2,1,0:T(8,128)S(1)}, f32[2,256,256]{2,1,0:T(8,128)S(1)}, u32[]{:S(2)}, u32[]{:S(2)}) collective-permute-start(f32[2,256,256]{2,1,0:T(8,128)S(1)} %get-tuple-element.33), channel_id=1, source_target_pairs={{0,8},{8,0},{1,9},{9,1},{2,10},{10,2},{3,11},{11,3},{4,12},{12,4},... | collective-permute-start | bytes 1572872 | tf_op jit(solution)/shard_map/ppermute | solution.py:19
  71.4 45.7 %collective-permute-start.3 = (f32[2,256,256]{2,1,0:T(8,128)S(1)}, f32[2,256,256]{2,1,0:T(8,128)S(1)}, u32[]{:S(2)}, u32[]{:S(2)}) collective-permute-start(f32[2,256,256]{2,1,0:T(8,128)S(1)} %get-tuple-element.32), channel_id=1, source_target_pairs={{0,8},{8,0},{1,9},{9,1},{2,10},{10,2},{3,11},{11,3},{4,12},{12,4},... | collective-permute-start | bytes 1572872 | tf_op jit(solution)/shard_map/ppermute | solution.py:19
  117.3 16.8 %collective-permute-start.4 = (f32[2,256,256]{2,1,0:T(8,128)S(1)}, f32[2,256,256]{2,1,0:T(8,128)S(1)}, u32[]{:S(2)}, u32[]{:S(2)}) collective-permute-start(f32[2,256,256]{2,1,0:T(8,128)S(1)} %get-tuple-element.31), channel_id=1, source_target_pairs={{0,4},{4,0},{1,5},{5,1},{2,6},{6,2},{3,7},{7,3},{8,12},{12,8},{9,1... | collective-permute-start | bytes 1572872 | tf_op jit(solution)/shard_map/ppermute | solution.py:19
  119.2 24.4 %collective-permute-start.5 = (f32[2,256,256]{2,1,0:T(8,128)S(1)}, f32[2,256,256]{2,1,0:T(8,128)S(1)}, u32[]{:S(2)}, u32[]{:S(2)}) collective-permute-start(f32[2,256,256]{2,1,0:T(8,128)S(1)} %get-tuple-element.30), channel_id=1, source_target_pairs={{0,4},{4,0},{1,5},{5,1},{2,6},{6,2},{3,7},{7,3},{8,12},{12,8},{9,1... | collective-permute-start | bytes 1572872 | tf_op jit(solution)/shard_map/ppermute | solution.py:19
  143.9 18.3 %collective-permute-start.6 = (f32[2,256,256]{2,1,0:T(8,128)S(1)}, f32[2,256,256]{2,1,0:T(8,128)S(1)}, u32[]{:S(2)}, u32[]{:S(2)}) collective-permute-start(f32[2,256,256]{2,1,0:T(8,128)S(1)} %get-tuple-element.29), channel_id=1, source_target_pairs={{0,2},{2,0},{1,3},{3,1},{4,6},{6,4},{5,7},{7,5},{8,10},{10,8},{9,1... | collective-permute-start | bytes 1572872 | tf_op jit(solution)/shard_map/ppermute | solution.py:19
  146.3 24.5 %collective-permute-start.7 = (f32[2,256,256]{2,1,0:T(8,128)S(1)}, f32[2,256,256]{2,1,0:T(8,128)S(1)}, u32[]{:S(2)}, u32[]{:S(2)}) collective-permute-start(f32[2,256,256]{2,1,0:T(8,128)S(1)} %get-tuple-element.28), channel_id=1, source_target_pairs={{0,2},{2,0},{1,3},{3,1},{4,6},{6,4},{5,7},{7,5},{8,10},{10,8},{9,1... | collective-permute-start | bytes 1572872 | tf_op jit(solution)/shard_map/ppermute | solution.py:19
  171.1 5.6 %collective-permute-start.8 = (f32[2,256,256]{2,1,0:T(8,128)S(1)}, f32[2,256,256]{2,1,0:T(8,128)S(1)}, u32[]{:S(2)}, u32[]{:S(2)}) collective-permute-start(f32[2,256,256]{2,1,0:T(8,128)S(1)} %get-tuple-element.27), channel_id=1, source_target_pairs={{0,1},{1,0},{2,3},{3,2},{4,5},{5,4},{6,7},{7,6},{8,9},{9,8},{10,11... | collective-permute-start | bytes 1572872 | tf_op jit(solution)/shard_map/ppermute | solution.py:19
  173.0 3.9 collective-permute-start.9
  186.8 4.3 collective-permute-start.11
  189.0 3.8 collective-permute-start.10
  193.2 18.2 %collective-permute-start.13 = (f32[2,256,256]{2,1,0:T(8,128)S(1)}, f32[2,256,256]{2,1,0:T(8,128)S(1)}, u32[]{:S(2)}, u32[]{:S(2)}) collective-permute-start(f32[2,256,256]{2,1,0:T(8,128)S(1)} %fusion.71), channel_id=1, source_target_pairs={{0,2},{2,0},{1,3},{3,1},{4,6},{6,4},{5,7},{7,5},{8,10},{10,8},{9,1... | collective-permute-start | bytes 1572872 | tf_op jit(solution)/shard_map/ppermute | solution.py:19
  195.6 26.2 %collective-permute-start.12 = (f32[2,256,256]{2,1,0:T(8,128)S(1)}, f32[2,256,256]{2,1,0:T(8,128)S(1)}, u32[]{:S(2)}, u32[]{:S(2)}) collective-permute-start(f32[2,256,256]{2,1,0:T(8,128)S(1)} %get-tuple-element.14), channel_id=1, source_target_pairs={{0,2},{2,0},{1,3},{3,1},{4,6},{6,4},{5,7},{7,5},{8,10},{10,8},{9,1... | collective-permute-start | bytes 1572872 | tf_op jit(solution)/shard_map/ppermute | solution.py:19
  222.2 16.8 %collective-permute-start.15 = (f32[2,256,256]{2,1,0:T(8,128)S(1)}, f32[2,256,256]{2,1,0:T(8,128)S(1)}, u32[]{:S(2)}, u32[]{:S(2)}) collective-permute-start(f32[2,256,256]{2,1,0:T(8,128)S(1)} %fusion.69), channel_id=1, source_target_pairs={{0,4},{4,0},{1,5},{5,1},{2,6},{6,2},{3,7},{7,3},{8,12},{12,8},{9,1... | collective-permute-start | bytes 1572872 | tf_op jit(solution)/shard_map/ppermute | solution.py:19
  224.7 23.7 %collective-permute-start.14 = (f32[2,256,256]{2,1,0:T(8,128)S(1)}, f32[2,256,256]{2,1,0:T(8,128)S(1)}, u32[]{:S(2)}, u32[]{:S(2)}) collective-permute-start(f32[2,256,256]{2,1,0:T(8,128)S(1)} %get-tuple-element.11), channel_id=1, source_target_pairs={{0,4},{4,0},{1,5},{5,1},{2,6},{6,2},{3,7},{7,3},{8,12},{12,8},{9,1... | collective-permute-start | bytes 1572872 | tf_op jit(solution)/shard_map/ppermute | solution.py:19
  248.8 37.6 %collective-permute-start.17 = (f32[2,256,256]{2,1,0:T(8,128)S(1)}, f32[2,256,256]{2,1,0:T(8,128)S(1)}, u32[]{:S(2)}, u32[]{:S(2)}) collective-permute-start(f32[2,256,256]{2,1,0:T(8,128)S(1)} %fusion.67), channel_id=1, source_target_pairs={{0,8},{8,0},{1,9},{9,1},{2,10},{10,2},{3,11},{11,3},{4,12},{12,4},... | collective-permute-start | bytes 1572872 | tf_op jit(solution)/shard_map/ppermute | solution.py:19
  250.7 58.5 %copy-start.1 = (bf16[256,256]{1,0:T(8,128)(2,1)S(1)}, bf16[256,256]{1,0:T(8,128)(2,1)}, u32[]{:S(2)}) copy-start(bf16[256,256]{1,0:T(8,128)(2,1)} %param.6) | copy-start | bytes 393220
  250.7 46.8 %collective-permute-start.16 = (f32[2,256,256]{2,1,0:T(8,128)S(1)}, f32[2,256,256]{2,1,0:T(8,128)S(1)}, u32[]{:S(2)}, u32[]{:S(2)}) collective-permute-start(f32[2,256,256]{2,1,0:T(8,128)S(1)} %get-tuple-element.8), channel_id=1, source_target_pairs={{0,8},{8,0},{1,9},{9,1},{2,10},{10,2},{3,11},{11,3},{4,12},{12,4},... | collective-permute-start | bytes 1572872 | tf_op jit(solution)/shard_map/ppermute | solution.py:19
  299.5 36.8 %collective-permute-start.19 = (f32[2,256,256]{2,1,0:T(8,128)}, f32[2,256,256]{2,1,0:T(8,128)}, u32[]{:S(2)}, u32[]{:S(2)}) collective-permute-start(f32[2,256,256]{2,1,0:T(8,128)} %fusion.66), channel_id=1, source_target_pairs={{0,16},{16,0},{1,17},{17,1},{2,18},{18,2},{3,19},{19,3},{4,20},{20... | collective-permute-start | bytes 1572872 | tf_op jit(solution)/shard_map/ppermute | solution.py:19
  307.2 46.5 %collective-permute-start.18 = (f32[2,256,256]{2,1,0:T(8,128)}, f32[2,256,256]{2,1,0:T(8,128)}, u32[]{:S(2)}, u32[]{:S(2)}) collective-permute-start(f32[2,256,256]{2,1,0:T(8,128)} %get-tuple-element.5), channel_id=1, source_target_pairs={{0,16},{16,0},{1,17},{17,1},{2,18},{18,2},{3,19},{19,3},{4,20},{20... | collective-permute-start | bytes 1572872 | tf_op jit(solution)/shard_map/ppermute | solution.py:19
Sparse Core Ops, SparseCore 0:
  358.1 80.6 reduce-scatter.1
where the time goes:
time: 448 us; the launch traced here: 447 us
  waiting for transfers between devices  312 us (70%)
  starting transfers between devices  93.2 us (21%)
  other arithmetic  20.5 us (5%)
  between operations  14.7 us (3%)
  matrix products  6.42 us (1%)
    ppermute x20, waiting for transfers between devices, swapped(): return lax.ppermute(block, axis, route)  231 us
    ppermute x20, starting transfers between devices, swapped(): return lax.ppermute(block, axis, route)  93.2 us
    reduce_scatter x1, waiting for transfers between devices, on_device(): lax.psum_scatter(partial_terms, 'chan', scatter_dimension=1, tiled=True)  80.8 us
  transfers between devices with their start and end apart: 21, of which 19 were waited for; matrix products, arithmetic and copies ran while one was open for 1% of the time, Pallas kernels for 0%

commit v1 on v0

v1 whole, which is shorter than its diff:
```python
import math

import jax
import jax.numpy as jnp
from jax import lax
from jax.experimental import pallas as pl
from jax.experimental.pallas import tpu as pltpu
from jax.sharding import Mesh, PartitionSpec as P

BLOCK = 64
LANES = 128
SUB = 8


def whole(shape):
    return pl.BlockSpec(shape, lambda *_: (0,) * len(shape))


def minus_expm1(x):
    series = 1.0 - x / 8.0
    for k in (7.0, 6.0, 5.0, 4.0, 3.0, 2.0):
        series = 1.0 - x / k * series
    return jnp.where(x < 0.5, x * series, 1.0 - jnp.exp(-x))


def sub_iota():
    return lax.broadcasted_iota(jnp.int32, (SUB, LANES), 0)


def state_kernel(key_ref, value_ref, decay_ref, blocks_ref, total_ref):
    modes = decay_ref.shape[0]
    count = key_ref.shape[0] // BLOCK
    tiles = BLOCK // SUB
    back = (SUB - 1 - sub_iota()).astype(jnp.float32)

    def lane_group(g, carry):
        lanes = pl.ds(pl.multiple_of(g * LANES, LANES), LANES)
        decay = decay_ref[:, lanes]
        lam8 = jnp.exp(-decay * SUB)
        step = [jnp.broadcast_to(lam8[n : n + 1], (SUB, LANES)) for n in range(modes)]
        lam_block = jnp.exp(-decay * BLOCK)
        ends = [jnp.exp(-decay[n : n + 1] * back) for n in range(modes)]
        total = jnp.zeros((modes, LANES), jnp.float32)
        for b in range(count):
            acc = [None] * modes
            for j in range(tiles):
                rows = pl.ds(b * BLOCK + j * SUB, SUB)
                mixed = key_ref[rows, lanes].astype(jnp.float32) * value_ref[
                    rows, lanes
                ].astype(jnp.float32)
                for n in range(modes):
                    acc[n] = mixed if j == 0 else acc[n] * step[n] + mixed
            rows = [
                jnp.sum(acc[n] * ends[n], axis=0, keepdims=True) for n in range(modes)
            ]
            state = jnp.concatenate(rows, axis=0)
            blocks_ref[b, :, lanes] = state
            total = total * lam_block + state
        total_ref[:, lanes] = total
        return carry

    lax.fori_loop(0, decay_ref.shape[1] // LANES, lane_group, 0)


def local_states(key_stream, value_stream, decay_rates):
    rows, chans = key_stream.shape
    modes = decay_rates.shape[0]
    return pl.pallas_call(
        state_kernel,
        out_shape=(
            jax.ShapeDtypeStruct((rows // BLOCK, modes, chans), jnp.float32),
            jax.ShapeDtypeStruct((modes, chans), jnp.float32),
        ),
        name="local_states",
    )(key_stream, value_stream, decay_rates)


def conv_kernel(
    place_ref,
    chips_ref,
    pair_ref,
    blocks_ref,
    gate_ref,
    key_ref,
    value_ref,
    residues_ref,
    decay_ref,
    out_ref,
    taps_ref,
):
    modes = decay_ref.shape[0]
    rows = key_ref.shape[0]
    count = rows // BLOCK
    tiles = BLOCK // SUB
    chip = place_ref[0]
    core = place_ref[1]
    sub = sub_iota()
    ahead = sub.astype(jnp.float32)

    def lane_group(g, carry):
        lanes = pl.ds(pl.multiple_of(g * LANES, LANES), LANES)
        decay = decay_ref[:, lanes]
        base = residues_ref[:, lanes] * jnp.sqrt(minus_expm1(2.0 * decay))
        lam_rows = jnp.exp(-decay * float(rows))
        lam_chip = jnp.exp(-decay * float(2 * rows))
        before = jnp.zeros((modes, LANES), jnp.float32)
        for j in range(chips_ref.shape[0]):
            before = jnp.where(
                j < chip, before * lam_chip + chips_ref[j, :, lanes], before
            )
        before = jnp.where(core == 0, before, before * lam_rows + pair_ref[0, :, lanes])
        lam1 = jnp.exp(-decay)
        lam8 = jnp.exp(-decay * float(SUB))
        step = [jnp.broadcast_to(lam8[n : n + 1], (SUB, LANES)) for n in range(modes)]
        within = [jnp.exp(-decay[n : n + 1] * ahead) for n in range(modes)]
        kernel = [base[n : n + 1] * within[n] for n in range(modes)]
        for j in range(tiles):
            taps_ref[pl.ds(j * SUB, SUB), :] = sum(kernel)
            if j + 1 < tiles:
                kernel = [kernel[n] * step[n] for n in range(modes)]
        scale = base * lam1
        entry = scale * before
        fade = [entry[n : n + 1] * within[n] for n in range(modes)]
        for b in range(count):
            if b:
                entry = scale * blocks_ref[b - 1, :, lanes]
                fade = [fade[n] + entry[n : n + 1] * within[n] for n in range(modes)]
            acc = []
            mixed = []
            for j in range(tiles):
                at = pl.ds(b * BLOCK + j * SUB, SUB)
                acc.append(sum(fade))
                fade = [fade[n] * step[n] for n in range(modes)]
                mixed.append(
                    key_ref[at, lanes].astype(jnp.float32)
                    * value_ref[at, lanes].astype(jnp.float32)
                )
            for r in range(SUB):
                if r == 0:
                    moved = mixed
                else:
                    rolled = [pltpu.roll(tile, r, 0) for tile in mixed]
                    moved = []
                    for j in range(tiles):
                        above = rolled[j - 1] if j else jnp.zeros_like(rolled[0])
                        moved.append(jnp.where(sub < r, above, rolled[j]))
                for q in range(tiles):
                    tap = taps_ref[pl.ds(q * SUB + r, 1), :]
                    for j in range(q, tiles):
                        acc[j] = acc[j] + tap * moved[j - q]
            for j in range(tiles):
                at = pl.ds(b * BLOCK + j * SUB, SUB)
                gated = gate_ref[at, lanes].astype(jnp.float32) * acc[j]
                out_ref[at, lanes] = gated.astype(jnp.bfloat16).astype(jnp.float32)
        return carry

    lax.fori_loop(0, decay_ref.shape[1] // LANES, lane_group, 0)


def gated_conv(place, chips, pair, blocks, gate, key, value, residues, decay):
    rows, chans = key.shape
    args = (chips, pair, blocks, gate, key, value, residues, decay)
    return pl.pallas_call(
        conv_kernel,
        out_shape=jax.ShapeDtypeStruct((rows, chans), jnp.float32),
        grid_spec=pltpu.PrefetchScalarGridSpec(
            num_scalar_prefetch=1,
            grid=(1,),
            in_specs=[whole(a.shape) for a in args],
            out_specs=whole((rows, chans)),
            scratch_shapes=[pltpu.VMEM((BLOCK, LANES), jnp.float32)],
        ),
        name="gated_conv",
    )(place, *args)


def project_kernel(place_ref, own_ref, peer_ref, wown_ref, first_ref, second_ref, out_ref):
    half = first_ref.shape[0]
    core = place_ref[1]
    here = pl.ds(pl.multiple_of(core * half, half), half)
    there = pl.ds(pl.multiple_of((1 - core) * half, half), half)

    def product(lhs, rhs):
        return jnp.dot(
            lhs.astype(jnp.bfloat16),
            rhs.astype(jnp.bfloat16),
            preferred_element_type=jnp.float32,
        )

    out_ref[...] = (
        product(own_ref[...], wown_ref[...])
        + product(peer_ref[:, here], first_ref[...])
        + product(peer_ref[:, there], second_ref[...])
    )


def project(place, own, peer, weight, first, second):
    rows, chans = own.shape
    cols = first.shape[1]
    half = first.shape[0]
    tile = 512
    steps = cols // tile
    return pl.pallas_call(
        project_kernel,
        out_shape=jax.ShapeDtypeStruct((rows, cols), jnp.float32),
        grid_spec=pltpu.PrefetchScalarGridSpec(
            num_scalar_prefetch=1,
            grid=(steps,),
            in_specs=[
                pl.BlockSpec((rows, chans), lambda i, p: (0, 0)),
                pl.BlockSpec((rows, chans), lambda i, p: (0, 0)),
                pl.BlockSpec((chans, tile), lambda i, p: (0, p[2] * steps + i)),
                pl.BlockSpec((half, tile), lambda i, p: (0, i)),
                pl.BlockSpec((half, tile), lambda i, p: (0, i)),
            ],
            out_specs=pl.BlockSpec((rows, tile), lambda i, p: (0, i)),
        ),
        name="project",
    )(place, own, peer, weight, first, second)


def on_device(gate_stream, key_stream, value_stream, residues, decay_rates, out_weight):
    swap = [(0, 1), (1, 0)]
    rows, chans = key_stream.shape
    cols = out_weight.shape[1] // 2
    side = lax.axis_index("xl")
    core = lax.axis_index("core")
    chip = lax.axis_index("z") * lax.axis_size("xh") + lax.axis_index("xh")
    place = jnp.stack([chip, core, side]).astype(jnp.int32)
    half = chans // 2
    sent = lax.dynamic_slice(
        out_weight, (core * half, (1 - side) * cols), (half, cols)
    ).astype(jnp.float32)
    first = lax.ppermute(sent, "xl", swap)
    second = lax.ppermute(first, "core", swap)

    blocks, total = local_states(key_stream, value_stream, decay_rates)
    pair = lax.all_gather(total, "core", axis=0)
    chip_state = pair[0] * jnp.exp(-decay_rates * float(rows)) + pair[1]
    chips = lax.axis_size("z") * lax.axis_size("xh")
    copies = jnp.broadcast_to(chip_state[None], (chips,) + chip_state.shape)
    states = lax.all_to_all(copies, ("z", "xh"), split_axis=0, concat_axis=0, tiled=True)
    own = gated_conv(
        place,
        states,
        pair,
        blocks,
        gate_stream,
        key_stream,
        value_stream,
        residues,
        decay_rates,
    )
    peer = lax.ppermute(own, "xl", swap)
    partial = project(place, own, peer, out_weight, first, second)
    return lax.psum_scatter(partial, "y", scatter_dimension=1, tiled=True).astype(
        jnp.bfloat16
    )


def solution(mesh):
    inner = Mesh(mesh.devices.reshape(2, 8, 8, 2, 2), ("xl", "y", "z", "xh", "core"))
    time = ("z", "xh", "core")
    chan = ("xl", "y")
    return jax.shard_map(
        on_device,
        mesh=inner,
        in_specs=(
            P(time, chan),
            P(time, chan),
            P(time, chan),
            P(None, chan),
            P(None, chan),
            P(chan, None),
        ),
        out_specs=P(time, chan),
        check_vma=False,
    )
```

time: 448 us -> 139 us (0.31)
  the two profiles are of different devices: /device:TPU:4 before, /device:TPU:2 now
where the time goes in v1:
time: 139 us; the launch traced here: 138 us
  waiting for transfers between devices  79 us (57%)
  starting transfers between devices  25.1 us (18%)
  between operations  13.5 us (10%)
  Pallas kernels  11.4 us (8%)
  other arithmetic  4.05 us (3%)
  local copies, waits for them, and re-layouts  3.15 us (2%)
  blocking collectives  2.19 us (2%)
    reduce_scatter x1, waiting for transfers between devices, on_device(): lax.psum_scatter(partial, 'y', scatter_dimension=1, tiled=True)  40.7 us
    ppermute x1, waiting for transfers between devices, on_device(): first = lax.ppermute(sent, 'xl', swap)  19 us
    all_to_all x1, waiting for transfers between devices, on_device(): lax.all_to_all(copies, ('z', 'xh'), split_axis=0, concat_axis=0, tiled=True)  13.4 us
    all_to_all x1, starting transfers between devices, on_device(): lax.all_to_all(copies, ('z', 'xh'), split_axis=0, concat_axis=0, tiled=True)  12 us
    ppermute x1, starting transfers between devices, on_device(): first = lax.ppermute(sent, 'xl', swap)  7.82 us
    ppermute x1, waiting for transfers between devices, on_device(): peer = lax.ppermute(own, 'xl', swap)  5.88 us
    pallas_call x1, Pallas kernels, project(): pl.pallas_call(project_kernel, out_shape=jax.ShapeDtypeStruct((rows, cols...  5.54 us
    pallas_call x1, Pallas kernels, gated_conv(): pl.pallas_call(conv_kernel, out_shape=jax.ShapeDtypeStruct((rows, chans),...  3.79 us
  transfers between devices with their start and end apart: 5, of which 4 were waited for; matrix products, arithmetic and copies ran while one was open for 1% of the time, Pallas kernels for 4%

profile of v1, /device:TPU:2, one launch (start us, length us, event | category | flops | bytes accessed | tf_op | source)
XLA Modules:
  0.0 138.3 jit_solution(8326809115666129088)
XLA Ops:
  6.5 1.1 dynamic-slice_convert_fusion
  7.7 7.8 %collective-permute-start.1 = (f32[128,2048]{1,0:T(8,128)S(1)}, f32[128,2048]{1,0:T(8,128)S(1)}, u32[]{:S(2)}, u32[]{:S(2)}) collective-permute-start(f32[128,2048]{1,0:T(8,128)S(1)} %dynamic-slice_convert_fusion), channel_id=1, source_target_pairs={{0,256},{256,0},{1,257},{257,1},{2,258},{258,2},{3,259},{259,3},{4... | collective-permute-start | bytes 3145736 | tf_op jit(solution)/shard_map/ppermute | solution.py:234
  15.5 19.0 %collective-permute-done.1.first_ref = f32[128,2048]{1,0:T(8,128)S(1)} collective-permute-done((f32[128,2048]{1,0:T(8,128)S(1)}, f32[128,2048]{1,0:T(8,128)S(1)}, u32[]{:S(2)}, u32[]{:S(2)}) %collective-permute-start.1) | collective-permute-done | bytes 1048608 | tf_op jit(solution)/shard_map/ppermute | solution.py:234
  34.5 0.0 copy-start.1
  34.5 1.9 %collective-permute-start.2 = (f32[128,2048]{1,0:T(8,128)S(1)}, f32[128,2048]{1,0:T(8,128)S(1)}, u32[]{:S(2)}, u32[]{:S(2)}) collective-permute-start(f32[128,2048]{1,0:T(8,128)S(1)} %collective-permute-done.1.first_ref), channel_id=1, source_target_pairs={{0,1},{1,0},{2,3},{3,2},{4,5},{5,4},{6,7},{7,6},{8,9},{9,8},{10,11... | collective-permute-start | bytes 3145736 | tf_op jit(solution)/shard_map/ppermute | solution.py:235
  36.4 2.0 %local_states.1 = (f32[4,16,256]{2,1,0:T(8,128)}, f32[16,256]{1,0:T(8,128)}) custom-call(bf16[256,256]{1,0:T(8,128)(2,1)} %key_ref.3, bf16[256,256]{1,0:T(8,128)(2,1)} %value_ref.3, f32[16,256]{1,0:T(8,128)} %decay_ref.3), custom_call_target="tpu_custom_call" | custom-call | tf_op jit(solution)/shard_map/local_states/pallas_call | solution.py:68
  38.4 2.2 %all-gather = f32[32,256]{1,0:T(8,128)S(1)} all-gather(f32[16,256]{1,0:T(8,128)} %get-tuple-element.7), channel_id=2, replica_groups=mesh['xl'=2,'y'=8,'z'=8,'xh'=2,'core'=2] {'core'}, dimensions={0}, use_global_device_ids=true | all-gather | bytes 49152 | tf_op jit(solution)/shard_map/all_gather | solution.py:238
  40.6 0.0 copy-start.3
  40.6 0.7 slice_add_fusion
  41.4 0.7 broadcast_in_dim.2
  42.1 12.0 %all-to-all-start = ((f32[16,16,256]{2,1,0:T(8,128)}), f32[16,16,256]{2,1,0:T(8,128)S(1)}, u32[]{:S(2)}, u32[]{:S(2)}) async-start(f32[16,16,256]{2,1,0:T(8,128)} %broadcast_in_dim.2), calls=%async_computation | async-start | bytes 524288 | tf_op jit(solution)/shard_map/all_to_all | solution.py:242
  54.1 0.0 reduce-scatter.2.cloned.1.call-start
  54.1 0.6 pad_add_fusion.place_ref
  54.7 13.4 %all-to-all-done.chips_ref = f32[16,16,256]{2,1,0:T(8,128)S(1)} async-done(((f32[16,16,256]{2,1,0:T(8,128)}), f32[16,16,256]{2,1,0:T(8,128)S(1)}, u32[]{:S(2)}, u32[]{:S(2)}) %all-to-all-start) | async-done | bytes 262176 | tf_op jit(solution)/shard_map/all_to_all | solution.py:242
  68.1 0.0 copy-start
  68.1 0.0 copy-done.3
  68.1 0.7 copy-done
  68.8 3.8 %gated_conv.1.own_ref = f32[256,256]{1,0:T(8,128)} custom-call(s32[3]{0:T(128)} %pad_add_fusion.place_ref, f32[16,16,256]{2,1,0:T(8,128)} %copy-done, f32[2,16,256]{2,1,0:T(8,128)} %bitcast.4, f32[4,16,256]{2,1,0:T(8,128)} %get-tuple-element.8.blocks_ref, bf16[256,256]{1,0:T(8,128)(2,1)} %gate_ref.1, bf16[256,256]{1,0:T(8,128)(2,1)} %key_ref.3, ...), custom_call_target="tpu_custom_call" | custom-call | tf_op jit(solution)/shard_map/gated_conv/pallas_call | solution.py:163
  72.6 3.3 %collective-permute-start = (f32[256,256]{1,0:T(8,128)}, f32[256,256]{1,0:T(8,128)S(1)}, u32[]{:S(2)}, u32[]{:S(2)}) collective-permute-start(f32[256,256]{1,0:T(8,128)} %gated_conv.1.own_ref), channel_id=1, source_target_pairs={{0,256},{256,0},{1,257},{257,1},{2,258},{258,2},{3,259},{259,3},{4... | collective-permute-start | bytes 786440 | tf_op jit(solution)/shard_map/ppermute | solution.py:254
  75.9 5.9 %collective-permute-done.peer_ref = f32[256,256]{1,0:T(8,128)S(1)} collective-permute-done((f32[256,256]{1,0:T(8,128)}, f32[256,256]{1,0:T(8,128)S(1)}, u32[]{:S(2)}, u32[]{:S(2)}) %collective-permute-start) | collective-permute-done | bytes 262176 | tf_op jit(solution)/shard_map/ppermute | solution.py:254
  81.8 0.0 copy-start.4
  81.8 0.0 collective-permute-done.2.second_ref
  81.8 0.0 copy-done.1
  81.8 0.7 copy-done.4
  82.5 0.0 copy-start.2
  82.5 1.0 copy-done.2
  83.5 5.5 %project.1 = f32[256,2048]{1,0:T(8,128)} custom-call(s32[3]{0:T(128)} %pad_add_fusion.place_ref, f32[256,256]{1,0:T(8,128)} %gated_conv.1.own_ref, f32[256,256]{1,0:T(8,128)} %copy-done.4, bf16[256,4096]{1,0:T(8,128)(2,1)} %wown_ref.1, f32[128,2048]{1,0:T(8,128)} %copy-done.1, f32[128,2048]{1,0:T(8,128)} %copy-done.2), custom_call_target="tpu_custom_call" | custom-call | tf_op jit(solution)/shard_map/project/pallas_call | solution.py:203
  89.0 0.0 reduce-scatter.2.cloned.1.call-update
  89.1 40.7 %reduce-scatter.2.cloned.1.call-done = f32[256,256]{1,0:T(8,128)} async-done(((f32[256,2048]{1,0:T(8,128)}), f32[256,256]{1,0:T(8,128)}) %reduce-scatter.2.cloned.1.call-update) | async-done | bytes 262160 | tf_op jit(solution)/shard_map/reduce_scatter | solution.py:256
  129.8 1.6 %convert_element_type.7 = bf16[256,256]{1,0:T(8,128)(2,1)} convert(f32[256,256]{1,0:T(8,128)} %reduce-scatter.2.cloned.1.call-done) | non-fusion elementwise | flops 65536 | bytes 393216 | tf_op jit(solution)/shard_map/convert_element_type | solution.py:256
Async XLA Ops:
  7.7 26.8 %collective-permute-start.1 = (f32[128,2048]{1,0:T(8,128)S(1)}, f32[128,2048]{1,0:T(8,128)S(1)}, u32[]{:S(2)}, u32[]{:S(2)}) collective-permute-start(f32[128,2048]{1,0:T(8,128)S(1)} %dynamic-slice_convert_fusion), channel_id=1, source_target_pairs={{0,256},{256,0},{1,257},{257,1},{2,258},{258,2},{3,259},{259,3},{4... | collective-permute-start | bytes 3145736 | tf_op jit(solution)/shard_map/ppermute | solution.py:234
  34.5 47.3 %copy-start.1 = (f32[128,2048]{1,0:T(8,128)}, f32[128,2048]{1,0:T(8,128)S(1)}, u32[]{:S(2)}) copy-start(f32[128,2048]{1,0:T(8,128)S(1)} %collective-permute-done.1.first_ref) | copy-start | bytes 3145732
  34.5 47.3 %collective-permute-start.2 = (f32[128,2048]{1,0:T(8,128)S(1)}, f32[128,2048]{1,0:T(8,128)S(1)}, u32[]{:S(2)}, u32[]{:S(2)}) collective-permute-start(f32[128,2048]{1,0:T(8,128)S(1)} %collective-permute-done.1.first_ref), channel_id=1, source_target_pairs={{0,1},{1,0},{2,3},{3,2},{4,5},{5,4},{6,7},{7,6},{8,9},{9,8},{10,11... | collective-permute-start | bytes 3145736 | tf_op jit(solution)/shard_map/ppermute | solution.py:235
  40.6 27.4 %copy-start.3 = (f32[32,256]{1,0:T(8,128)}, f32[32,256]{1,0:T(8,128)S(1)}, u32[]{:S(2)}) copy-start(f32[32,256]{1,0:T(8,128)S(1)} %all-gather) | copy-start | bytes 98308
  42.1 26.0 %all-to-all-start = ((f32[16,16,256]{2,1,0:T(8,128)}), f32[16,16,256]{2,1,0:T(8,128)S(1)}, u32[]{:S(2)}, u32[]{:S(2)}) async-start(f32[16,16,256]{2,1,0:T(8,128)} %broadcast_in_dim.2), calls=%async_computation | async-start | bytes 524288 | tf_op jit(solution)/shard_map/all_to_all | solution.py:242
  54.1 75.7 %reduce-scatter.2.cloned.1.call-start = ((), (), s32[]{:S(2)}) async-start(), calls=%async_computation.2 | async-start | bytes 2359296 | tf_op jit(solution)/shard_map/reduce_scatter | solution.py:256
  68.1 0.7 copy-start
  72.6 9.2 %collective-permute-start = (f32[256,256]{1,0:T(8,128)}, f32[256,256]{1,0:T(8,128)S(1)}, u32[]{:S(2)}, u32[]{:S(2)}) collective-permute-start(f32[256,256]{1,0:T(8,128)} %gated_conv.1.own_ref), channel_id=1, source_target_pairs={{0,256},{256,0},{1,257},{257,1},{2,258},{258,2},{3,259},{259,3},{4... | collective-permute-start | bytes 786440 | tf_op jit(solution)/shard_map/ppermute | solution.py:254
  81.8 0.7 copy-start.4
  82.5 1.0 copy-start.2
Sparse Core Ops, SparseCore 0:
  89.2 40.5 reduce-scatter.1

commit v2 on v1

--- a/solution.py
+++ b/solution.py
@@ -174,8 +174,53 @@
     )(place, *args)
 
 
-def project_kernel(place_ref, own_ref, peer_ref, wown_ref, first_ref, second_ref, out_ref):
-    half = first_ref.shape[0]
+def pick_kernel(place_ref, *refs):
+    for d in range(3):
+        out_ref = refs[12 + d]
+        for h in range(4):
+            out_ref[:, h * 256 : (h + 1) * 256] = refs[4 * d + h][...].astype(jnp.float32)
+
+
+def picked_weights(place, weight):
+    half = weight.shape[0] // 2
+    tile = 256
+
+    def spec(d, h):
+        return pl.BlockSpec(
+            (half, tile),
+            lambda i, p: (p[1], 8 * (p[2] ^ (d >> 1)) + 2 * h + (p[3] ^ (d & 1))),
+        )
+
+    specs = [spec(d, h) for d in (1, 2, 3) for h in range(4)]
+    shape = (half, 4 * tile)
+    return pl.pallas_call(
+        pick_kernel,
+        out_shape=[jax.ShapeDtypeStruct(shape, jnp.float32)] * 3,
+        grid_spec=pltpu.PrefetchScalarGridSpec(
+            num_scalar_prefetch=1,
+            grid=(1,),
+            in_specs=specs,
+            out_specs=[whole(shape)] * 3,
+        ),
+        name="picked_weights",
+    )(place, *[weight] * 12)
+
+
+def spread_kernel(pair_ref, decay_ref, out_ref, *, rows):
+    state = pair_ref[0] * jnp.exp(-decay_ref[...] * float(rows)) + pair_ref[1]
+    out_ref[...] = jnp.broadcast_to(state[None], out_ref.shape)
+
+
+def spread_states(pair, decay_rates, rows, chips):
+    return pl.pallas_call(
+        lambda *refs: spread_kernel(*refs, rows=rows),
+        out_shape=jax.ShapeDtypeStruct((chips,) + decay_rates.shape, jnp.float32),
+        name="spread_states",
+    )(pair, decay_rates)
+
+
+def project_kernel(place_ref, own_ref, p1_ref, p2_ref, p3_ref, wown_ref, near_ref, far_ref, out_ref):
+    half = wown_ref.shape[0] // 2
     core = place_ref[1]
     here = pl.ds(pl.multiple_of(core * half, half), half)
     there = pl.ds(pl.multiple_of((1 - core) * half, half), half)
@@ -187,59 +232,52 @@
             preferred_element_type=jnp.float32,
         )
 
-    out_ref[...] = (
-        product(own_ref[...], wown_ref[...])
-        + product(peer_ref[:, here], first_ref[...])
-        + product(peer_ref[:, there], second_ref[...])
-    )
-
-
-def project(place, own, peer, weight, first, second):
+    acc = product(own_ref[...], wown_ref[...])
+    for d, peer_ref in enumerate((p1_ref, p2_ref, p3_ref)):
+        acc += product(peer_ref[:, here], near_ref[d * half : (d + 1) * half, :])
+        acc += product(peer_ref[:, there], far_ref[d * half : (d + 1) * half, :])
+    out_ref[0] = acc
+
+
+def project(place, own, peers, weight, near, far):
     rows, chans = own.shape
-    cols = first.shape[1]
-    half = first.shape[0]
-    tile = 512
-    steps = cols // tile
+    tile = chans
+    gated = pl.BlockSpec((rows, chans), lambda i, p: (0, 0))
+    other = pl.BlockSpec((near.shape[0], tile), lambda i, p: (0, i))
     return pl.pallas_call(
         project_kernel,
-        out_shape=jax.ShapeDtypeStruct((rows, cols), jnp.float32),
+        out_shape=jax.ShapeDtypeStruct((4, rows, tile), jnp.float32),
         grid_spec=pltpu.PrefetchScalarGridSpec(
             num_scalar_prefetch=1,
-            grid=(steps,),
-            in_specs=[
-                pl.BlockSpec((rows, chans), lambda i, p: (0, 0)),
-                pl.BlockSpec((rows, chans), lambda i, p: (0, 0)),
-                pl.BlockSpec((chans, tile), lambda i, p: (0, p[2] * steps + i)),
-                pl.BlockSpec((half, tile), lambda i, p: (0, i)),
-                pl.BlockSpec((half, tile), lambda i, p: (0, i)),
-            ],
-            out_specs=pl.BlockSpec((rows, tile), lambda i, p: (0, i)),
+            grid=(4,),
+            in_specs=[gated] * 4
+            + [pl.BlockSpec((chans, tile), lambda i, p: (0, 8 * p[2] + 2 * i + p[3]))]
+            + [other] * 2,
+            out_specs=pl.BlockSpec((1, rows, tile), lambda i, p: (i, 0, 0)),
         ),
         name="project",
-    )(place, own, peer, weight, first, second)
+    )(place, own, *peers, weight, near, far)
 
 
 def on_device(gate_stream, key_stream, value_stream, residues, decay_rates, out_weight):
-    swap = [(0, 1), (1, 0)]
     rows, chans = key_stream.shape
-    cols = out_weight.shape[1] // 2
-    side = lax.axis_index("xl")
-    core = lax.axis_index("core")
+    quad = ("xl", "yl")
+    routes = [[(g, g ^ d) for g in range(4)] for d in (1, 2, 3)]
     chip = lax.axis_index("z") * lax.axis_size("xh") + lax.axis_index("xh")
-    place = jnp.stack([chip, core, side]).astype(jnp.int32)
-    half = chans // 2
-    sent = lax.dynamic_slice(
-        out_weight, (core * half, (1 - side) * cols), (half, cols)
-    ).astype(jnp.float32)
-    first = lax.ppermute(sent, "xl", swap)
-    second = lax.ppermute(first, "core", swap)
-
+    place = jnp.stack(
+        [chip, lax.axis_index("core"), lax.axis_index("xl"), lax.axis_index("yl")]
+    ).astype(jnp.int32)
     blocks, total = local_states(key_stream, value_stream, decay_rates)
     pair = lax.all_gather(total, "core", axis=0)
-    chip_state = pair[0] * jnp.exp(-decay_rates * float(rows)) + pair[1]
     chips = lax.axis_size("z") * lax.axis_size("xh")
-    copies = jnp.broadcast_to(chip_state[None], (chips,) + chip_state.shape)
+    copies = spread_states(pair, decay_rates, rows, chips)
+    sent = picked_weights(place, out_weight)
+    *sent, copies = lax.optimization_barrier((*sent, copies))
     states = lax.all_to_all(copies, ("z", "xh"), split_axis=0, concat_axis=0, tiled=True)
+    near = [lax.ppermute(s, quad, r) for s, r in zip(sent, routes)]
+    *near, states = lax.optimization_barrier((*near, states))
+    near = jnp.concatenate(near, axis=0)
+    far = lax.ppermute(near, "core", [(0, 1), (1, 0)])
     own = gated_conv(
         place,
         states,
@@ -251,17 +289,18 @@
         residues,
         decay_rates,
     )
-    peer = lax.ppermute(own, "xl", swap)
-    partial = project(place, own, peer, out_weight, first, second)
-    return lax.psum_scatter(partial, "y", scatter_dimension=1, tiled=True).astype(
-        jnp.bfloat16
+    peers = [lax.ppermute(own, quad, r) for r in routes]
+    partial = project(place, own, peers, out_weight, near, far)
+    parts = lax.all_to_all(partial, "yh", split_axis=0, concat_axis=0, tiled=True)
+    return jnp.sum(parts, axis=0).astype(jnp.bfloat16)
+
+
+def solution(mesh):
+    inner = Mesh(
+        mesh.devices.reshape(2, 4, 2, 8, 2, 2), ("xl", "yh", "yl", "z", "xh", "core")
     )
-
-
-def solution(mesh):
-    inner = Mesh(mesh.devices.reshape(2, 8, 8, 2, 2), ("xl", "y", "z", "xh", "core"))
     time = ("z", "xh", "core")
-    chan = ("xl", "y")
+    chan = ("xl", "yh", "yl")
     return jax.shard_map(
         on_device,
         mesh=inner,

time: 139 us -> 113 us (0.81)
  the two profiles are of different devices: /device:TPU:2 before, /device:TPU:1 now
where the time goes in v2:
time: 113 us
  blocking collectives  62.4 us (55%)
  starting transfers between devices  19.8 us (18%)
  Pallas kernels  16.2 us (14%)
  waiting for transfers between devices  10.1 us (9%)
  local copies, waits for them, and re-layouts  2.7 us (2%)
  other arithmetic  1.35 us (1%)
    all_to_all x1, blocking collectives, on_device(): lax.all_to_all(partial, 'yh', split_axis=0, concat_axis=0, tiled=True)  31.6 us
    all_to_all x1, blocking collectives, on_device(): lax.all_to_all(copies, ('z', 'xh'), split_axis=0, concat_axis=0, tiled=True)  21 us
    all_gather x1, blocking collectives, on_device(): pair = lax.all_gather(total, 'core', axis=0)  9.85 us
    ppermute x3, waiting for transfers between devices, on_device(): peers = [lax.ppermute(own, quad, r) for r in routes]  8.48 us
    ppermute x3, starting transfers between devices, on_device(): peers = [lax.ppermute(own, quad, r) for r in routes]  8.36 us
    ppermute x3, starting transfers between devices, on_device(): near = [lax.ppermute(s, quad, r) for s, r in zip(sent, routes)]  8.36 us
    pallas_call x1, Pallas kernels, project(): pl.pallas_call(project_kernel, out_shape=jax.ShapeDtypeStruct((4, rows, t...  5.72 us
    pallas_call x1, Pallas kernels, gated_conv(): pl.pallas_call(conv_kernel, out_shape=jax.ShapeDtypeStruct((rows, chans),...  3.79 us
  transfers between devices with their start and end apart: 7, of which 3 were waited for; matrix products, arithmetic and copies ran while one was open for 0% of the time, Pallas kernels for 3%

profile of v2, /device:TPU:1, one launch (start us, length us, event | category | flops | bytes accessed | tf_op | source)
XLA Modules:
  0.0 112.7 jit_solution(325915939506453576)
XLA Ops:
  0.0 2.0 %local_states.1 = (f32[4,16,256]{2,1,0:T(8,128)}, f32[16,256]{1,0:T(8,128)}) custom-call(bf16[256,256]{1,0:T(8,128)(2,1)} %key_ref.3, bf16[256,256]{1,0:T(8,128)(2,1)} %value_ref.3, f32[16,256]{1,0:T(8,128)} %decay_ref.3), custom_call_target="tpu_custom_call" | custom-call | tf_op jit(solution)/shard_map/local_states/pallas_call | solution.py:68
  2.0 9.9 %all-gather = f32[32,256]{1,0:T(8,128)} all-gather(f32[16,256]{1,0:T(8,128)} %get-tuple-element.21), channel_id=2, replica_groups=mesh['xl'=2,'yh'=4,'yl'=2,'z'=8,'xh'=2,'core'=2] {'core'}, dimensions={0}, use_global_device_ids=true | all-gather | bytes 49152 | tf_op jit(solution)/shard_map/all_gather | solution.py:271
  11.9 1.5 %spread_states.1 = f32[16,16,256]{2,1,0:T(8,128)} custom-call(f32[2,16,256]{2,1,0:T(8,128)} %bitcast.5, f32[16,256]{1,0:T(8,128)} %decay_ref.3), custom_call_target="tpu_custom_call" | custom-call | tf_op jit(solution)/shard_map/spread_states/pallas_call | solution.py:215
  13.4 0.6 pad_add_fusion.place_ref
  14.0 0.0 copy-start.2
  14.0 3.2 %picked_weights.1 = (f32[128,1024]{1,0:T(8,128)}, f32[128,1024]{1,0:T(8,128)}, f32[128,1024]{1,0:T(8,128)}) custom-call(s32[4]{0:T(128)} %pad_add_fusion.place_ref, bf16[256,4096]{1,0:T(8,128)(2,1)} %wown_ref.1, bf16[256,4096]{1,0:T(8,128)(2,1)} %wown_ref.1, bf16[256,4096]{1,0:T(8,128)(2,1)} %wown_ref.1, bf16[256,4096]{1,0:T(8,128)(2,1)} %wown_ref.1, ...), custom_call_target="tpu_custom_call" | custom-call | tf_op jit(solution)/shard_map/picked_weights/pallas_call | solution.py:196
  17.2 1.9 %collective-permute-start = (f32[128,1024]{1,0:T(8,128)}, f32[128,1024]{1,0:T(8,128)S(1)}, u32[]{:S(2)}, u32[]{:S(2)}) collective-permute-start(f32[128,1024]{1,0:T(8,128)} %get-tuple-element.22), channel_id=1, source_target_pairs={{0,32},{32,0},{256,288},{288,256},{1,33},{33,1},{257,289},{289,257... | collective-permute-start | bytes 1572872 | tf_op jit(solution)/shard_map/ppermute | solution.py:277
  19.1 1.9 %collective-permute-start.1 = (f32[128,1024]{1,0:T(8,128)}, f32[128,1024]{1,0:T(8,128)S(1)}, u32[]{:S(2)}, u32[]{:S(2)}) collective-permute-start(f32[128,1024]{1,0:T(8,128)} %get-tuple-element.23), channel_id=1, source_target_pairs={{0,256},{32,288},{256,0},{288,32},{1,257},{33,289},{257,1},{289,33... | collective-permute-start | bytes 1572872 | tf_op jit(solution)/shard_map/ppermute | solution.py:277
  21.0 4.5 %collective-permute-start.2 = (f32[128,1024]{1,0:T(8,128)}, f32[128,1024]{1,0:T(8,128)S(1)}, u32[]{:S(2)}, u32[]{:S(2)}) collective-permute-start(f32[128,1024]{1,0:T(8,128)} %get-tuple-element.24), channel_id=1, source_target_pairs={{0,288},{32,256},{256,32},{288,0},{1,289},{33,257},{257,33},{289,1... | collective-permute-start | bytes 1572872 | tf_op jit(solution)/shard_map/ppermute | solution.py:277
  25.6 0.0 copy-done.2
  25.6 21.0 %all_to_all.10.chips_ref = f32[16,16,256]{2,1,0:T(8,128)} all-to-all(f32[16,16,256]{2,1,0:T(8,128)S(1)} %copy-done.2), channel_id=1, replica_groups=mesh['xl'=2,'yh'=4,'yl'=2,'z'=8,'xh'=2,'core'=2] {'z','xh'}, dimensions={0} | all-to-all | bytes 524288 | tf_op jit(solution)/shard_map/all_to_all | solution.py:276
  46.6 0.0 collective-permute-done
  46.6 1.7 %collective-permute-done.1 = f32[128,1024]{1,0:T(8,128)S(1)} collective-permute-done((f32[128,1024]{1,0:T(8,128)}, f32[128,1024]{1,0:T(8,128)S(1)}, u32[]{:S(2)}, u32[]{:S(2)}) %collective-permute-start.1) | collective-permute-done | bytes 524320 | tf_op jit(solution)/shard_map/ppermute | solution.py:277
  48.3 0.0 collective-permute-done.2
  48.4 0.0 copy-start
  48.4 3.1 %collective-permute-start.6 = (f32[384,1024]{1,0:T(8,128)S(1)}, f32[384,1024]{1,0:T(8,128)S(1)}, u32[]{:S(2)}, u32[]{:S(2)}) collective-permute-start(f32[384,1024]{1,0:T(8,128)S(1)} %constant_dynamic-update-slice_fusion.near_ref), channel_id=1, source_target_pairs={{0,1},{1,0},{2,3},{3,2},{4,5},{5,4},{6,7},{7,6},{8,9},{9,8},{10,11... | collective-permute-start | bytes 4718600 | tf_op jit(solution)/shard_map/ppermute | solution.py:280
  51.5 3.8 %gated_conv.1.own_ref = f32[256,256]{1,0:T(8,128)} custom-call(s32[4]{0:T(128)} %pad_add_fusion.place_ref, f32[16,16,256]{2,1,0:T(8,128)} %all_to_all.10.chips_ref, f32[2,16,256]{2,1,0:T(8,128)} %bitcast.6, f32[4,16,256]{2,1,0:T(8,128)} %get-tuple-element.27.blocks_ref, bf16[256,256]{1,0:T(8,128)(2,1)} %gate_ref.1, bf16[256,256]{1,0:T(8,128)(2,1)} %key_ref.3, ...), custom_call_target="tpu_custom_call" | custom-call | tf_op jit(solution)/shard_map/gated_conv/pallas_call | solution.py:163
  55.3 3.1 %collective-permute-start.5 = (f32[256,256]{1,0:T(8,128)}, f32[256,256]{1,0:T(8,128)S(1)}, u32[]{:S(2)}, u32[]{:S(2)}) collective-permute-start(f32[256,256]{1,0:T(8,128)} %gated_conv.1.own_ref), channel_id=1, source_target_pairs={{0,288},{32,256},{256,32},{288,0},{1,289},{33,257},{257,33},{289,1... | collective-permute-start | bytes 786440 | tf_op jit(solution)/shard_map/ppermute | solution.py:292
  58.4 3.4 %collective-permute-start.4 = (f32[256,256]{1,0:T(8,128)}, f32[256,256]{1,0:T(8,128)S(1)}, u32[]{:S(2)}, u32[]{:S(2)}) collective-permute-start(f32[256,256]{1,0:T(8,128)} %gated_conv.1.own_ref), channel_id=1, source_target_pairs={{0,256},{32,288},{256,0},{288,32},{1,257},{33,289},{257,1},{289,33... | collective-permute-start | bytes 786440 | tf_op jit(solution)/shard_map/ppermute | solution.py:292
  61.7 1.9 %collective-permute-start.3 = (f32[256,256]{1,0:T(8,128)}, f32[256,256]{1,0:T(8,128)S(1)}, u32[]{:S(2)}, u32[]{:S(2)}) collective-permute-start(f32[256,256]{1,0:T(8,128)} %gated_conv.1.own_ref), channel_id=1, source_target_pairs={{0,32},{32,0},{256,288},{288,256},{1,33},{33,1},{257,289},{289,257... | collective-permute-start | bytes 786440 | tf_op jit(solution)/shard_map/ppermute | solution.py:292
  63.7 2.6 %collective-permute-done.5.p3_ref = f32[256,256]{1,0:T(8,128)S(1)} collective-permute-done((f32[256,256]{1,0:T(8,128)}, f32[256,256]{1,0:T(8,128)S(1)}, u32[]{:S(2)}, u32[]{:S(2)}) %collective-permute-start.5) | collective-permute-done | bytes 262176 | tf_op jit(solution)/shard_map/ppermute | solution.py:292
  66.2 0.0 copy-start.3
  66.2 5.9 %collective-permute-done.4.p2_ref = f32[256,256]{1,0:T(8,128)S(1)} collective-permute-done((f32[256,256]{1,0:T(8,128)}, f32[256,256]{1,0:T(8,128)S(1)}, u32[]{:S(2)}, u32[]{:S(2)}) %collective-permute-start.4) | collective-permute-done | bytes 262176 | tf_op jit(solution)/shard_map/ppermute | solution.py:292
  72.1 0.0 copy-start.4
  72.1 0.7 copy-done.4
  72.9 0.0 collective-permute-done.3.p1_ref
  72.9 0.0 copy-start.5
  72.9 0.7 copy-done.5
  73.6 0.0 collective-permute-done.6.far_ref
  73.6 0.0 copy-done
  73.6 0.0 copy-done.3
  73.6 0.0 copy-start.1
  73.6 1.1 %copy-done.1 = f32[384,1024]{1,0:T(8,128)} copy-done((f32[384,1024]{1,0:T(8,128)}, f32[384,1024]{1,0:T(8,128)S(1)}, u32[]{:S(2)}) %copy-start.1) | copy-done | bytes 1572888
  74.7 5.7 %project.1 = f32[4,256,256]{2,1,0:T(8,128)} custom-call(s32[4]{0:T(128)} %pad_add_fusion.place_ref, f32[256,256]{1,0:T(8,128)} %gated_conv.1.own_ref, f32[256,256]{1,0:T(8,128)} %copy-done.5, f32[256,256]{1,0:T(8,128)} %copy-done.4, f32[256,256]{1,0:T(8,128)} %copy-done.3, bf16[256,4096]{1,0:T(8,128)(2,1)} %wown_ref.1, f32[384,1024]{1,0:T(8,128)} %copy-done, ...), custom_call_target="tpu_custom_call" | custom-call | tf_op jit(solution)/shard_map/project/pallas_call | solution.py:247
  80.5 31.6 %all_to_all.11 = f32[4,256,256]{2,1,0:T(8,128)S(1)} all-to-all(f32[4,256,256]{2,1,0:T(8,128)} %project.1), channel_id=1, replica_groups=mesh['xl'=2,'yh'=4,'yl'=2,'z'=8,'xh'=2,'core'=2] {'yh'}, dimensions={0} | all-to-all | bytes 2097152 | tf_op jit(solution)/shard_map/all_to_all | solution.py:294
  112.0 0.7 reduce_sum.9
  (3 shorter events, 0.1 us)
Async XLA Ops:
  14.0 11.6 %copy-start.2 = (f32[16,16,256]{2,1,0:T(8,128)S(1)}, f32[16,16,256]{2,1,0:T(8,128)}, u32[]{:S(2)}) copy-start(f32[16,16,256]{2,1,0:T(8,128)} %spread_states.1) | copy-start | bytes 786436
  17.2 29.4 %collective-permute-start = (f32[128,1024]{1,0:T(8,128)}, f32[128,1024]{1,0:T(8,128)S(1)}, u32[]{:S(2)}, u32[]{:S(2)}) collective-permute-start(f32[128,1024]{1,0:T(8,128)} %get-tuple-element.22), channel_id=1, source_target_pairs={{0,32},{32,0},{256,288},{288,256},{1,33},{33,1},{257,289},{289,257... | collective-permute-start | bytes 1572872 | tf_op jit(solution)/shard_map/ppermute | solution.py:277
  19.1 29.2 %collective-permute-start.1 = (f32[128,1024]{1,0:T(8,128)}, f32[128,1024]{1,0:T(8,128)S(1)}, u32[]{:S(2)}, u32[]{:S(2)}) collective-permute-start(f32[128,1024]{1,0:T(8,128)} %get-tuple-element.23), channel_id=1, source_target_pairs={{0,256},{32,288},{256,0},{288,32},{1,257},{33,289},{257,1},{289,33... | collective-permute-start | bytes 1572872 | tf_op jit(solution)/shard_map/ppermute | solution.py:277
  21.0 27.2 %collective-permute-start.2 = (f32[128,1024]{1,0:T(8,128)}, f32[128,1024]{1,0:T(8,128)S(1)}, u32[]{:S(2)}, u32[]{:S(2)}) collective-permute-start(f32[128,1024]{1,0:T(8,128)} %get-tuple-element.24), channel_id=1, source_target_pairs={{0,288},{32,256},{256,32},{288,0},{1,289},{33,257},{257,33},{289,1... | collective-permute-start | bytes 1572872 | tf_op jit(solution)/shard_map/ppermute | solution.py:277
  48.4 25.2 %copy-start = (f32[384,1024]{1,0:T(8,128)}, f32[384,1024]{1,0:T(8,128)S(1)}, u32[]{:S(2)}) copy-start(f32[384,1024]{1,0:T(8,128)S(1)} %constant_dynamic-update-slice_fusion.near_ref) | copy-start | bytes 4718596
  48.4 25.2 %collective-permute-start.6 = (f32[384,1024]{1,0:T(8,128)S(1)}, f32[384,1024]{1,0:T(8,128)S(1)}, u32[]{:S(2)}, u32[]{:S(2)}) collective-permute-start(f32[384,1024]{1,0:T(8,128)S(1)} %constant_dynamic-update-slice_fusion.near_ref), channel_id=1, source_target_pairs={{0,1},{1,0},{2,3},{3,2},{4,5},{5,4},{6,7},{7,6},{8,9},{9,8},{10,11... | collective-permute-start | bytes 4718600 | tf_op jit(solution)/shard_map/ppermute | solution.py:280
  55.3 11.0 %collective-permute-start.5 = (f32[256,256]{1,0:T(8,128)}, f32[256,256]{1,0:T(8,128)S(1)}, u32[]{:S(2)}, u32[]{:S(2)}) collective-permute-start(f32[256,256]{1,0:T(8,128)} %gated_conv.1.own_ref), channel_id=1, source_target_pairs={{0,288},{32,256},{256,32},{288,0},{1,289},{33,257},{257,33},{289,1... | collective-permute-start | bytes 786440 | tf_op jit(solution)/shard_map/ppermute | solution.py:292
  58.4 13.8 %collective-permute-start.4 = (f32[256,256]{1,0:T(8,128)}, f32[256,256]{1,0:T(8,128)S(1)}, u32[]{:S(2)}, u32[]{:S(2)}) collective-permute-start(f32[256,256]{1,0:T(8,128)} %gated_conv.1.own_ref), channel_id=1, source_target_pairs={{0,256},{32,288},{256,0},{288,32},{1,257},{33,289},{257,1},{289,33... | collective-permute-start | bytes 786440 | tf_op jit(solution)/shard_map/ppermute | solution.py:292
  61.7 11.1 %collective-permute-start.3 = (f32[256,256]{1,0:T(8,128)}, f32[256,256]{1,0:T(8,128)S(1)}, u32[]{:S(2)}, u32[]{:S(2)}) collective-permute-start(f32[256,256]{1,0:T(8,128)} %gated_conv.1.own_ref), channel_id=1, source_target_pairs={{0,32},{32,0},{256,288},{288,256},{1,33},{33,1},{257,289},{289,257... | collective-permute-start | bytes 786440 | tf_op jit(solution)/shard_map/ppermute | solution.py:292
  66.2 7.3 %copy-start.3 = (f32[256,256]{1,0:T(8,128)}, f32[256,256]{1,0:T(8,128)S(1)}, u32[]{:S(2)}) copy-start(f32[256,256]{1,0:T(8,128)S(1)} %collective-permute-done.5.p3_ref) | copy-start | bytes 786436
  72.1 0.7 copy-start.4
  72.9 0.7 copy-start.5
  73.6 1.2 %copy-start.1 = (f32[384,1024]{1,0:T(8,128)}, f32[384,1024]{1,0:T(8,128)S(1)}, u32[]{:S(2)}) copy-start(f32[384,1024]{1,0:T(8,128)S(1)} %collective-permute-done.6.far_ref) | copy-start | bytes 4718596

commit v3 on v2

--- a/solution.py
+++ b/solution.py
@@ -10,6 +10,14 @@
 BLOCK = 64
 LANES = 128
 SUB = 8
+
+
+def near_core(array):
+    return pltpu.with_memory_space_constraint(array, pltpu.VMEM)
+
+
+def in_hbm(*arrays):
+    return [pltpu.with_memory_space_constraint(a, pltpu.HBM) for a in arrays]
 
 
 def whole(shape):
@@ -159,7 +167,7 @@
 
 def gated_conv(place, chips, pair, blocks, gate, key, value, residues, decay):
     rows, chans = key.shape
-    args = (chips, pair, blocks, gate, key, value, residues, decay)
+    args = (near_core(chips), pair, blocks, gate, key, value, residues, decay)
     return pl.pallas_call(
         conv_kernel,
         out_shape=jax.ShapeDtypeStruct((rows, chans), jnp.float32),
@@ -170,6 +178,9 @@
             out_specs=whole((rows, chans)),
             scratch_shapes=[pltpu.VMEM((BLOCK, LANES), jnp.float32)],
         ),
+        cost_estimate=pl.CostEstimate(
+            flops=2 * 10**11, transcendentals=0, bytes_accessed=2 * 10**8
+        ),
         name="gated_conv",
     )(place, *args)
 
@@ -219,44 +230,64 @@
     )(pair, decay_rates)
 
 
-def project_kernel(place_ref, own_ref, p1_ref, p2_ref, p3_ref, wown_ref, near_ref, far_ref, out_ref):
+def weights_kernel(place_ref, wown_ref, near_ref, far_ref, out_ref):
     half = wown_ref.shape[0] // 2
     core = place_ref[1]
-    here = pl.ds(pl.multiple_of(core * half, half), half)
-    there = pl.ds(pl.multiple_of((1 - core) * half, half), half)
-
-    def product(lhs, rhs):
-        return jnp.dot(
-            lhs.astype(jnp.bfloat16),
-            rhs.astype(jnp.bfloat16),
-            preferred_element_type=jnp.float32,
-        )
-
-    acc = product(own_ref[...], wown_ref[...])
-    for d, peer_ref in enumerate((p1_ref, p2_ref, p3_ref)):
-        acc += product(peer_ref[:, here], near_ref[d * half : (d + 1) * half, :])
-        acc += product(peer_ref[:, there], far_ref[d * half : (d + 1) * half, :])
-    out_ref[0] = acc
-
-
-def project(place, own, peers, weight, near, far):
-    rows, chans = own.shape
-    tile = chans
-    gated = pl.BlockSpec((rows, chans), lambda i, p: (0, 0))
-    other = pl.BlockSpec((near.shape[0], tile), lambda i, p: (0, i))
-    return pl.pallas_call(
-        project_kernel,
-        out_shape=jax.ShapeDtypeStruct((4, rows, tile), jnp.float32),
+    out_ref[: 2 * half, :] = wown_ref[...]
+    for d in range(3):
+        top = 2 * half * (d + 1)
+        part = pl.ds(d * half, half)
+        here = pl.ds(pl.multiple_of(top + core * half, half), half)
+        there = pl.ds(pl.multiple_of(top + (1 - core) * half, half), half)
+        out_ref[here, :] = near_ref[part, :].astype(jnp.bfloat16)
+        out_ref[there, :] = far_ref[part, :].astype(jnp.bfloat16)
+
+
+def joined_weights(place, weight, near, far):
+    chans = weight.shape[0]
+    other = pl.BlockSpec((near.shape[0], chans), lambda i, p: (0, i))
+    return pl.pallas_call(
+        weights_kernel,
+        out_shape=jax.ShapeDtypeStruct((4 * chans, 4 * chans), jnp.bfloat16),
         grid_spec=pltpu.PrefetchScalarGridSpec(
             num_scalar_prefetch=1,
             grid=(4,),
-            in_specs=[gated] * 4
-            + [pl.BlockSpec((chans, tile), lambda i, p: (0, 8 * p[2] + 2 * i + p[3]))]
-            + [other] * 2,
-            out_specs=pl.BlockSpec((1, rows, tile), lambda i, p: (i, 0, 0)),
-        ),
+            in_specs=[
+                pl.BlockSpec((chans, chans), lambda i, p: (0, 8 * p[2] + 2 * i + p[3])),
+                other,
+                other,
+            ],
+            out_specs=pl.BlockSpec((4 * chans, chans), lambda i, p: (0, i)),
+        ),
+        cost_estimate=pl.CostEstimate(flops=1000, transcendentals=0, bytes_accessed=1000),
+        name="joined_weights",
+    )(place, weight, *in_hbm(near, far))
+
+
+def project_kernel(own_ref, p1_ref, p2_ref, p3_ref, weight_ref, out_ref):
+    chans = own_ref.shape[1]
+    acc = None
+    for d, ref in enumerate((own_ref, p1_ref, p2_ref, p3_ref)):
+        term = jnp.dot(
+            ref[...].astype(jnp.bfloat16),
+            weight_ref[d * chans : (d + 1) * chans, :],
+            preferred_element_type=jnp.float32,
+        )
+        acc = term if acc is None else acc + term
+    out_ref[0] = acc
+
+
+def project(own, peers, weight):
+    rows, chans = own.shape
+    return pl.pallas_call(
+        project_kernel,
+        out_shape=jax.ShapeDtypeStruct((4, rows, chans), jnp.float32),
+        grid=(4,),
+        in_specs=[pl.BlockSpec((rows, chans), lambda i: (0, 0))] * 4
+        + [pl.BlockSpec((4 * chans, chans), lambda i: (0, i))],
+        out_specs=pl.BlockSpec((1, rows, chans), lambda i: (i, 0, 0)),
         name="project",
-    )(place, own, *peers, weight, near, far)
+    )(*in_hbm(own, *peers), weight)
 
 
 def on_device(gate_stream, key_stream, value_stream, residues, decay_rates, out_weight):
@@ -272,12 +303,8 @@
     chips = lax.axis_size("z") * lax.axis_size("xh")
     copies = spread_states(pair, decay_rates, rows, chips)
     sent = picked_weights(place, out_weight)
-    *sent, copies = lax.optimization_barrier((*sent, copies))
     states = lax.all_to_all(copies, ("z", "xh"), split_axis=0, concat_axis=0, tiled=True)
     near = [lax.ppermute(s, quad, r) for s, r in zip(sent, routes)]
-    *near, states = lax.optimization_barrier((*near, states))
-    near = jnp.concatenate(near, axis=0)
-    far = lax.ppermute(near, "core", [(0, 1), (1, 0)])
     own = gated_conv(
         place,
         states,
@@ -290,7 +317,11 @@
         decay_rates,
     )
     peers = [lax.ppermute(own, quad, r) for r in routes]
-    partial = project(place, own, peers, out_weight, near, far)
+    near = jnp.concatenate(near, axis=0)
+    near, _ = lax.optimization_barrier((near, peers[2]))
+    far = lax.ppermute(near, "core", [(0, 1), (1, 0)])
+    weight = joined_weights(place, out_weight, near, far)
+    partial = project(own, peers, weight)
     parts = lax.all_to_all(partial, "yh", split_axis=0, concat_axis=0, tiled=True)
     return jnp.sum(parts, axis=0).astype(jnp.bfloat16)
 

time: 113 us -> 116 us (1.027); the launches traced: 113 us -> 114 us
  blocking collectives: 62.4 us -> 42.5 us
  waiting for transfers between devices: 10.1 us -> 20.7 us
  starting transfers between devices: 19.8 us -> 27.1 us
  Pallas kernels: 16.2 us -> 19.6 us
  local copies, waits for them, and re-layouts: 2.7 us -> 1.14 us
  other arithmetic: 1.35 us -> 2.86 us
    all_to_all x1 -> x0, blocking collectives: 21 us -> none  [on_device(): lax.all_to_all(copies, ('z', 'xh'), split_axis=0, concat_axis=0, tiled=True)]
    ppermute x3, waiting for transfers between devices: 1.66 us -> 18.8 us  [on_device(): near = [lax.ppermute(s, quad, r) for s, r in zip(sent, routes)]]
    ppermute x3, waiting for transfers between devices: 8.48 us -> 1.19 us  [on_device(): peers = [lax.ppermute(own, quad, r) for r in routes]]
    all_to_all x0 -> x1, starting transfers between devices: none -> 7.23 us  [on_device(): lax.all_to_all(copies, ('z', 'xh'), split_axis=0, concat_axis=0, tiled=True)]
    pallas_call x1 -> x2, Pallas kernels: 5.72 us -> 9.32 us  [the longest x1 4.86 us: joined_weights(): pl.pallas_call(weights_kernel, out_shape=jax.ShapeDtypeStruct((4 * chans,...]
    unnamed x14 -> x6, local copies, waits for them, and re-layouts: 2.66 us -> 1.14 us
    concatenate x0 -> x1, other arithmetic: none -> 1.46 us  [on_device(): near = jnp.concatenate(near, axis=0)]
  transfers between devices with their start and end apart: 7 -> 8, of which waited for: 3 -> 3; matrix products, arithmetic and copies ran while one was open for 0% -> 2% of each run, Pallas kernels for 3% -> 10%
where the time goes in v3:
time: 116 us; the launch traced here: 114 us
  blocking collectives  42.5 us (37%)
  starting transfers between devices  27.1 us (23%)
  waiting for transfers between devices  20.7 us (18%)
  Pallas kernels  19.6 us (17%)
  other arithmetic  2.86 us (2%)
    all_to_all x1, blocking collectives, on_device(): lax.all_to_all(partial, 'yh', split_axis=0, concat_axis=0, tiled=True)  32.7 us
    ppermute x3, waiting for transfers between devices, on_device(): near = [lax.ppermute(s, quad, r) for s, r in zip(sent, routes)]  18.8 us
    all_gather x1, blocking collectives, on_device(): pair = lax.all_gather(total, 'core', axis=0)  9.85 us
    ppermute x3, starting transfers between devices, on_device(): near = [lax.ppermute(s, quad, r) for s, r in zip(sent, routes)]  8.36 us
    ppermute x3, starting transfers between devices, on_device(): peers = [lax.ppermute(own, quad, r) for r in routes]  8 us
    all_to_all x1, starting transfers between devices, on_device(): lax.all_to_all(copies, ('z', 'xh'), split_axis=0, concat_axis=0, tiled=True)  7.23 us
    pallas_call x1, Pallas kernels, joined_weights(): pl.pallas_call(weights_kernel, out_shape=jax.ShapeDtypeStruct((4 * chans,...  4.86 us
    pallas_call x1, Pallas kernels, project(): pl.pallas_call(project_kernel, out_shape=jax.ShapeDtypeStruct((4, rows, c...  4.46 us
  transfers between devices with their start and end apart: 8, of which 3 were waited for; matrix products, arithmetic and copies ran while one was open for 2% of the time, Pallas kernels for 10%

profile of v3, /device:TPU:1, one launch (start us, length us, event | category | flops | bytes accessed | tf_op | source)
XLA Modules:
  0.0 114.1 jit_solution(7976300900597661081)
XLA Ops:
  0.0 2.0 %local_states.1 = (f32[4,16,256]{2,1,0:T(8,128)}, f32[16,256]{1,0:T(8,128)}) custom-call(bf16[256,256]{1,0:T(8,128)(2,1)} %key_ref.3, bf16[256,256]{1,0:T(8,128)(2,1)} %value_ref.3, f32[16,256]{1,0:T(8,128)} %decay_ref.3), custom_call_target="tpu_custom_call" | custom-call | tf_op jit(solution)/shard_map/local_states/pallas_call | solution.py:76
  2.0 9.8 %all-gather = f32[32,256]{1,0:T(8,128)} all-gather(f32[16,256]{1,0:T(8,128)} %get-tuple-element.11), channel_id=2, replica_groups=mesh['xl'=2,'yh'=4,'yl'=2,'z'=8,'xh'=2,'core'=2] {'core'}, dimensions={0}, use_global_device_ids=true | all-gather | bytes 49152 | tf_op jit(solution)/shard_map/all_gather | solution.py:302
  11.9 1.5 %spread_states.1 = f32[16,16,256]{2,1,0:T(8,128)} custom-call(f32[2,16,256]{2,1,0:T(8,128)} %bitcast.5, f32[16,256]{1,0:T(8,128)} %decay_ref.3), custom_call_target="tpu_custom_call" | custom-call | tf_op jit(solution)/shard_map/spread_states/pallas_call | solution.py:226
  13.4 7.2 %all-to-all-start = ((f32[16,16,256]{2,1,0:T(8,128)}), f32[16,16,256]{2,1,0:T(8,128)S(1)}, u32[]{:S(2)}, u32[]{:S(2)}) async-start(f32[16,16,256]{2,1,0:T(8,128)} %spread_states.1), calls=%async_computation | async-start | bytes 524288 | tf_op jit(solution)/shard_map/all_to_all | solution.py:306
  20.6 0.7 pad_add_fusion.place_ref
  21.3 3.0 %picked_weights.1 = (f32[128,1024]{1,0:T(8,128)}, f32[128,1024]{1,0:T(8,128)}, f32[128,1024]{1,0:T(8,128)}) custom-call(s32[4]{0:T(128)} %pad_add_fusion.place_ref, bf16[256,4096]{1,0:T(8,128)(2,1)} %wown_ref.1, bf16[256,4096]{1,0:T(8,128)(2,1)} %wown_ref.1, bf16[256,4096]{1,0:T(8,128)(2,1)} %wown_ref.1, bf16[256,4096]{1,0:T(8,128)(2,1)} %wown_ref.1, ...), custom_call_target="tpu_custom_call" | custom-call | tf_op jit(solution)/shard_map/picked_weights/pallas_call | solution.py:207
  24.3 3.2 %collective-permute-start.3 = (f32[128,1024]{1,0:T(8,128)}, f32[128,1024]{1,0:T(8,128)}, u32[]{:S(2)}, u32[]{:S(2)}) collective-permute-start(f32[128,1024]{1,0:T(8,128)} %get-tuple-element.13), channel_id=1, source_target_pairs={{0,32},{32,0},{256,288},{288,256},{1,33},{33,1},{257,289},{289,257... | collective-permute-start | bytes 1572872 | tf_op jit(solution)/shard_map/ppermute | solution.py:307
  27.5 2.2 %collective-permute-start.4 = (f32[128,1024]{1,0:T(8,128)}, f32[128,1024]{1,0:T(8,128)}, u32[]{:S(2)}, u32[]{:S(2)}) collective-permute-start(f32[128,1024]{1,0:T(8,128)} %get-tuple-element.14), channel_id=1, source_target_pairs={{0,256},{32,288},{256,0},{288,32},{1,257},{33,289},{257,1},{289,33... | collective-permute-start | bytes 1572872 | tf_op jit(solution)/shard_map/ppermute | solution.py:307
  29.7 2.9 %collective-permute-start.5 = (f32[128,1024]{1,0:T(8,128)}, f32[128,1024]{1,0:T(8,128)}, u32[]{:S(2)}, u32[]{:S(2)}) collective-permute-start(f32[128,1024]{1,0:T(8,128)} %get-tuple-element.15), channel_id=1, source_target_pairs={{0,288},{32,256},{256,32},{288,0},{1,289},{33,257},{257,33},{289,1... | collective-permute-start | bytes 1572872 | tf_op jit(solution)/shard_map/ppermute | solution.py:307
  32.7 0.8 all-to-all-done.chips_ref
  33.5 3.7 %gated_conv.1.own_ref = f32[256,256]{1,0:T(8,128)} custom-call(s32[4]{0:T(128)} %pad_add_fusion.place_ref, f32[16,16,256]{2,1,0:T(8,128)S(1)} %all-to-all-done.chips_ref, f32[2,16,256]{2,1,0:T(8,128)} %bitcast.6, f32[4,16,256]{2,1,0:T(8,128)} %get-tuple-element.12.blocks_ref, bf16[256,256]{1,0:T(8,128)(2,1)} %gate_ref.1, bf16[256,256]{1,0:T(8,128)(2,1)} %key_ref.3, ...), custom_call_target="tpu_custom_call" | custom-call | flops 199999995904 | bytes 200000000 | tf_op jit(solution)/shard_map/gated_conv/pallas_call | solution.py:171
  37.2 0.0 copy-start.2
  37.2 3.4 %collective-permute-start.2 = (f32[256,256]{1,0:T(8,128)}, f32[256,256]{1,0:T(8,128)}, u32[]{:S(2)}, u32[]{:S(2)}) collective-permute-start(f32[256,256]{1,0:T(8,128)} %gated_conv.1.own_ref), channel_id=1, source_target_pairs={{0,288},{32,256},{256,32},{288,0},{1,289},{33,257},{257,33},{289,1... | collective-permute-start | bytes 786440 | tf_op jit(solution)/shard_map/ppermute | solution.py:319
  40.6 0.0 collective-permute-done.3
  40.6 18.7 %collective-permute-done.4 = f32[128,1024]{1,0:T(8,128)} collective-permute-done((f32[128,1024]{1,0:T(8,128)}, f32[128,1024]{1,0:T(8,128)}, u32[]{:S(2)}, u32[]{:S(2)}) %collective-permute-start.4) | collective-permute-done | bytes 524320 | tf_op jit(solution)/shard_map/ppermute | solution.py:307
  59.3 0.0 collective-permute-done.5
  59.3 1.5 %pad_maximum_fusion.near_ref = f32[384,1024]{1,0:T(8,128)S(1)} fusion(f32[128,1024]{1,0:T(8,128)} %collective-permute-done.5, f32[128,1024]{1,0:T(8,128)} %collective-permute-done.4, f32[128,1024]{1,0:T(8,128)} %collective-permute-done.3), kind=kLoop, calls=%fused_computation | loop fusion | flops 786432 | bytes 3145728 | tf_op jit(solution)/shard_map/concatenate | solution.py:320
  60.8 0.0 copy-start
  60.8 0.0 collective-permute-done.2.p3_ref
  60.8 3.5 %collective-permute-start.6 = (f32[384,1024]{1,0:T(8,128)S(1)}, f32[384,1024]{1,0:T(8,128)S(1)}, u32[]{:S(2)}, u32[]{:S(2)}) collective-permute-start(f32[384,1024]{1,0:T(8,128)S(1)} %pad_maximum_fusion.near_ref), channel_id=1, source_target_pairs={{0,1},{1,0},{2,3},{3,2},{4,5},{5,4},{6,7},{7,6},{8,9},{9,8},{10,11... | collective-permute-start | bytes 4718600 | tf_op jit(solution)/shard_map/ppermute | solution.py:322
  64.3 0.0 copy-done.2
  64.3 2.3 %collective-permute-start = (f32[256,256]{1,0:T(8,128)S(1)}, f32[256,256]{1,0:T(8,128)}, u32[]{:S(2)}, u32[]{:S(2)}) collective-permute-start(f32[256,256]{1,0:T(8,128)S(1)} %copy-done.2), channel_id=1, source_target_pairs={{0,32},{32,0},{256,288},{288,256},{1,33},{33,1},{257,289},{289,257... | collective-permute-start | bytes 786440 | tf_op jit(solution)/shard_map/ppermute | solution.py:319
  66.6 2.4 %collective-permute-start.1 = (f32[256,256]{1,0:T(8,128)S(1)}, f32[256,256]{1,0:T(8,128)}, u32[]{:S(2)}, u32[]{:S(2)}) collective-permute-start(f32[256,256]{1,0:T(8,128)S(1)} %copy-done.2), channel_id=1, source_target_pairs={{0,256},{32,288},{256,0},{288,32},{1,257},{33,289},{257,1},{289,33... | collective-permute-start | bytes 786440 | tf_op jit(solution)/shard_map/ppermute | solution.py:319
  69.0 0.0 collective-permute-done.6.far_ref
  69.0 0.0 copy-done
  69.0 0.0 copy-start.1
  69.0 1.1 copy-done.1
  70.2 4.9 %joined_weights.1.weight_ref = bf16[1024,1024]{1,0:T(8,128)(2,1)} custom-call(s32[4]{0:T(128)} %pad_add_fusion.place_ref, bf16[256,4096]{1,0:T(8,128)(2,1)} %wown_ref.1, f32[384,1024]{1,0:T(8,128)} %copy-done, f32[384,1024]{1,0:T(8,128)} %copy-done.1), custom_call_target="tpu_custom_call" | custom-call | flops 1000 | bytes 1000 | tf_op jit(solution)/shard_map/joined_weights/pallas_call | solution.py:249
  75.0 0.0 collective-permute-done.p1_ref
  75.0 1.2 %collective-permute-done.1.p2_ref = f32[256,256]{1,0:T(8,128)} collective-permute-done((f32[256,256]{1,0:T(8,128)S(1)}, f32[256,256]{1,0:T(8,128)}, u32[]{:S(2)}, u32[]{:S(2)}) %collective-permute-start.1) | collective-permute-done | bytes 262176 | tf_op jit(solution)/shard_map/ppermute | solution.py:319
  76.2 4.5 %project.1 = f32[4,256,256]{2,1,0:T(8,128)} custom-call(f32[256,256]{1,0:T(8,128)} %gated_conv.1.own_ref, f32[256,256]{1,0:T(8,128)} %collective-permute-done.p1_ref, f32[256,256]{1,0:T(8,128)} %collective-permute-done.1.p2_ref, f32[256,256]{1,0:T(8,128)} %collective-permute-done.2.p3_ref, bf16[1024,1024]{1,0:T(8,128)(2,1)} %joined_weights.1.weight_ref), custom_call_target="tpu_custom_call" | custom-call | tf_op jit(solution)/shard_map/project/pallas_call | solution.py:282
  80.7 32.7 %all_to_all.10 = f32[4,256,256]{2,1,0:T(8,128)S(1)} all-to-all(f32[4,256,256]{2,1,0:T(8,128)} %project.1), channel_id=1, replica_groups=mesh['xl'=2,'yh'=4,'yl'=2,'z'=8,'xh'=2,'core'=2] {'yh'}, dimensions={0} | all-to-all | bytes 2097152 | tf_op jit(solution)/shard_map/all_to_all | solution.py:325
  113.4 0.7 reduce_sum.9
Async XLA Ops:
  13.4 20.1 %all-to-all-start = ((f32[16,16,256]{2,1,0:T(8,128)}), f32[16,16,256]{2,1,0:T(8,128)S(1)}, u32[]{:S(2)}, u32[]{:S(2)}) async-start(f32[16,16,256]{2,1,0:T(8,128)} %spread_states.1), calls=%async_computation | async-start | bytes 524288 | tf_op jit(solution)/shard_map/all_to_all | solution.py:306
  24.3 16.3 %collective-permute-start.3 = (f32[128,1024]{1,0:T(8,128)}, f32[128,1024]{1,0:T(8,128)}, u32[]{:S(2)}, u32[]{:S(2)}) collective-permute-start(f32[128,1024]{1,0:T(8,128)} %get-tuple-element.13), channel_id=1, source_target_pairs={{0,32},{32,0},{256,288},{288,256},{1,33},{33,1},{257,289},{289,257... | collective-permute-start | bytes 1572872 | tf_op jit(solution)/shard_map/ppermute | solution.py:307
  27.5 31.8 %collective-permute-start.4 = (f32[128,1024]{1,0:T(8,128)}, f32[128,1024]{1,0:T(8,128)}, u32[]{:S(2)}, u32[]{:S(2)}) collective-permute-start(f32[128,1024]{1,0:T(8,128)} %get-tuple-element.14), channel_id=1, source_target_pairs={{0,256},{32,288},{256,0},{288,32},{1,257},{33,289},{257,1},{289,33... | collective-permute-start | bytes 1572872 | tf_op jit(solution)/shard_map/ppermute | solution.py:307
  29.7 29.6 %collective-permute-start.5 = (f32[128,1024]{1,0:T(8,128)}, f32[128,1024]{1,0:T(8,128)}, u32[]{:S(2)}, u32[]{:S(2)}) collective-permute-start(f32[128,1024]{1,0:T(8,128)} %get-tuple-element.15), channel_id=1, source_target_pairs={{0,288},{32,256},{256,32},{288,0},{1,289},{33,257},{257,33},{289,1... | collective-permute-start | bytes 1572872 | tf_op jit(solution)/shard_map/ppermute | solution.py:307
  37.2 27.1 %copy-start.2 = (f32[256,256]{1,0:T(8,128)S(1)}, f32[256,256]{1,0:T(8,128)}, u32[]{:S(2)}) copy-start(f32[256,256]{1,0:T(8,128)} %gated_conv.1.own_ref) | copy-start | bytes 786436
  37.2 23.6 %collective-permute-start.2 = (f32[256,256]{1,0:T(8,128)}, f32[256,256]{1,0:T(8,128)}, u32[]{:S(2)}, u32[]{:S(2)}) collective-permute-start(f32[256,256]{1,0:T(8,128)} %gated_conv.1.own_ref), channel_id=1, source_target_pairs={{0,288},{32,256},{256,32},{288,0},{1,289},{33,257},{257,33},{289,1... | collective-permute-start | bytes 786440 | tf_op jit(solution)/shard_map/ppermute | solution.py:319
  60.8 8.2 %copy-start = (f32[384,1024]{1,0:T(8,128)}, f32[384,1024]{1,0:T(8,128)S(1)}, u32[]{:S(2)}) copy-start(f32[384,1024]{1,0:T(8,128)S(1)} %pad_maximum_fusion.near_ref) | copy-start | bytes 4718596
  60.8 8.2 %collective-permute-start.6 = (f32[384,1024]{1,0:T(8,128)S(1)}, f32[384,1024]{1,0:T(8,128)S(1)}, u32[]{:S(2)}, u32[]{:S(2)}) collective-permute-start(f32[384,1024]{1,0:T(8,128)S(1)} %pad_maximum_fusion.near_ref), channel_id=1, source_target_pairs={{0,1},{1,0},{2,3},{3,2},{4,5},{5,4},{6,7},{7,6},{8,9},{9,8},{10,11... | collective-permute-start | bytes 4718600 | tf_op jit(solution)/shard_map/ppermute | solution.py:322
  64.3 10.7 %collective-permute-start = (f32[256,256]{1,0:T(8,128)S(1)}, f32[256,256]{1,0:T(8,128)}, u32[]{:S(2)}, u32[]{:S(2)}) collective-permute-start(f32[256,256]{1,0:T(8,128)S(1)} %copy-done.2), channel_id=1, source_target_pairs={{0,32},{32,0},{256,288},{288,256},{1,33},{33,1},{257,289},{289,257... | collective-permute-start | bytes 786440 | tf_op jit(solution)/shard_map/ppermute | solution.py:319
  66.6 9.6 %collective-permute-start.1 = (f32[256,256]{1,0:T(8,128)S(1)}, f32[256,256]{1,0:T(8,128)}, u32[]{:S(2)}, u32[]{:S(2)}) collective-permute-start(f32[256,256]{1,0:T(8,128)S(1)} %copy-done.2), channel_id=1, source_target_pairs={{0,256},{32,288},{256,0},{288,32},{1,257},{33,289},{257,1},{289,33... | collective-permute-start | bytes 786440 | tf_op jit(solution)/shard_map/ppermute | solution.py:319
  69.0 1.1 %copy-start.1 = (f32[384,1024]{1,0:T(8,128)}, f32[384,1024]{1,0:T(8,128)S(1)}, u32[]{:S(2)}) copy-start(f32[384,1024]{1,0:T(8,128)S(1)} %collective-permute-done.6.far_ref) | copy-start | bytes 4718596

commit v4 on v3

--- a/solution.py
+++ b/solution.py
@@ -185,36 +185,24 @@
     )(place, *args)
 
 
-def pick_kernel(place_ref, *refs):
-    for d in range(3):
-        out_ref = refs[12 + d]
-        for h in range(4):
-            out_ref[:, h * 256 : (h + 1) * 256] = refs[4 * d + h][...].astype(jnp.float32)
+def pick_kernel(place_ref, weight_ref, out_ref):
+    out_ref[...] = weight_ref[...].astype(jnp.float32)
 
 
 def picked_weights(place, weight):
     half = weight.shape[0] // 2
-    tile = 256
-
-    def spec(d, h):
-        return pl.BlockSpec(
-            (half, tile),
-            lambda i, p: (p[1], 8 * (p[2] ^ (d >> 1)) + 2 * h + (p[3] ^ (d & 1))),
-        )
-
-    specs = [spec(d, h) for d in (1, 2, 3) for h in range(4)]
-    shape = (half, 4 * tile)
+    cols = weight.shape[1] // 2
     return pl.pallas_call(
         pick_kernel,
-        out_shape=[jax.ShapeDtypeStruct(shape, jnp.float32)] * 3,
+        out_shape=jax.ShapeDtypeStruct((half, cols), jnp.float32),
         grid_spec=pltpu.PrefetchScalarGridSpec(
             num_scalar_prefetch=1,
             grid=(1,),
-            in_specs=specs,
-            out_specs=[whole(shape)] * 3,
+            in_specs=[pl.BlockSpec((half, cols), lambda i, p: (p[1], 1 - p[2]))],
+            out_specs=whole((half, cols)),
         ),
         name="picked_weights",
-    )(place, *[weight] * 12)
+    )(place, weight)
 
 
 def spread_kernel(pair_ref, decay_ref, out_ref, *, rows):
@@ -230,70 +218,92 @@
     )(pair, decay_rates)
 
 
-def weights_kernel(place_ref, wown_ref, near_ref, far_ref, out_ref):
-    half = wown_ref.shape[0] // 2
+def weights_kernel(place_ref, own_ref, near_ref, far_ref, out_ref):
+    half = near_ref.shape[0]
+    chans = 2 * half
     core = place_ref[1]
-    out_ref[: 2 * half, :] = wown_ref[...]
-    for d in range(3):
-        top = 2 * half * (d + 1)
-        part = pl.ds(d * half, half)
-        here = pl.ds(pl.multiple_of(top + core * half, half), half)
-        there = pl.ds(pl.multiple_of(top + (1 - core) * half, half), half)
-        out_ref[here, :] = near_ref[part, :].astype(jnp.bfloat16)
-        out_ref[there, :] = far_ref[part, :].astype(jnp.bfloat16)
+    parity = place_ref[3]
+    here = pl.ds(pl.multiple_of(chans + core * half, half), half)
+    there = pl.ds(pl.multiple_of(chans + (1 - core) * half, half), half)
+    for h in range(4):
+        for kept in range(2):
+            side = parity if kept else 1 - parity
+            source = pl.ds(pl.multiple_of((2 * h + side) * chans, chans), chans)
+            target = slice((4 * kept + h) * chans, (4 * kept + h + 1) * chans)
+            out_ref[:chans, target] = own_ref[:, source]
+            out_ref[here, target] = near_ref[:, source].astype(jnp.bfloat16)
+            out_ref[there, target] = far_ref[:, source].astype(jnp.bfloat16)
 
 
 def joined_weights(place, weight, near, far):
     chans = weight.shape[0]
-    other = pl.BlockSpec((near.shape[0], chans), lambda i, p: (0, i))
+    half, cols = near.shape
     return pl.pallas_call(
         weights_kernel,
-        out_shape=jax.ShapeDtypeStruct((4 * chans, 4 * chans), jnp.bfloat16),
+        out_shape=jax.ShapeDtypeStruct((2 * chans, cols), jnp.bfloat16),
         grid_spec=pltpu.PrefetchScalarGridSpec(
             num_scalar_prefetch=1,
-            grid=(4,),
+            grid=(1,),
             in_specs=[
-                pl.BlockSpec((chans, chans), lambda i, p: (0, 8 * p[2] + 2 * i + p[3])),
-                other,
-                other,
+                pl.BlockSpec((chans, cols), lambda i, p: (0, p[2])),
+                whole((half, cols)),
+                whole((half, cols)),
             ],
-            out_specs=pl.BlockSpec((4 * chans, chans), lambda i, p: (0, i)),
-        ),
-        cost_estimate=pl.CostEstimate(flops=1000, transcendentals=0, bytes_accessed=1000),
+            out_specs=whole((2 * chans, cols)),
+        ),
         name="joined_weights",
-    )(place, weight, *in_hbm(near, far))
-
-
-def project_kernel(own_ref, p1_ref, p2_ref, p3_ref, weight_ref, out_ref):
+    )(place, weight, near, far)
+
+
+def project_kernel(own_ref, peer_ref, weight_ref, out_ref):
     chans = own_ref.shape[1]
-    acc = None
-    for d, ref in enumerate((own_ref, p1_ref, p2_ref, p3_ref)):
-        term = jnp.dot(
-            ref[...].astype(jnp.bfloat16),
-            weight_ref[d * chans : (d + 1) * chans, :],
+    gated = jnp.concatenate([own_ref[...], peer_ref[...]], axis=1).astype(jnp.bfloat16)
+    for h in range(4):
+        out_ref[h] = jnp.dot(
+            gated,
+            weight_ref[:, h * chans : (h + 1) * chans],
             preferred_element_type=jnp.float32,
         )
-        acc = term if acc is None else acc + term
-    out_ref[0] = acc
-
-
-def project(own, peers, weight):
+
+
+def project(own, peer, weight, part, name):
     rows, chans = own.shape
     return pl.pallas_call(
         project_kernel,
         out_shape=jax.ShapeDtypeStruct((4, rows, chans), jnp.float32),
-        grid=(4,),
-        in_specs=[pl.BlockSpec((rows, chans), lambda i: (0, 0))] * 4
-        + [pl.BlockSpec((4 * chans, chans), lambda i: (0, i))],
-        out_specs=pl.BlockSpec((1, rows, chans), lambda i: (i, 0, 0)),
-        name="project",
-    )(*in_hbm(own, *peers), weight)
+        grid=(1,),
+        in_specs=[
+            whole((rows, chans)),
+            whole((rows, chans)),
+            pl.BlockSpec((2 * chans, 4 * chans), lambda i: (0, part)),
+        ],
+        out_specs=whole((4, rows, chans)),
+        name=name,
+    )(own, peer, weight)
+
+
+def neighbour_routes(count):
+    routes = []
+    for y in range(count):
+        routes.append((2 * y, 2 * (y ^ 1)))
+        other = (y + 1) % count if y % 2 else (y - 1) % count
+        routes.append((2 * y + 1, 2 * other + 1))
+    return routes
+
+
+def weight_routes():
+    routes = []
+    for side in range(2):
+        for xh in range(2):
+            for core in range(2):
+                source = 4 * side + 2 * xh + core
+                routes.append((source, 4 * (1 - side) + 2 * (xh ^ core) + core))
+    return routes
 
 
 def on_device(gate_stream, key_stream, value_stream, residues, decay_rates, out_weight):
     rows, chans = key_stream.shape
-    quad = ("xl", "yl")
-    routes = [[(g, g ^ d) for g in range(4)] for d in (1, 2, 3)]
+    swap = [(0, 1), (1, 0)]
     chip = lax.axis_index("z") * lax.axis_size("xh") + lax.axis_index("xh")
     place = jnp.stack(
         [chip, lax.axis_index("core"), lax.axis_index("xl"), lax.axis_index("yl")]
@@ -302,9 +312,11 @@
     pair = lax.all_gather(total, "core", axis=0)
     chips = lax.axis_size("z") * lax.axis_size("xh")
     copies = spread_states(pair, decay_rates, rows, chips)
+    states = lax.all_to_all(copies, ("z", "xh"), split_axis=0, concat_axis=0, tiled=True)
     sent = picked_weights(place, out_weight)
-    states = lax.all_to_all(copies, ("z", "xh"), split_axis=0, concat_axis=0, tiled=True)
-    near = [lax.ppermute(s, quad, r) for s, r in zip(sent, routes)]
+    near = lax.ppermute(sent, ("xl", "xh", "core"), weight_routes())
+    far = lax.ppermute(near, "core", swap)
+    weight = joined_weights(place, out_weight, near, far)
     own = gated_conv(
         place,
         states,
@@ -316,13 +328,11 @@
         residues,
         decay_rates,
     )
-    peers = [lax.ppermute(own, quad, r) for r in routes]
-    near = jnp.concatenate(near, axis=0)
-    near, _ = lax.optimization_barrier((near, peers[2]))
-    far = lax.ppermute(near, "core", [(0, 1), (1, 0)])
-    weight = joined_weights(place, out_weight, near, far)
-    partial = project(own, peers, weight)
-    parts = lax.all_to_all(partial, "yh", split_axis=0, concat_axis=0, tiled=True)
+    peer = lax.ppermute(own, "xl", swap)
+    leaving = project(own, peer, weight, 0, "project_leaving")
+    arrived = lax.ppermute(leaving, ("yh", "yl", "core"), neighbour_routes(8))
+    kept = project(own, peer, weight, 1, "project_kept")
+    parts = lax.all_to_all(kept + arrived, "yh", split_axis=0, concat_axis=0, tiled=True)
     return jnp.sum(parts, axis=0).astype(jnp.bfloat16)
 
 

time: 116 us -> 108 us (0.931)
  blocking collectives: 42.5 us -> 38 us
  starting transfers between devices: 27.1 us -> 23 us
  waiting for transfers between devices: 20.7 us -> 22.2 us
    all_to_all x1, waiting for transfers between devices: 0.76 us -> 10.4 us  [on_device(): lax.all_to_all(copies, ('z', 'xh'), split_axis=0, concat_axis=0, tiled=True)]
    ppermute x7 -> x4, waiting for transfers between devices: 20 us -> 11.8 us  [the longest x1 9.56 us: on_device(): arrived = lax.ppermute(leaving, ('yh', 'yl', 'core'), neighbour_routes(8))]
    ppermute x7 -> x4, starting transfers between devices: 19.9 us -> 14.6 us  [the longest x1 5.21 us: on_device(): near = lax.ppermute(sent, ('xl', 'xh', 'core'), weight_routes())]
    all_gather x1, blocking collectives: 9.85 us -> 6.55 us  [on_device(): pair = lax.all_gather(total, 'core', axis=0)]
    concatenate x1 -> x0, other arithmetic: 1.46 us -> none  [on_device(): near = jnp.concatenate(near, axis=0)]
    add x0 -> x1, other arithmetic: none -> 1.36 us  [on_device(): kept + arrived]
    all_to_all x1, blocking collectives: 32.7 us -> 31.4 us  [on_device(): lax.all_to_all(kept + arrived, 'yh', split_axis=0, concat_axis=0, tiled=T...]
    all_to_all x1, starting transfers between devices: 7.23 us -> 8.41 us  [on_device(): lax.all_to_all(copies, ('z', 'xh'), split_axis=0, concat_axis=0, tiled=True)]
  transfers between devices with their start and end apart: 8 -> 5, of which waited for: 3 -> 3; matrix products, arithmetic and copies ran while one was open for 2% -> 0% of each run, Pallas kernels for 10% -> 13%
where the time goes in v4:
time: 108 us; the launch traced here: 107 us
  blocking collectives  38 us (35%)
  starting transfers between devices  23 us (21%)
  waiting for transfers between devices  22.2 us (21%)
  Pallas kernels  19.8 us (18%)
  other arithmetic  2.75 us (3%)
    all_to_all x1, blocking collectives, on_device(): lax.all_to_all(kept + arrived, 'yh', split_axis=0, concat_axis=0, tiled=T...  31.4 us
    all_to_all x1, waiting for transfers between devices, on_device(): lax.all_to_all(copies, ('z', 'xh'), split_axis=0, concat_axis=0, tiled=True)  10.4 us
    ppermute x1, waiting for transfers between devices, on_device(): arrived = lax.ppermute(leaving, ('yh', 'yl', 'core'), neighbour_routes(8))  9.56 us
    all_to_all x1, starting transfers between devices, on_device(): lax.all_to_all(copies, ('z', 'xh'), split_axis=0, concat_axis=0, tiled=True)  8.41 us
    all_gather x1, blocking collectives, on_device(): pair = lax.all_gather(total, 'core', axis=0)  6.55 us
    pallas_call x2, Pallas kernels, project(): pl.pallas_call(project_kernel, out_shape=jax.ShapeDtypeStruct((4, rows, c...  5.63 us
    ppermute x1, starting transfers between devices, on_device(): near = lax.ppermute(sent, ('xl', 'xh', 'core'), weight_routes())  5.21 us
    ppermute x1, starting transfers between devices, on_device(): arrived = lax.ppermute(leaving, ('yh', 'yl', 'core'), neighbour_routes(8))  5.09 us
  transfers between devices with their start and end apart: 5, of which 3 were waited for; matrix products, arithmetic and copies ran while one was open for 0% of the time, Pallas kernels for 13%

profile of v4, /device:TPU:1, one launch (start us, length us, event | category | flops | bytes accessed | tf_op | source)
XLA Modules:
  0.0 106.5 jit_solution(2020784447376231993)
XLA Ops:
  0.0 0.7 pad_add_fusion.place_ref
  0.7 2.7 %picked_weights.1 = f32[128,2048]{1,0:T(8,128)} custom-call(s32[4]{0:T(128)} %pad_add_fusion.place_ref, bf16[256,4096]{1,0:T(8,128)(2,1)} %own_ref.1), custom_call_target="tpu_custom_call" | custom-call | tf_op jit(solution)/shard_map/picked_weights/pallas_call | solution.py:195
  3.4 5.2 %collective-permute-start.1 = (f32[128,2048]{1,0:T(8,128)}, f32[128,2048]{1,0:T(8,128)}, u32[]{:S(2)}, u32[]{:S(2)}) collective-permute-start(f32[128,2048]{1,0:T(8,128)} %picked_weights.1), channel_id=1, source_target_pairs={{0,256},{1,259},{2,258},{3,257},{256,0},{257,3},{258,2},{259,1},{4... | collective-permute-start | bytes 3145736 | tf_op jit(solution)/shard_map/ppermute | solution.py:317
  8.6 2.0 %local_states.1 = (f32[4,16,256]{2,1,0:T(8,128)}, f32[16,256]{1,0:T(8,128)}) custom-call(bf16[256,256]{1,0:T(8,128)(2,1)} %key_ref.3, bf16[256,256]{1,0:T(8,128)(2,1)} %value_ref.3, f32[16,256]{1,0:T(8,128)} %decay_ref.3), custom_call_target="tpu_custom_call" | custom-call | tf_op jit(solution)/shard_map/local_states/pallas_call | solution.py:76
  10.7 6.6 %all-gather = f32[32,256]{1,0:T(8,128)} all-gather(f32[16,256]{1,0:T(8,128)} %get-tuple-element.7), channel_id=2, replica_groups=mesh['xl'=2,'yh'=4,'yl'=2,'z'=8,'xh'=2,'core'=2] {'core'}, dimensions={0}, use_global_device_ids=true | all-gather | bytes 49152 | tf_op jit(solution)/shard_map/all_gather | solution.py:312
  17.2 1.5 %spread_states.1 = f32[16,16,256]{2,1,0:T(8,128)} custom-call(f32[2,16,256]{2,1,0:T(8,128)} %bitcast.5, f32[16,256]{1,0:T(8,128)} %decay_ref.3), custom_call_target="tpu_custom_call" | custom-call | tf_op jit(solution)/shard_map/spread_states/pallas_call | solution.py:214
  18.7 8.4 %all-to-all-start = ((f32[16,16,256]{2,1,0:T(8,128)}), f32[16,16,256]{2,1,0:T(8,128)S(1)}, u32[]{:S(2)}, u32[]{:S(2)}) async-start(f32[16,16,256]{2,1,0:T(8,128)} %spread_states.1), calls=%async_computation | async-start | bytes 524288 | tf_op jit(solution)/shard_map/all_to_all | solution.py:315
  27.1 0.0 collective-permute-done.1.near_ref
  27.1 2.4 %collective-permute-start.2 = (f32[128,2048]{1,0:T(8,128)}, f32[128,2048]{1,0:T(8,128)}, u32[]{:S(2)}, u32[]{:S(2)}) collective-permute-start(f32[128,2048]{1,0:T(8,128)} %collective-permute-done.1.near_ref), channel_id=1, source_target_pairs={{0,1},{1,0},{2,3},{3,2},{4,5},{5,4},{6,7},{7,6},{8,9},{9,8},{10,11... | collective-permute-start | bytes 3145736 | tf_op jit(solution)/shard_map/ppermute | solution.py:318
  29.5 10.4 %all-to-all-done.chips_ref = f32[16,16,256]{2,1,0:T(8,128)S(1)} async-done(((f32[16,16,256]{2,1,0:T(8,128)}), f32[16,16,256]{2,1,0:T(8,128)S(1)}, u32[]{:S(2)}, u32[]{:S(2)}) %all-to-all-start) | async-done | bytes 262176 | tf_op jit(solution)/shard_map/all_to_all | solution.py:315
  39.9 3.7 %gated_conv.1.own_ref = f32[256,256]{1,0:T(8,128)} custom-call(s32[4]{0:T(128)} %pad_add_fusion.place_ref, f32[16,16,256]{2,1,0:T(8,128)S(1)} %all-to-all-done.chips_ref, f32[2,16,256]{2,1,0:T(8,128)} %bitcast.6, f32[4,16,256]{2,1,0:T(8,128)} %get-tuple-element.8.blocks_ref, bf16[256,256]{1,0:T(8,128)(2,1)} %gate_ref.1, bf16[256,256]{1,0:T(8,128)(2,1)} %key_ref.3, ...), custom_call_target="tpu_custom_call" | custom-call | flops 199999995904 | bytes 200000000 | tf_op jit(solution)/shard_map/gated_conv/pallas_call | solution.py:171
  43.7 1.9 %collective-permute-start = (f32[256,256]{1,0:T(8,128)}, f32[256,256]{1,0:T(8,128)S(1)}, u32[]{:S(2)}, u32[]{:S(2)}) collective-permute-start(f32[256,256]{1,0:T(8,128)} %gated_conv.1.own_ref), channel_id=1, source_target_pairs={{0,256},{256,0},{1,257},{257,1},{2,258},{258,2},{3,259},{259,3},{4... | collective-permute-start | bytes 786440 | tf_op jit(solution)/shard_map/ppermute | solution.py:331
  45.6 0.0 collective-permute-done.2.far_ref
  45.6 4.2 %joined_weights.1.weight_ref = bf16[512,2048]{1,0:T(8,128)(2,1)} custom-call(s32[4]{0:T(128)} %pad_add_fusion.place_ref, bf16[256,4096]{1,0:T(8,128)(2,1)} %own_ref.1, f32[128,2048]{1,0:T(8,128)} %collective-permute-done.1.near_ref, f32[128,2048]{1,0:T(8,128)} %collective-permute-done.2.far_ref), custom_call_target="tpu_custom_call" | custom-call | tf_op jit(solution)/shard_map/joined_weights/pallas_call | solution.py:241
  49.8 2.2 %collective-permute-done.peer_ref = f32[256,256]{1,0:T(8,128)S(1)} collective-permute-done((f32[256,256]{1,0:T(8,128)}, f32[256,256]{1,0:T(8,128)S(1)}, u32[]{:S(2)}, u32[]{:S(2)}) %collective-permute-start) | collective-permute-done | bytes 262176 | tf_op jit(solution)/shard_map/ppermute | solution.py:331
  52.0 0.0 copy-start
  52.0 0.7 copy-done
  52.7 2.8 %project_leaving.1 = f32[4,256,256]{2,1,0:T(8,128)} custom-call(f32[256,256]{1,0:T(8,128)} %gated_conv.1.own_ref, f32[256,256]{1,0:T(8,128)} %copy-done, bf16[512,2048]{1,0:T(8,128)(2,1)} %joined_weights.1.weight_ref), custom_call_target="tpu_custom_call" | custom-call | tf_op jit(solution)/shard_map/project_leaving/pallas_call | solution.py:271
  55.5 5.1 %collective-permute-start.3 = (f32[4,256,256]{2,1,0:T(8,128)}, f32[4,256,256]{2,1,0:T(8,128)S(1)}, u32[]{:S(2)}, u32[]{:S(2)}) collective-permute-start(f32[4,256,256]{2,1,0:T(8,128)} %project_leaving.1), channel_id=1, source_target_pairs={{0,32},{1,225},{32,0},{33,65},{64,96},{65,33},{96,64},{97,129},{12... | collective-permute-start | bytes 3145736 | tf_op jit(solution)/shard_map/ppermute | solution.py:333
  60.6 2.8 %project_kept.1 = f32[4,256,256]{2,1,0:T(8,128)} custom-call(f32[256,256]{1,0:T(8,128)} %gated_conv.1.own_ref, f32[256,256]{1,0:T(8,128)} %copy-done, bf16[512,2048]{1,0:T(8,128)(2,1)} %joined_weights.1.weight_ref), custom_call_target="tpu_custom_call" | custom-call | tf_op jit(solution)/shard_map/project_kept/pallas_call | solution.py:271
  63.4 9.6 %collective-permute-done.3 = f32[4,256,256]{2,1,0:T(8,128)S(1)} collective-permute-done((f32[4,256,256]{2,1,0:T(8,128)}, f32[4,256,256]{2,1,0:T(8,128)S(1)}, u32[]{:S(2)}, u32[]{:S(2)}) %collective-permute-start.3) | collective-permute-done | bytes 1048608 | tf_op jit(solution)/shard_map/ppermute | solution.py:333
  73.0 1.4 %add.7 = f32[4,256,256]{2,1,0:T(8,128)S(1)} add(f32[4,256,256]{2,1,0:T(8,128)} %project_kept.1, f32[4,256,256]{2,1,0:T(8,128)S(1)} %collective-permute-done.3) | non-fusion elementwise | flops 262144 | bytes 3145728 | tf_op jit(solution)/shard_map/add | solution.py:335
  74.3 31.4 %all_to_all.10 = f32[4,256,256]{2,1,0:T(8,128)S(1)} all-to-all(f32[4,256,256]{2,1,0:T(8,128)S(1)} %add.7), channel_id=1, replica_groups=mesh['xl'=2,'yh'=4,'yl'=2,'z'=8,'xh'=2,'core'=2] {'yh'}, dimensions={0} | all-to-all | bytes 2097152 | tf_op jit(solution)/shard_map/all_to_all | solution.py:335
  105.8 0.7 reduce_sum.9
Async XLA Ops:
  3.4 23.7 %collective-permute-start.1 = (f32[128,2048]{1,0:T(8,128)}, f32[128,2048]{1,0:T(8,128)}, u32[]{:S(2)}, u32[]{:S(2)}) collective-permute-start(f32[128,2048]{1,0:T(8,128)} %picked_weights.1), channel_id=1, source_target_pairs={{0,256},{1,259},{2,258},{3,257},{256,0},{257,3},{258,2},{259,1},{4... | collective-permute-start | bytes 3145736 | tf_op jit(solution)/shard_map/ppermute | solution.py:317
  18.7 21.2 %all-to-all-start = ((f32[16,16,256]{2,1,0:T(8,128)}), f32[16,16,256]{2,1,0:T(8,128)S(1)}, u32[]{:S(2)}, u32[]{:S(2)}) async-start(f32[16,16,256]{2,1,0:T(8,128)} %spread_states.1), calls=%async_computation | async-start | bytes 524288 | tf_op jit(solution)/shard_map/all_to_all | solution.py:315
  27.1 18.5 %collective-permute-start.2 = (f32[128,2048]{1,0:T(8,128)}, f32[128,2048]{1,0:T(8,128)}, u32[]{:S(2)}, u32[]{:S(2)}) collective-permute-start(f32[128,2048]{1,0:T(8,128)} %collective-permute-done.1.near_ref), channel_id=1, source_target_pairs={{0,1},{1,0},{2,3},{3,2},{4,5},{5,4},{6,7},{7,6},{8,9},{9,8},{10,11... | collective-permute-start | bytes 3145736 | tf_op jit(solution)/shard_map/ppermute | solution.py:318
  43.7 8.3 %collective-permute-start = (f32[256,256]{1,0:T(8,128)}, f32[256,256]{1,0:T(8,128)S(1)}, u32[]{:S(2)}, u32[]{:S(2)}) collective-permute-start(f32[256,256]{1,0:T(8,128)} %gated_conv.1.own_ref), channel_id=1, source_target_pairs={{0,256},{256,0},{1,257},{257,1},{2,258},{258,2},{3,259},{259,3},{4... | collective-permute-start | bytes 786440 | tf_op jit(solution)/shard_map/ppermute | solution.py:331
  52.0 0.7 copy-start
  55.5 17.5 %collective-permute-start.3 = (f32[4,256,256]{2,1,0:T(8,128)}, f32[4,256,256]{2,1,0:T(8,128)S(1)}, u32[]{:S(2)}, u32[]{:S(2)}) collective-permute-start(f32[4,256,256]{2,1,0:T(8,128)} %project_leaving.1), channel_id=1, source_target_pairs={{0,32},{1,225},{32,0},{33,65},{64,96},{65,33},{96,64},{97,129},{12... | collective-permute-start | bytes 3145736 | tf_op jit(solution)/shard_map/ppermute | solution.py:333

commit v5 on v4

v5 whole, which is shorter than its diff:
```python
import functools

import jax
import jax.numpy as jnp
from jax import lax
from jax.experimental import pallas as pl
from jax.experimental.pallas import tpu as pltpu
from jax.sharding import Mesh, PartitionSpec as P

BLOCK = 64
LANES = 128
SUB = 8


def near_core(array):
    return pltpu.with_memory_space_constraint(array, pltpu.VMEM)


def whole(shape):
    return pl.BlockSpec(shape, lambda *_: (0,) * len(shape))


def minus_expm1(x):
    series = 1.0 - x / 8.0
    for k in (7.0, 6.0, 5.0, 4.0, 3.0, 2.0):
        series = 1.0 - x / k * series
    return jnp.where(x < 0.5, x * series, 1.0 - jnp.exp(-x))


def sub_iota():
    return lax.broadcasted_iota(jnp.int32, (SUB, LANES), 0)


def state_kernel(key_ref, value_ref, decay_ref, blocks_ref, copies_ref):
    modes = decay_ref.shape[0]
    count = key_ref.shape[0] // BLOCK
    tiles = BLOCK // SUB
    back = (SUB - 1 - sub_iota()).astype(jnp.float32)

    def lane_group(g, carry):
        lanes = pl.ds(pl.multiple_of(g * LANES, LANES), LANES)
        decay = decay_ref[:, lanes]
        lam8 = jnp.exp(-decay * SUB)
        step = [jnp.broadcast_to(lam8[n : n + 1], (SUB, LANES)) for n in range(modes)]
        lam_block = jnp.exp(-decay * BLOCK)
        ends = [jnp.exp(-decay[n : n + 1] * back) for n in range(modes)]
        total = jnp.zeros((modes, LANES), jnp.float32)
        for b in range(count):
            acc = [None] * modes
            for j in range(tiles):
                rows = pl.ds(b * BLOCK + j * SUB, SUB)
                mixed = key_ref[rows, lanes].astype(jnp.float32) * value_ref[
                    rows, lanes
                ].astype(jnp.float32)
                for n in range(modes):
                    acc[n] = mixed if j == 0 else acc[n] * step[n] + mixed
            rows = [
                jnp.sum(acc[n] * ends[n], axis=0, keepdims=True) for n in range(modes)
            ]
            state = jnp.concatenate(rows, axis=0)
            blocks_ref[b, :, lanes] = state
            total = total * lam_block + state
        for j in range(copies_ref.shape[0]):
            copies_ref[j, :, lanes] = total
        return carry

    lax.fori_loop(0, decay_ref.shape[1] // LANES, lane_group, 0)


def local_states(key_stream, value_stream, decay_rates, chips):
    rows, chans = key_stream.shape
    modes = decay_rates.shape[0]
    return pl.pallas_call(
        state_kernel,
        out_shape=(
            jax.ShapeDtypeStruct((rows // BLOCK, modes, chans), jnp.float32),
            jax.ShapeDtypeStruct((chips, modes, chans), jnp.float32),
        ),
        name="local_states",
    )(key_stream, value_stream, decay_rates)


def local_kernel(
    blocks_ref, gate_ref, key_ref, value_ref, residues_ref, decay_ref, out_ref, taps_ref
):
    modes = decay_ref.shape[0]
    rows = key_ref.shape[0]
    count = rows // BLOCK
    tiles = BLOCK // SUB
    sub = sub_iota()
    ahead = sub.astype(jnp.float32)

    def lane_group(g, carry):
        lanes = pl.ds(pl.multiple_of(g * LANES, LANES), LANES)
        decay = decay_ref[:, lanes]
        base = residues_ref[:, lanes] * jnp.sqrt(minus_expm1(2.0 * decay))
        lam8 = jnp.exp(-decay * float(SUB))
        step = [jnp.broadcast_to(lam8[n : n + 1], (SUB, LANES)) for n in range(modes)]
        within = [jnp.exp(-decay[n : n + 1] * ahead) for n in range(modes)]
        kernel = [base[n : n + 1] * within[n] for n in range(modes)]
        for j in range(tiles):
            taps_ref[pl.ds(j * SUB, SUB), :] = sum(kernel)
            if j + 1 < tiles:
                kernel = [kernel[n] * step[n] for n in range(modes)]
        scale = base * jnp.exp(-decay)
        out_ref[2 * rows : 2 * rows + modes, lanes] = decay
        out_ref[2 * rows + modes :, lanes] = scale
        fade = None
        for b in range(count):
            if b:
                entry = scale * blocks_ref[b - 1, :, lanes]
                entry = [entry[n : n + 1] * within[n] for n in range(modes)]
                if fade is None:
                    fade = entry
                else:
                    fade = [fade[n] + entry[n] for n in range(modes)]
            acc = []
            mixed = []
            for j in range(tiles):
                at = pl.ds(b * BLOCK + j * SUB, SUB)
                if fade is None:
                    acc.append(jnp.zeros((SUB, LANES), jnp.float32))
                else:
                    acc.append(sum(fade))
                    fade = [fade[n] * step[n] for n in range(modes)]
                mixed.append(
                    key_ref[at, lanes].astype(jnp.float32)
                    * value_ref[at, lanes].astype(jnp.float32)
                )
            for r in range(SUB):
                if r == 0:
                    moved = mixed
                else:
                    rolled = [pltpu.roll(tile, r, 0) for tile in mixed]
                    moved = []
                    for j in range(tiles):
                        above = rolled[j - 1] if j else jnp.zeros_like(rolled[0])
                        moved.append(jnp.where(sub < r, above, rolled[j]))
                for q in range(tiles):
                    tap = taps_ref[pl.ds(q * SUB + r, 1), :]
                    for j in range(q, tiles):
                        acc[j] = acc[j] + tap * moved[j - q]
            for j in range(tiles):
                row = b * BLOCK + j * SUB
                gate = gate_ref[pl.ds(row, SUB), lanes].astype(jnp.float32)
                out_ref[pl.ds(row, SUB), lanes] = gate * acc[j]
                out_ref[pl.ds(rows + row, SUB), lanes] = gate
        return carry

    lax.fori_loop(0, decay_ref.shape[1] // LANES, lane_group, 0)


def local_conv(blocks, gate, key, value, residues, decay):
    rows, chans = key.shape
    modes = decay.shape[0]
    return pl.pallas_call(
        local_kernel,
        out_shape=jax.ShapeDtypeStruct((2 * (rows + modes), chans), jnp.float32),
        scratch_shapes=[pltpu.VMEM((BLOCK, LANES), jnp.float32)],
        name="local_conv",
    )(blocks, gate, key, value, residues, decay)


def scan_kernel(place_ref, chips_ref, own_ref, decay_ref, out_ref, *, rows):
    lam_chip = jnp.exp(-decay_ref[...] * float(2 * rows))
    before = jnp.zeros_like(lam_chip)
    for j in range(chips_ref.shape[0]):
        before = jnp.where(
            j < place_ref[0], before * lam_chip + chips_ref[j], before
        )
    out_ref[0] = before
    out_ref[1] = own_ref[0]


def chip_scan(place, chips, copies, decay, rows):
    shape = (2,) + decay.shape
    return pl.pallas_call(
        functools.partial(scan_kernel, rows=rows),
        out_shape=jax.ShapeDtypeStruct(shape, jnp.float32),
        grid_spec=pltpu.PrefetchScalarGridSpec(
            num_scalar_prefetch=1,
            grid=(1,),
            in_specs=[whole(chips.shape), whole((1,) + decay.shape), whole(decay.shape)],
            out_specs=whole(shape),
        ),
        cost_estimate=pl.CostEstimate(
            flops=2 * 10**11, transcendentals=0, bytes_accessed=2 * 10**8
        ),
        name="chip_scan",
    )(place, near_core(chips), copies, decay)


def gate_kernel(place_ref, states_ref, own_ref, peer_ref, out_ref):
    modes = states_ref.shape[2]
    chans = own_ref.shape[1]
    rows = out_ref.shape[0]
    core = place_ref[1]
    ahead = sub_iota().astype(jnp.float32)

    for part, pack_ref in enumerate((own_ref, peer_ref)):
        side = place_ref[2] if part == 0 else 1 - place_ref[2]

        def lane_group(g, carry, part=part, pack_ref=pack_ref, side=side):
            start = pl.multiple_of(g * LANES, LANES)
            lanes = pl.ds(start, LANES)
            decay = pack_ref[2 * rows : 2 * rows + modes, lanes]
            scale = pack_ref[2 * rows + modes :, lanes]
            lam_rows = jnp.exp(-decay * float(rows))
            before = states_ref[2 * side, 0, :, lanes] * lam_rows
            before = before + states_ref[2 * side + 1, 0, :, lanes]
            after = before * lam_rows + states_ref[2 * side, 1, :, lanes]
            entry = scale * jnp.where(core == 0, before, after)
            lam8 = jnp.exp(-decay * float(SUB))
            step = [
                jnp.broadcast_to(lam8[n : n + 1], (SUB, LANES)) for n in range(modes)
            ]
            fade = [
                entry[n : n + 1] * jnp.exp(-decay[n : n + 1] * ahead)
                for n in range(modes)
            ]
            target = pl.ds(pl.multiple_of(part * chans + start, LANES), LANES)
            for j in range(0, rows, 2 * SUB):
                tiles = []
                for row in (j, j + SUB):
                    gate = pack_ref[pl.ds(rows + row, SUB), lanes]
                    tiles.append(pack_ref[pl.ds(row, SUB), lanes] + gate * sum(fade))
                    fade = [fade[n] * step[n] for n in range(modes)]
                out_ref[pl.ds(j, 2 * SUB), target] = jnp.concatenate(tiles).astype(
                    jnp.bfloat16
                )
            return carry

        lax.fori_loop(0, chans // LANES, lane_group, 0)


def gated_both(place, states, own, peer, rows):
    chans = own.shape[1]
    args = (states, own, peer)
    return pl.pallas_call(
        gate_kernel,
        out_shape=jax.ShapeDtypeStruct((rows, 2 * chans), jnp.bfloat16),
        grid_spec=pltpu.PrefetchScalarGridSpec(
            num_scalar_prefetch=1,
            grid=(1,),
            in_specs=[whole(a.shape) for a in args],
            out_specs=whole((rows, 2 * chans)),
        ),
        name="gated_both",
    )(place, *args)


def weights_kernel(place_ref, own_ref, near_ref, far_ref, out_ref):
    half = near_ref.shape[0]
    chans = 2 * half
    core = place_ref[1]
    parity = place_ref[3]
    here = pl.ds(pl.multiple_of(chans + core * half, half), half)
    there = pl.ds(pl.multiple_of(chans + (1 - core) * half, half), half)
    for kept in range(2):
        side = parity if kept else 1 - parity
        source = pl.ds(pl.multiple_of(side * chans, chans), chans)
        out_ref[kept, :chans, :] = own_ref[:, source]
        out_ref[kept, here, :] = near_ref[:, source].astype(jnp.bfloat16)
        out_ref[kept, there, :] = far_ref[:, source].astype(jnp.bfloat16)


def joined_weights(place, weight, near, far):
    chans = weight.shape[0]
    half, cols = near.shape
    wide = pl.BlockSpec((half, 2 * chans), lambda i, p: (0, i))
    return pl.pallas_call(
        weights_kernel,
        out_shape=jax.ShapeDtypeStruct((2, 2 * chans, cols // 2), jnp.bfloat16),
        grid_spec=pltpu.PrefetchScalarGridSpec(
            num_scalar_prefetch=1,
            grid=(4,),
            in_specs=[
                pl.BlockSpec((chans, 2 * chans), lambda i, p: (0, 4 * p[2] + i)),
                wide,
                wide,
            ],
            out_specs=pl.BlockSpec((2, 2 * chans, chans), lambda i, p: (0, 0, i)),
        ),
        name="joined_weights",
    )(place, weight, near, far)


def project_kernel(gated_ref, weight_ref, out_ref):
    chans = out_ref.shape[2]
    for h in range(4):
        out_ref[h] = jnp.dot(
            gated_ref[...],
            weight_ref[:, h * chans : (h + 1) * chans],
            preferred_element_type=jnp.float32,
        )


def project(gated, weight, part, name):
    rows, deep = gated.shape
    cols = weight.shape[2]
    return pl.pallas_call(
        project_kernel,
        out_shape=jax.ShapeDtypeStruct((4, rows, cols // 4), jnp.float32),
        grid=(1,),
        in_specs=[
            whole((rows, deep)),
            pl.BlockSpec((None, deep, cols), lambda i: (part, 0, 0)),
        ],
        out_specs=whole((4, rows, cols // 4)),
        name=name,
    )(gated, weight)


def neighbour_routes(count):
    routes = []
    for y in range(count):
        routes.append((2 * y, 2 * (y ^ 1)))
        other = (y + 1) % count if y % 2 else (y - 1) % count
        routes.append((2 * y + 1, 2 * other + 1))
    return routes


def weight_routes():
    routes = []
    for side in range(2):
        for xh in range(2):
            for core in range(2):
                source = 4 * side + 2 * xh + core
                routes.append((source, 4 * (1 - side) + 2 * (xh ^ core) + core))
    return routes


def on_device(gate_stream, key_stream, value_stream, residues, decay_rates, out_weight):
    rows, chans = key_stream.shape
    swap = [(0, 1), (1, 0)]
    chip = lax.axis_index("z") * lax.axis_size("xh") + lax.axis_index("xh")
    core = lax.axis_index("core")
    side = lax.axis_index("xl")
    place = jnp.stack([chip, core, side, lax.axis_index("yl")]).astype(jnp.int32)
    half, cols = chans // 2, out_weight.shape[1] // 2
    sent = lax.dynamic_slice(
        out_weight, (core * half, (1 - side) * cols), (half, cols)
    ).astype(jnp.float32)
    near = lax.ppermute(sent, ("xl", "xh", "core"), weight_routes())
    far = lax.ppermute(near, "core", swap)
    weight = joined_weights(place, out_weight, near, far)

    chips = lax.axis_size("z") * lax.axis_size("xh")
    blocks, copies = local_states(key_stream, value_stream, decay_rates, chips)
    states = lax.all_to_all(copies, ("z", "xh"), split_axis=0, concat_axis=0, tiled=True)
    own = local_conv(
        blocks, gate_stream, key_stream, value_stream, residues, decay_rates
    )
    peer = lax.ppermute(own, "xl", swap)
    scanned = chip_scan(place, states, copies, decay_rates, rows)
    scanned = lax.all_gather(scanned, ("xl", "core"), axis=0)
    gated = gated_both(place, scanned, own, peer, rows)
    leaving = project(gated, weight, 0, "project_leaving")
    arrived = lax.ppermute(leaving, ("yh", "yl", "core"), neighbour_routes(8))
    kept = project(gated, weight, 1, "project_kept")
    parts = lax.all_to_all(kept + arrived, "yh", split_axis=0, concat_axis=0, tiled=True)
    return jnp.sum(parts, axis=0).astype(jnp.bfloat16)


def solution(mesh):
    inner = Mesh(
        mesh.devices.reshape(2, 4, 2, 8, 2, 2), ("xl", "yh", "yl", "z", "xh", "core")
    )
    time = ("z", "xh", "core")
    chan = ("xl", "yh", "yl")
    return jax.shard_map(
        on_device,
        mesh=inner,
        in_specs=(
            P(time, chan),
            P(time, chan),
            P(time, chan),
            P(None, chan),
            P(None, chan),
            P(chan, None),
        ),
        out_specs=P(time, chan),
        check_vma=False,
    )
```

time: 108 us -> 106 us (0.981)
  waiting for transfers between devices: 22.2 us -> 11.3 us
  blocking collectives: 38 us -> 42 us
  starting transfers between devices: 23 us -> 26.6 us
  other arithmetic: 2.75 us -> 3.89 us
    all_to_all x1, waiting for transfers between devices: 10.4 us -> 1.64 us  [on_device(): lax.all_to_all(copies, ('z', 'xh'), split_axis=0, concat_axis=0, tiled=True)]
    all_gather x1, blocking collectives: 6.55 us -> 9.7 us  [on_device(): scanned = lax.all_gather(scanned, ('xl', 'core'), axis=0)]
    ppermute x1, waiting for transfers between devices: 2.19 us -> 0.01 us  [on_device(): peer = lax.ppermute(own, 'xl', swap)]
    all_to_all x1, starting transfers between devices: 8.41 us -> 10.4 us  [on_device(): lax.all_to_all(copies, ('z', 'xh'), split_axis=0, concat_axis=0, tiled=True)]
    ppermute x1, starting transfers between devices: 2.36 us -> 3.76 us  [on_device(): far = lax.ppermute(near, 'core', swap)]
    convert_element_type x0 -> x1, other arithmetic: none -> 1.13 us  [on_device(): sent = lax.dynamic_slice(out_weight, (core * half, (1 - side) * cols), (h...]
  transfers between devices with their start and end apart: 5 -> 5, of which waited for: 3 -> 2; matrix products, arithmetic and copies ran while one was open for 0% -> 1% of each run, Pallas kernels for 13% -> 13%
where the time goes in v5:
time: 106 us; the launch traced here: 105 us
  blocking collectives  42 us (40%)
  starting transfers between devices  26.6 us (25%)
  Pallas kernels  20.8 us (20%)
  waiting for transfers between devices  11.3 us (11%)
  other arithmetic  3.89 us (4%)
    all_to_all x1, blocking collectives, on_device(): lax.all_to_all(kept + arrived, 'yh', split_axis=0, concat_axis=0, tiled=T...  32.3 us
    all_to_all x1, starting transfers between devices, on_device(): lax.all_to_all(copies, ('z', 'xh'), split_axis=0, concat_axis=0, tiled=True)  10.4 us
    all_gather x1, blocking collectives, on_device(): scanned = lax.all_gather(scanned, ('xl', 'core'), axis=0)  9.7 us
    ppermute x1, waiting for transfers between devices, on_device(): arrived = lax.ppermute(leaving, ('yh', 'yl', 'core'), neighbour_routes(8))  9.64 us
    pallas_call x2, Pallas kernels, project(): pl.pallas_call(project_kernel, out_shape=jax.ShapeDtypeStruct((4, rows, c...  5.48 us
    ppermute x1, starting transfers between devices, on_device(): near = lax.ppermute(sent, ('xl', 'xh', 'core'), weight_routes())  5.22 us
    ppermute x1, starting transfers between devices, on_device(): arrived = lax.ppermute(leaving, ('yh', 'yl', 'core'), neighbour_routes(8))  5.07 us
    pallas_call x1, Pallas kernels, joined_weights(): pl.pallas_call(weights_kernel, out_shape=jax.ShapeDtypeStruct((2, 2 * cha...  4.76 us
  transfers between devices with their start and end apart: 5, of which 2 were waited for; matrix products, arithmetic and copies ran while one was open for 1% of the time, Pallas kernels for 13%

profile of v5, /device:TPU:1, one launch (start us, length us, event | category | flops | bytes accessed | tf_op | source)
XLA Modules:
  0.0 104.7 jit_solution(6338135262637862670)
XLA Ops:
  0.0 1.1 %dynamic-slice_convert_fusion = f32[128,2048]{1,0:T(8,128)S(1)} fusion(bf16[256,4096]{1,0:T(8,128)(2,1)} %own_ref.1, s32[]{:T(128)S(6)} %select_n.6, s32[]{:T(128)S(6)} %select_n.7), kind=kLoop, calls=%fused_computation | loop fusion | flops 262144 | bytes 1572872 | tf_op jit(solution)/shard_map/convert_element_type | solution.py:343
  1.1 5.2 %collective-permute-start.1 = (f32[128,2048]{1,0:T(8,128)S(1)}, f32[128,2048]{1,0:T(8,128)}, u32[]{:S(2)}, u32[]{:S(2)}) collective-permute-start(f32[128,2048]{1,0:T(8,128)S(1)} %dynamic-slice_convert_fusion), channel_id=1, source_target_pairs={{0,256},{1,259},{2,258},{3,257},{256,0},{257,3},{258,2},{259,1},{4... | collective-permute-start | bytes 3145736 | tf_op jit(solution)/shard_map/ppermute | solution.py:344
  6.4 2.2 %local_states.1 = (f32[4,16,256]{2,1,0:T(8,128)}, f32[16,16,256]{2,1,0:T(8,128)}) custom-call(bf16[256,256]{1,0:T(8,128)(2,1)} %key_ref.3, bf16[256,256]{1,0:T(8,128)(2,1)} %value_ref.3, f32[16,256]{1,0:T(8,128)} %decay_ref.5), custom_call_target="tpu_custom_call" | custom-call | tf_op jit(solution)/shard_map/local_states/pallas_call | solution.py:73
  8.5 10.4 %all-to-all-start = ((f32[16,16,256]{2,1,0:T(8,128)}), f32[16,16,256]{2,1,0:T(8,128)S(1)}, u32[]{:S(2)}, u32[]{:S(2)}) async-start(f32[16,16,256]{2,1,0:T(8,128)} %get-tuple-element.7.own_ref), calls=%async_computation | async-start | bytes 524288 | tf_op jit(solution)/shard_map/all_to_all | solution.py:350
  18.9 3.0 %local_conv.1.own_ref = f32[544,256]{1,0:T(8,128)} custom-call(f32[4,16,256]{2,1,0:T(8,128)} %get-tuple-element.8.blocks_ref, bf16[256,256]{1,0:T(8,128)(2,1)} %gate_ref.1, bf16[256,256]{1,0:T(8,128)(2,1)} %key_ref.3, bf16[256,256]{1,0:T(8,128)(2,1)} %value_ref.3, f32[16,256]{1,0:T(8,128)} %residues_ref.1, f32[16,256]{1,0:T(8,128)} %decay_ref.5), custom_call_target="tpu_custom_call" | custom-call | tf_op jit(solution)/shard_map/local_conv/pallas_call | solution.py:156
  21.9 2.2 %collective-permute-start = (f32[544,256]{1,0:T(8,128)}, f32[544,256]{1,0:T(8,128)}, u32[]{:S(2)}, u32[]{:S(2)}) collective-permute-start(f32[544,256]{1,0:T(8,128)} %local_conv.1.own_ref), channel_id=1, source_target_pairs={{0,256},{256,0},{1,257},{257,1},{2,258},{258,2},{3,259},{259,3},{4... | collective-permute-start | bytes 1671176 | tf_op jit(solution)/shard_map/ppermute | solution.py:354
  24.1 0.7 pad_add_fusion.place_ref
  24.8 0.0 collective-permute-done.1.near_ref
  24.8 3.8 %collective-permute-start.2 = (f32[128,2048]{1,0:T(8,128)}, f32[128,2048]{1,0:T(8,128)}, u32[]{:S(2)}, u32[]{:S(2)}) collective-permute-start(f32[128,2048]{1,0:T(8,128)} %collective-permute-done.1.near_ref), channel_id=1, source_target_pairs={{0,1},{1,0},{2,3},{3,2},{4,5},{5,4},{6,7},{7,6},{8,9},{9,8},{10,11... | collective-permute-start | bytes 3145736 | tf_op jit(solution)/shard_map/ppermute | solution.py:345
  28.5 1.6 %all-to-all-done.chips_ref = f32[16,16,256]{2,1,0:T(8,128)S(1)} async-done(((f32[16,16,256]{2,1,0:T(8,128)}), f32[16,16,256]{2,1,0:T(8,128)S(1)}, u32[]{:S(2)}, u32[]{:S(2)}) %all-to-all-start) | async-done | bytes 262176 | tf_op jit(solution)/shard_map/all_to_all | solution.py:350
  30.2 2.1 %chip_scan.1 = f32[2,16,256]{2,1,0:T(8,128)} custom-call(s32[4]{0:T(128)} %pad_add_fusion.place_ref, f32[16,16,256]{2,1,0:T(8,128)S(1)} %all-to-all-done.chips_ref, f32[16,16,256]{2,1,0:T(8,128)} %get-tuple-element.7.own_ref, f32[16,256]{1,0:T(8,128)} %decay_ref.5), custom_call_target="tpu_custom_call" | custom-call | flops 199999995904 | bytes 200000000 | tf_op jit(solution)/shard_map/chip_scan/pallas_call | solution.py:177
  32.2 9.7 %all-gather = f32[8,16,256]{2,1,0:T(8,128)} all-gather(f32[2,16,256]{2,1,0:T(8,128)} %chip_scan.1), channel_id=2, replica_groups=mesh['xl'=2,'yh'=4,'yl'=2,'z'=8,'xh'=2,'core'=2] {'xl','core'}, dimensions={0}, use_global_device_ids=true | all-gather | bytes 163840 | tf_op jit(solution)/shard_map/all_gather | solution.py:356
  41.9 0.0 collective-permute-done.peer_ref
  41.9 3.3 %gated_both.1.gated_ref = bf16[256,512]{1,0:T(8,128)(2,1)} custom-call(s32[4]{0:T(128)} %pad_add_fusion.place_ref, f32[4,2,16,256]{3,2,1,0:T(8,128)} %bitcast.5, f32[544,256]{1,0:T(8,128)} %local_conv.1.own_ref, f32[544,256]{1,0:T(8,128)} %collective-permute-done.peer_ref), custom_call_target="tpu_custom_call" | custom-call | tf_op jit(solution)/shard_map/gated_both/pallas_call | solution.py:239
  45.3 0.0 collective-permute-done.2.far_ref
  45.3 4.8 %joined_weights.1.weight_ref = bf16[2,512,1024]{2,1,0:T(8,128)(2,1)} custom-call(s32[4]{0:T(128)} %pad_add_fusion.place_ref, bf16[256,4096]{1,0:T(8,128)(2,1)} %own_ref.1, f32[128,2048]{1,0:T(8,128)} %collective-permute-done.1.near_ref, f32[128,2048]{1,0:T(8,128)} %collective-permute-done.2.far_ref), custom_call_target="tpu_custom_call" | custom-call | tf_op jit(solution)/shard_map/joined_weights/pallas_call | solution.py:271
  50.0 2.7 %project_leaving.1 = f32[4,256,256]{2,1,0:T(8,128)} custom-call(bf16[256,512]{1,0:T(8,128)(2,1)} %gated_both.1.gated_ref, bf16[2,512,1024]{2,1,0:T(8,128)(2,1)} %joined_weights.1.weight_ref), custom_call_target="tpu_custom_call" | custom-call | tf_op jit(solution)/shard_map/project_leaving/pallas_call | solution.py:301
  52.8 5.1 %collective-permute-start.3 = (f32[4,256,256]{2,1,0:T(8,128)}, f32[4,256,256]{2,1,0:T(8,128)S(1)}, u32[]{:S(2)}, u32[]{:S(2)}) collective-permute-start(f32[4,256,256]{2,1,0:T(8,128)} %project_leaving.1), channel_id=1, source_target_pairs={{0,32},{1,225},{32,0},{33,65},{64,96},{65,33},{96,64},{97,129},{12... | collective-permute-start | bytes 3145736 | tf_op jit(solution)/shard_map/ppermute | solution.py:359
  57.8 2.7 %project_kept.1 = f32[4,256,256]{2,1,0:T(8,128)} custom-call(bf16[256,512]{1,0:T(8,128)(2,1)} %gated_both.1.gated_ref, bf16[2,512,1024]{2,1,0:T(8,128)(2,1)} %joined_weights.1.weight_ref), custom_call_target="tpu_custom_call" | custom-call | tf_op jit(solution)/shard_map/project_kept/pallas_call | solution.py:301
  60.6 9.6 %collective-permute-done.3 = f32[4,256,256]{2,1,0:T(8,128)S(1)} collective-permute-done((f32[4,256,256]{2,1,0:T(8,128)}, f32[4,256,256]{2,1,0:T(8,128)S(1)}, u32[]{:S(2)}, u32[]{:S(2)}) %collective-permute-start.3) | collective-permute-done | bytes 1048608 | tf_op jit(solution)/shard_map/ppermute | solution.py:359
  70.2 1.4 %add.15 = f32[4,256,256]{2,1,0:T(8,128)S(1)} add(f32[4,256,256]{2,1,0:T(8,128)} %project_kept.1, f32[4,256,256]{2,1,0:T(8,128)S(1)} %collective-permute-done.3) | non-fusion elementwise | flops 262144 | bytes 3145728 | tf_op jit(solution)/shard_map/add | solution.py:361
  71.6 32.3 %all_to_all.10 = f32[4,256,256]{2,1,0:T(8,128)S(1)} all-to-all(f32[4,256,256]{2,1,0:T(8,128)S(1)} %add.15), channel_id=1, replica_groups=mesh['xl'=2,'yh'=4,'yl'=2,'z'=8,'xh'=2,'core'=2] {'yh'}, dimensions={0} | all-to-all | bytes 2097152 | tf_op jit(solution)/shard_map/all_to_all | solution.py:361
  103.9 0.7 reduce_sum.9
Async XLA Ops:
  1.1 23.6 %collective-permute-start.1 = (f32[128,2048]{1,0:T(8,128)S(1)}, f32[128,2048]{1,0:T(8,128)}, u32[]{:S(2)}, u32[]{:S(2)}) collective-permute-start(f32[128,2048]{1,0:T(8,128)S(1)} %dynamic-slice_convert_fusion), channel_id=1, source_target_pairs={{0,256},{1,259},{2,258},{3,257},{256,0},{257,3},{258,2},{259,1},{4... | collective-permute-start | bytes 3145736 | tf_op jit(solution)/shard_map/ppermute | solution.py:344
  8.5 21.6 %all-to-all-start = ((f32[16,16,256]{2,1,0:T(8,128)}), f32[16,16,256]{2,1,0:T(8,128)S(1)}, u32[]{:S(2)}, u32[]{:S(2)}) async-start(f32[16,16,256]{2,1,0:T(8,128)} %get-tuple-element.7.own_ref), calls=%async_computation | async-start | bytes 524288 | tf_op jit(solution)/shard_map/all_to_all | solution.py:350
  21.9 20.0 %collective-permute-start = (f32[544,256]{1,0:T(8,128)}, f32[544,256]{1,0:T(8,128)}, u32[]{:S(2)}, u32[]{:S(2)}) collective-permute-start(f32[544,256]{1,0:T(8,128)} %local_conv.1.own_ref), channel_id=1, source_target_pairs={{0,256},{256,0},{1,257},{257,1},{2,258},{258,2},{3,259},{259,3},{4... | collective-permute-start | bytes 1671176 | tf_op jit(solution)/shard_map/ppermute | solution.py:354
  24.8 20.5 %collective-permute-start.2 = (f32[128,2048]{1,0:T(8,128)}, f32[128,2048]{1,0:T(8,128)}, u32[]{:S(2)}, u32[]{:S(2)}) collective-permute-start(f32[128,2048]{1,0:T(8,128)} %collective-permute-done.1.near_ref), channel_id=1, source_target_pairs={{0,1},{1,0},{2,3},{3,2},{4,5},{5,4},{6,7},{7,6},{8,9},{9,8},{10,11... | collective-permute-start | bytes 3145736 | tf_op jit(solution)/shard_map/ppermute | solution.py:345
  52.8 17.5 %collective-permute-start.3 = (f32[4,256,256]{2,1,0:T(8,128)}, f32[4,256,256]{2,1,0:T(8,128)S(1)}, u32[]{:S(2)}, u32[]{:S(2)}) collective-permute-start(f32[4,256,256]{2,1,0:T(8,128)} %project_leaving.1), channel_id=1, source_target_pairs={{0,32},{1,225},{32,0},{33,65},{64,96},{65,33},{96,64},{97,129},{12... | collective-permute-start | bytes 3145736 | tf_op jit(solution)/shard_map/ppermute | solution.py:359

commit v6 on v5

--- a/solution.py
+++ b/solution.py
@@ -235,7 +235,7 @@
 
 def gated_both(place, states, own, peer, rows):
     chans = own.shape[1]
-    args = (states, own, peer)
+    args = (near_core(states), near_core(own), near_core(peer))
     return pl.pallas_call(
         gate_kernel,
         out_shape=jax.ShapeDtypeStruct((rows, 2 * chans), jnp.bfloat16),
@@ -249,66 +249,51 @@
     )(place, *args)
 
 
-def weights_kernel(place_ref, own_ref, near_ref, far_ref, out_ref):
-    half = near_ref.shape[0]
+def project_kernel(place_ref, gated_ref, *refs):
+    *weights, out_ref = refs
+    half = weights[1].shape[0]
     chans = 2 * half
     core = place_ref[1]
-    parity = place_ref[3]
     here = pl.ds(pl.multiple_of(chans + core * half, half), half)
     there = pl.ds(pl.multiple_of(chans + (1 - core) * half, half), half)
-    for kept in range(2):
-        side = parity if kept else 1 - parity
-        source = pl.ds(pl.multiple_of(side * chans, chans), chans)
-        out_ref[kept, :chans, :] = own_ref[:, source]
-        out_ref[kept, here, :] = near_ref[:, source].astype(jnp.bfloat16)
-        out_ref[kept, there, :] = far_ref[:, source].astype(jnp.bfloat16)
-
-
-def joined_weights(place, weight, near, far):
-    chans = weight.shape[0]
-    half, cols = near.shape
-    wide = pl.BlockSpec((half, 2 * chans), lambda i, p: (0, i))
-    return pl.pallas_call(
-        weights_kernel,
-        out_shape=jax.ShapeDtypeStruct((2, 2 * chans, cols // 2), jnp.bfloat16),
+
+    def product(lhs, rhs):
+        return jnp.dot(
+            lhs, rhs.astype(jnp.bfloat16), preferred_element_type=jnp.float32
+        )
+
+    for h in range(4):
+        own_ref, near_ref, far_ref = weights[3 * h : 3 * h + 3]
+        out_ref[h] = (
+            product(gated_ref[:, :chans], own_ref[...])
+            + product(gated_ref[:, here], near_ref[...])
+            + product(gated_ref[:, there], far_ref[...])
+        )
+
+
+def project(place, gated, weight, near, far, part, name):
+    rows, deep = gated.shape
+    chans = deep // 2
+
+    def columns(h):
+        def at(p):
+            return 2 * h + (p[3] if part else 1 - p[3])
+
+        other = pl.BlockSpec((chans // 2, chans), lambda i, p: (0, at(p)))
+        own = pl.BlockSpec((chans, chans), lambda i, p: (0, 8 * p[2] + at(p)))
+        return [own, other, other]
+
+    return pl.pallas_call(
+        project_kernel,
+        out_shape=jax.ShapeDtypeStruct((4, rows, chans), jnp.float32),
         grid_spec=pltpu.PrefetchScalarGridSpec(
             num_scalar_prefetch=1,
-            grid=(4,),
-            in_specs=[
-                pl.BlockSpec((chans, 2 * chans), lambda i, p: (0, 4 * p[2] + i)),
-                wide,
-                wide,
-            ],
-            out_specs=pl.BlockSpec((2, 2 * chans, chans), lambda i, p: (0, 0, i)),
-        ),
-        name="joined_weights",
-    )(place, weight, near, far)
-
-
-def project_kernel(gated_ref, weight_ref, out_ref):
-    chans = out_ref.shape[2]
-    for h in range(4):
-        out_ref[h] = jnp.dot(
-            gated_ref[...],
-            weight_ref[:, h * chans : (h + 1) * chans],
-            preferred_element_type=jnp.float32,
-        )
-
-
-def project(gated, weight, part, name):
-    rows, deep = gated.shape
-    cols = weight.shape[2]
-    return pl.pallas_call(
-        project_kernel,
-        out_shape=jax.ShapeDtypeStruct((4, rows, cols // 4), jnp.float32),
-        grid=(1,),
-        in_specs=[
-            whole((rows, deep)),
-            pl.BlockSpec((None, deep, cols), lambda i: (part, 0, 0)),
-        ],
-        out_specs=whole((4, rows, cols // 4)),
+            grid=(1,),
+            in_specs=[whole((rows, deep))] + sum([columns(h) for h in range(4)], []),
+            out_specs=whole((4, rows, chans)),
+        ),
         name=name,
-    )(gated, weight)
+    )(place, gated, *[weight, near, far] * 4)
 
 
 def neighbour_routes(count):
@@ -343,7 +328,6 @@
     ).astype(jnp.float32)
     near = lax.ppermute(sent, ("xl", "xh", "core"), weight_routes())
     far = lax.ppermute(near, "core", swap)
-    weight = joined_weights(place, out_weight, near, far)
 
     chips = lax.axis_size("z") * lax.axis_size("xh")
     blocks, copies = local_states(key_stream, value_stream, decay_rates, chips)
@@ -355,9 +339,9 @@
     scanned = chip_scan(place, states, copies, decay_rates, rows)
     scanned = lax.all_gather(scanned, ("xl", "core"), axis=0)
     gated = gated_both(place, scanned, own, peer, rows)
-    leaving = project(gated, weight, 0, "project_leaving")
+    leaving = project(place, gated, out_weight, near, far, 0, "project_leaving")
     arrived = lax.ppermute(leaving, ("yh", "yl", "core"), neighbour_routes(8))
-    kept = project(gated, weight, 1, "project_kept")
+    kept = project(place, gated, out_weight, near, far, 1, "project_kept")
     parts = lax.all_to_all(kept + arrived, "yh", split_axis=0, concat_axis=0, tiled=True)
     return jnp.sum(parts, axis=0).astype(jnp.bfloat16)
 

time: 106 us -> 101 us (0.953)
  Pallas kernels: 20.8 us -> 18 us
    pallas_call x1 -> x0, Pallas kernels: 4.76 us -> none  [joined_weights(): pl.pallas_call(weights_kernel, out_shape=jax.ShapeDtypeStruct((2, 2 * cha...]
    pallas_call x2, Pallas kernels: 5.48 us -> 7.5 us  [project(): pl.pallas_call(project_kernel, out_shape=jax.ShapeDtypeStruct((4, rows, c...]
  transfers between devices with their start and end apart: 5 -> 5, of which waited for: 2 -> 2; matrix products, arithmetic and copies ran while one was open for 1% -> 1% of each run, Pallas kernels for 13% -> 14%
where the time goes in v6:
time: 101 us; the launch traced here: 100 us
  blocking collectives  41.5 us (41%)
  starting transfers between devices  26.6 us (26%)
  Pallas kernels  18 us (18%)
  waiting for transfers between devices  10.3 us (10%)
  other arithmetic  3.88 us (4%)
    all_to_all x1, blocking collectives, on_device(): lax.all_to_all(kept + arrived, 'yh', split_axis=0, concat_axis=0, tiled=T...  32.3 us
    all_to_all x1, starting transfers between devices, on_device(): lax.all_to_all(copies, ('z', 'xh'), split_axis=0, concat_axis=0, tiled=True)  10.4 us
    all_gather x1, blocking collectives, on_device(): scanned = lax.all_gather(scanned, ('xl', 'core'), axis=0)  9.13 us
    ppermute x1, waiting for transfers between devices, on_device(): arrived = lax.ppermute(leaving, ('yh', 'yl', 'core'), neighbour_routes(8))  8.62 us
    pallas_call x2, Pallas kernels, project(): pl.pallas_call(project_kernel, out_shape=jax.ShapeDtypeStruct((4, rows, c...  7.5 us
    ppermute x1, starting transfers between devices, on_device(): near = lax.ppermute(sent, ('xl', 'xh', 'core'), weight_routes())  5.22 us
    ppermute x1, starting transfers between devices, on_device(): arrived = lax.ppermute(leaving, ('yh', 'yl', 'core'), neighbour_routes(8))  5.09 us
    ppermute x1, starting transfers between devices, on_device(): far = lax.ppermute(near, 'core', swap)  3.76 us
  transfers between devices with their start and end apart: 5, of which 2 were waited for; matrix products, arithmetic and copies ran while one was open for 1% of the time, Pallas kernels for 14%

profile of v6, /device:TPU:1, one launch (start us, length us, event | category | flops | bytes accessed | tf_op | source)
XLA Modules:
  0.0 100.3 jit_solution(2197272084424042585)
XLA Ops:
  0.0 1.1 %dynamic-slice_convert_fusion = f32[128,2048]{1,0:T(8,128)S(1)} fusion(bf16[256,4096]{1,0:T(8,128)(2,1)} %refs_9_.3, s32[]{:T(128)S(6)} %select_n.6, s32[]{:T(128)S(6)} %select_n.7), kind=kLoop, calls=%fused_computation | loop fusion | flops 262144 | bytes 1572872 | tf_op jit(solution)/shard_map/convert_element_type | solution.py:328
  1.1 5.2 %collective-permute-start.1 = (f32[128,2048]{1,0:T(8,128)S(1)}, f32[128,2048]{1,0:T(8,128)}, u32[]{:S(2)}, u32[]{:S(2)}) collective-permute-start(f32[128,2048]{1,0:T(8,128)S(1)} %dynamic-slice_convert_fusion), channel_id=1, source_target_pairs={{0,256},{1,259},{2,258},{3,257},{256,0},{257,3},{258,2},{259,1},{4... | collective-permute-start | bytes 3145736 | tf_op jit(solution)/shard_map/ppermute | solution.py:329
  6.4 2.2 %local_states.1 = (f32[4,16,256]{2,1,0:T(8,128)}, f32[16,16,256]{2,1,0:T(8,128)}) custom-call(bf16[256,256]{1,0:T(8,128)(2,1)} %key_ref.3, bf16[256,256]{1,0:T(8,128)(2,1)} %value_ref.3, f32[16,256]{1,0:T(8,128)} %decay_ref.5), custom_call_target="tpu_custom_call" | custom-call | tf_op jit(solution)/shard_map/local_states/pallas_call | solution.py:73
  8.5 10.4 %all-to-all-start = ((f32[16,16,256]{2,1,0:T(8,128)}), f32[16,16,256]{2,1,0:T(8,128)S(1)}, u32[]{:S(2)}, u32[]{:S(2)}) async-start(f32[16,16,256]{2,1,0:T(8,128)} %get-tuple-element.7.own_ref), calls=%async_computation | async-start | bytes 524288 | tf_op jit(solution)/shard_map/all_to_all | solution.py:334
  18.9 3.0 %local_conv.1.own_ref = f32[544,256]{1,0:T(8,128)} custom-call(f32[4,16,256]{2,1,0:T(8,128)} %get-tuple-element.8.blocks_ref, bf16[256,256]{1,0:T(8,128)(2,1)} %gate_ref.1, bf16[256,256]{1,0:T(8,128)(2,1)} %key_ref.3, bf16[256,256]{1,0:T(8,128)(2,1)} %value_ref.3, f32[16,256]{1,0:T(8,128)} %residues_ref.1, f32[16,256]{1,0:T(8,128)} %decay_ref.5), custom_call_target="tpu_custom_call" | custom-call | tf_op jit(solution)/shard_map/local_conv/pallas_call | solution.py:156
  21.9 2.2 %collective-permute-start = (f32[544,256]{1,0:T(8,128)}, f32[544,256]{1,0:T(8,128)}, u32[]{:S(2)}, u32[]{:S(2)}) collective-permute-start(f32[544,256]{1,0:T(8,128)} %local_conv.1.own_ref), channel_id=1, source_target_pairs={{0,256},{256,0},{1,257},{257,1},{2,258},{258,2},{3,259},{259,3},{4... | collective-permute-start | bytes 1671176 | tf_op jit(solution)/shard_map/ppermute | solution.py:338
  24.1 0.7 pad_add_fusion.place_ref
  24.8 0.0 collective-permute-done.1.refs_1_.refs_4_.refs_7_.refs_10_
  24.8 3.8 %collective-permute-start.2 = (f32[128,2048]{1,0:T(8,128)}, f32[128,2048]{1,0:T(8,128)}, u32[]{:S(2)}, u32[]{:S(2)}) collective-permute-start(f32[128,2048]{1,0:T(8,128)} %collective-permute-done.1.refs_1_.refs_4_.refs_7_.refs_10_), channel_id=1, source_target_pairs={{0,1},{1,0},{2,3},{3,2},{4,5},{5,4},{6,7},{7,6},{8,9},{9,8},{10,11... | collective-permute-start | bytes 3145736 | tf_op jit(solution)/shard_map/ppermute | solution.py:330
  28.5 1.6 %all-to-all-done.chips_ref = f32[16,16,256]{2,1,0:T(8,128)S(1)} async-done(((f32[16,16,256]{2,1,0:T(8,128)}), f32[16,16,256]{2,1,0:T(8,128)S(1)}, u32[]{:S(2)}, u32[]{:S(2)}) %all-to-all-start) | async-done | bytes 262176 | tf_op jit(solution)/shard_map/all_to_all | solution.py:334
  30.2 0.0 copy-start
  30.2 2.2 %chip_scan.1 = f32[2,16,256]{2,1,0:T(8,128)} custom-call(s32[4]{0:T(128)} %pad_add_fusion.place_ref, f32[16,16,256]{2,1,0:T(8,128)S(1)} %all-to-all-done.chips_ref, f32[16,16,256]{2,1,0:T(8,128)} %get-tuple-element.7.own_ref, f32[16,256]{1,0:T(8,128)} %decay_ref.5), custom_call_target="tpu_custom_call" | custom-call | flops 199999995904 | bytes 200000000 | tf_op jit(solution)/shard_map/chip_scan/pallas_call | solution.py:177
  32.4 9.1 %all-gather = f32[8,16,256]{2,1,0:T(8,128)S(1)} all-gather(f32[2,16,256]{2,1,0:T(8,128)} %chip_scan.1), channel_id=2, replica_groups=mesh['xl'=2,'yh'=4,'yl'=2,'z'=8,'xh'=2,'core'=2] {'xl','core'}, dimensions={0}, use_global_device_ids=true | all-gather | bytes 163840 | tf_op jit(solution)/shard_map/all_gather | solution.py:340
  41.5 0.0 collective-permute-done.peer_ref
  41.5 0.0 copy-done
  41.5 3.1 %gated_both.1.gated_ref = bf16[256,512]{1,0:T(8,128)(2,1)} custom-call(s32[4]{0:T(128)} %pad_add_fusion.place_ref, f32[4,2,16,256]{3,2,1,0:T(8,128)S(1)} %bitcast.5, f32[544,256]{1,0:T(8,128)S(1)} %copy-done, f32[544,256]{1,0:T(8,128)} %collective-permute-done.peer_ref), custom_call_target="tpu_custom_call" | custom-call | tf_op jit(solution)/shard_map/gated_both/pallas_call | solution.py:239
  44.6 0.0 collective-permute-done.2.refs_2_.refs_5_.refs_8_.refs_11_
  44.6 3.7 %project_leaving.1 = f32[4,256,256]{2,1,0:T(8,128)} custom-call(s32[4]{0:T(128)} %pad_add_fusion.place_ref, bf16[256,512]{1,0:T(8,128)(2,1)} %gated_both.1.gated_ref, bf16[256,4096]{1,0:T(8,128)(2,1)} %refs_9_.3, f32[128,2048]{1,0:T(8,128)} %collective-permute-done.1.refs_1_.refs_4_.refs_7_.refs_10_, ...), custom_call_target="tpu_custom_call" | custom-call | tf_op jit(solution)/shard_map/project_leaving/pallas_call | solution.py:286
  48.3 5.1 %collective-permute-start.3 = (f32[4,256,256]{2,1,0:T(8,128)}, f32[4,256,256]{2,1,0:T(8,128)S(1)}, u32[]{:S(2)}, u32[]{:S(2)}) collective-permute-start(f32[4,256,256]{2,1,0:T(8,128)} %project_leaving.1), channel_id=1, source_target_pairs={{0,32},{1,225},{32,0},{33,65},{64,96},{65,33},{96,64},{97,129},{12... | collective-permute-start | bytes 3145736 | tf_op jit(solution)/shard_map/ppermute | solution.py:343
  53.4 3.8 %project_kept.1 = f32[4,256,256]{2,1,0:T(8,128)} custom-call(s32[4]{0:T(128)} %pad_add_fusion.place_ref, bf16[256,512]{1,0:T(8,128)(2,1)} %gated_both.1.gated_ref, bf16[256,4096]{1,0:T(8,128)(2,1)} %refs_9_.3, f32[128,2048]{1,0:T(8,128)} %collective-permute-done.1.refs_1_.refs_4_.refs_7_.refs_10_, ...), custom_call_target="tpu_custom_call" | custom-call | tf_op jit(solution)/shard_map/project_kept/pallas_call | solution.py:286
  57.2 8.6 %collective-permute-done.3 = f32[4,256,256]{2,1,0:T(8,128)S(1)} collective-permute-done((f32[4,256,256]{2,1,0:T(8,128)}, f32[4,256,256]{2,1,0:T(8,128)S(1)}, u32[]{:S(2)}, u32[]{:S(2)}) %collective-permute-start.3) | collective-permute-done | bytes 1048608 | tf_op jit(solution)/shard_map/ppermute | solution.py:343
  65.8 1.4 %add.15 = f32[4,256,256]{2,1,0:T(8,128)S(1)} add(f32[4,256,256]{2,1,0:T(8,128)} %project_kept.1, f32[4,256,256]{2,1,0:T(8,128)S(1)} %collective-permute-done.3) | non-fusion elementwise | flops 262144 | bytes 3145728 | tf_op jit(solution)/shard_map/add | solution.py:345
  67.2 32.3 %all_to_all.10 = f32[4,256,256]{2,1,0:T(8,128)S(1)} all-to-all(f32[4,256,256]{2,1,0:T(8,128)S(1)} %add.15), channel_id=1, replica_groups=mesh['xl'=2,'yh'=4,'yl'=2,'z'=8,'xh'=2,'core'=2] {'yh'}, dimensions={0} | all-to-all | bytes 2097152 | tf_op jit(solution)/shard_map/all_to_all | solution.py:345
  99.5 0.7 reduce_sum.9
Async XLA Ops:
  1.1 23.6 %collective-permute-start.1 = (f32[128,2048]{1,0:T(8,128)S(1)}, f32[128,2048]{1,0:T(8,128)}, u32[]{:S(2)}, u32[]{:S(2)}) collective-permute-start(f32[128,2048]{1,0:T(8,128)S(1)} %dynamic-slice_convert_fusion), channel_id=1, source_target_pairs={{0,256},{1,259},{2,258},{3,257},{256,0},{257,3},{258,2},{259,1},{4... | collective-permute-start | bytes 3145736 | tf_op jit(solution)/shard_map/ppermute | solution.py:329
  8.5 21.6 %all-to-all-start = ((f32[16,16,256]{2,1,0:T(8,128)}), f32[16,16,256]{2,1,0:T(8,128)S(1)}, u32[]{:S(2)}, u32[]{:S(2)}) async-start(f32[16,16,256]{2,1,0:T(8,128)} %get-tuple-element.7.own_ref), calls=%async_computation | async-start | bytes 524288 | tf_op jit(solution)/shard_map/all_to_all | solution.py:334
  21.9 19.6 %collective-permute-start = (f32[544,256]{1,0:T(8,128)}, f32[544,256]{1,0:T(8,128)}, u32[]{:S(2)}, u32[]{:S(2)}) collective-permute-start(f32[544,256]{1,0:T(8,128)} %local_conv.1.own_ref), channel_id=1, source_target_pairs={{0,256},{256,0},{1,257},{257,1},{2,258},{258,2},{3,259},{259,3},{4... | collective-permute-start | bytes 1671176 | tf_op jit(solution)/shard_map/ppermute | solution.py:338
  24.8 19.8 %collective-permute-start.2 = (f32[128,2048]{1,0:T(8,128)}, f32[128,2048]{1,0:T(8,128)}, u32[]{:S(2)}, u32[]{:S(2)}) collective-permute-start(f32[128,2048]{1,0:T(8,128)} %collective-permute-done.1.refs_1_.refs_4_.refs_7_.refs_10_), channel_id=1, source_target_pairs={{0,1},{1,0},{2,3},{3,2},{4,5},{5,4},{6,7},{7,6},{8,9},{9,8},{10,11... | collective-permute-start | bytes 3145736 | tf_op jit(solution)/shard_map/ppermute | solution.py:330
  30.2 11.3 %copy-start = (f32[544,256]{1,0:T(8,128)S(1)}, f32[544,256]{1,0:T(8,128)}, u32[]{:S(2)}) copy-start(f32[544,256]{1,0:T(8,128)} %local_conv.1.own_ref) | copy-start | bytes 1671172
  48.3 17.5 %collective-permute-start.3 = (f32[4,256,256]{2,1,0:T(8,128)}, f32[4,256,256]{2,1,0:T(8,128)S(1)}, u32[]{:S(2)}, u32[]{:S(2)}) collective-permute-start(f32[4,256,256]{2,1,0:T(8,128)} %project_leaving.1), channel_id=1, source_target_pairs={{0,32},{1,225},{32,0},{33,65},{64,96},{65,33},{96,64},{97,129},{12... | collective-permute-start | bytes 3145736 | tf_op jit(solution)/shard_map/ppermute | solution.py:343

commit v7 on v6

--- a/solution.py
+++ b/solution.py
@@ -285,7 +285,9 @@
 
     return pl.pallas_call(
         project_kernel,
-        out_shape=jax.ShapeDtypeStruct((4, rows, chans), jnp.float32),
+        out_shape=pltpu.VMEM(
+            (4, rows, chans), jnp.float32
+        ),
         grid_spec=pltpu.PrefetchScalarGridSpec(
             num_scalar_prefetch=1,
             grid=(1,),
@@ -342,8 +344,13 @@
     leaving = project(place, gated, out_weight, near, far, 0, "project_leaving")
     arrived = lax.ppermute(leaving, ("yh", "yl", "core"), neighbour_routes(8))
     kept = project(place, gated, out_weight, near, far, 1, "project_kept")
-    parts = lax.all_to_all(kept + arrived, "yh", split_axis=0, concat_axis=0, tiled=True)
-    return jnp.sum(parts, axis=0).astype(jnp.bfloat16)
+    total = kept + arrived
+    here = lax.axis_index("yh")
+    result = lax.dynamic_index_in_dim(total, here, 0, keepdims=False)
+    for d in (1, 3, 2):
+        block = lax.dynamic_index_in_dim(total, (here + d) & 3, 0, keepdims=False)
+        result += lax.ppermute(block, "yh", [(h, (h + d) % 4) for h in range(4)])
+    return result.astype(jnp.bfloat16)
 
 
 def solution(mesh):

time: 101 us -> 96.8 us (0.958)
  blocking collectives: 41.5 us -> 9.14 us
  waiting for transfers between devices: 10.3 us -> 28.4 us
  starting transfers between devices: 26.6 us -> 39.7 us
  Pallas kernels: 18 us -> 16 us
  other arithmetic: 3.88 us -> 2.57 us
    all_to_all x1 -> x0, blocking collectives: 32.3 us -> none  [on_device(): lax.all_to_all(kept + arrived, 'yh', split_axis=0, concat_axis=0, tiled=T...]
    ppermute x0 -> x3, waiting for transfers between devices: none -> 17.4 us  [on_device(): result += lax.ppermute(block, 'yh', [(h, (h + d) % 4) for h in range(4)])]
    ppermute x0 -> x3, starting transfers between devices: none -> 13.1 us  [on_device(): result += lax.ppermute(block, 'yh', [(h, (h + d) % 4) for h in range(4)])]
    pallas_call x2, Pallas kernels: 7.5 us -> 5.53 us  [project(): pl.pallas_call(project_kernel, out_shape=pltpu.VMEM((4, rows, chans), jnp...]
    add x1, other arithmetic: 1.36 us -> 0.14 us  [on_device(): total = kept + arrived]
  transfers between devices with their start and end apart: 5 -> 8, of which waited for: 2 -> 4; matrix products, arithmetic and copies ran while one was open for 1% -> 1% of each run, Pallas kernels for 14% -> 14%
where the time goes in v7:
time: 96.8 us; the launch traced here: 96.1 us
  starting transfers between devices  39.7 us (41%)
  waiting for transfers between devices  28.4 us (29%)
  Pallas kernels  16 us (17%)
  blocking collectives  9.14 us (9%)
  other arithmetic  2.57 us (3%)
    ppermute x3, waiting for transfers between devices, on_device(): result += lax.ppermute(block, 'yh', [(h, (h + d) % 4) for h in range(4)])  17.4 us
    ppermute x3, starting transfers between devices, on_device(): result += lax.ppermute(block, 'yh', [(h, (h + d) % 4) for h in range(4)])  13.1 us
    all_to_all x1, starting transfers between devices, on_device(): lax.all_to_all(copies, ('z', 'xh'), split_axis=0, concat_axis=0, tiled=True)  10.4 us
    ppermute x1, waiting for transfers between devices, on_device(): arrived = lax.ppermute(leaving, ('yh', 'yl', 'core'), neighbour_routes(8))  9.39 us
    all_gather x1, blocking collectives, on_device(): scanned = lax.all_gather(scanned, ('xl', 'core'), axis=0)  9.14 us
    pallas_call x2, Pallas kernels, project(): pl.pallas_call(project_kernel, out_shape=pltpu.VMEM((4, rows, chans), jnp...  5.53 us
    ppermute x1, starting transfers between devices, on_device(): near = lax.ppermute(sent, ('xl', 'xh', 'core'), weight_routes())  5.22 us
    ppermute x1, starting transfers between devices, on_device(): arrived = lax.ppermute(leaving, ('yh', 'yl', 'core'), neighbour_routes(8))  5.1 us
  transfers between devices with their start and end apart: 8, of which 4 were waited for; matrix products, arithmetic and copies ran while one was open for 1% of the time, Pallas kernels for 14%

profile of v7, /device:TPU:1, one launch (start us, length us, event | category | flops | bytes accessed | tf_op | source)
XLA Modules:
  0.0 96.1 jit_solution(1146306127493233697)
XLA Ops:
  0.0 1.1 %dynamic-slice_convert_fusion = f32[128,2048]{1,0:T(8,128)S(1)} fusion(bf16[256,4096]{1,0:T(8,128)(2,1)} %refs_9_.3, s32[]{:T(128)S(6)} %select_n.19, s32[]{:T(128)S(6)} %select_n.20), kind=kLoop, calls=%fused_computation | loop fusion | flops 262144 | bytes 1572872 | tf_op jit(solution)/shard_map/convert_element_type | solution.py:330
  1.1 5.2 %collective-permute-start.1 = (f32[128,2048]{1,0:T(8,128)S(1)}, f32[128,2048]{1,0:T(8,128)}, u32[]{:S(2)}, u32[]{:S(2)}) collective-permute-start(f32[128,2048]{1,0:T(8,128)S(1)} %dynamic-slice_convert_fusion), channel_id=1, source_target_pairs={{0,256},{1,259},{2,258},{3,257},{256,0},{257,3},{258,2},{259,1},{4... | collective-permute-start | bytes 3145736 | tf_op jit(solution)/shard_map/ppermute | solution.py:331
  6.4 2.2 %local_states.1 = (f32[4,16,256]{2,1,0:T(8,128)}, f32[16,16,256]{2,1,0:T(8,128)}) custom-call(bf16[256,256]{1,0:T(8,128)(2,1)} %key_ref.3, bf16[256,256]{1,0:T(8,128)(2,1)} %value_ref.3, f32[16,256]{1,0:T(8,128)} %decay_ref.5), custom_call_target="tpu_custom_call" | custom-call | tf_op jit(solution)/shard_map/local_states/pallas_call | solution.py:73
  8.5 10.4 %all-to-all-start = ((f32[16,16,256]{2,1,0:T(8,128)}), f32[16,16,256]{2,1,0:T(8,128)S(1)}, u32[]{:S(2)}, u32[]{:S(2)}) async-start(f32[16,16,256]{2,1,0:T(8,128)} %get-tuple-element.7.own_ref), calls=%async_computation | async-start | bytes 524288 | tf_op jit(solution)/shard_map/all_to_all | solution.py:336
  18.9 3.0 %local_conv.1.own_ref = f32[544,256]{1,0:T(8,128)} custom-call(f32[4,16,256]{2,1,0:T(8,128)} %get-tuple-element.8.blocks_ref, bf16[256,256]{1,0:T(8,128)(2,1)} %gate_ref.1, bf16[256,256]{1,0:T(8,128)(2,1)} %key_ref.3, bf16[256,256]{1,0:T(8,128)(2,1)} %value_ref.3, f32[16,256]{1,0:T(8,128)} %residues_ref.1, f32[16,256]{1,0:T(8,128)} %decay_ref.5), custom_call_target="tpu_custom_call" | custom-call | tf_op jit(solution)/shard_map/local_conv/pallas_call | solution.py:156
  22.0 2.2 %collective-permute-start = (f32[544,256]{1,0:T(8,128)}, f32[544,256]{1,0:T(8,128)}, u32[]{:S(2)}, u32[]{:S(2)}) collective-permute-start(f32[544,256]{1,0:T(8,128)} %local_conv.1.own_ref), channel_id=1, source_target_pairs={{0,256},{256,0},{1,257},{257,1},{2,258},{258,2},{3,259},{259,3},{4... | collective-permute-start | bytes 1671176 | tf_op jit(solution)/shard_map/ppermute | solution.py:340
  24.1 0.6 pad_add_fusion.place_ref
  24.7 0.0 collective-permute-done.1.refs_1_.refs_4_.refs_7_.refs_10_
  24.7 3.8 %collective-permute-start.2 = (f32[128,2048]{1,0:T(8,128)}, f32[128,2048]{1,0:T(8,128)}, u32[]{:S(2)}, u32[]{:S(2)}) collective-permute-start(f32[128,2048]{1,0:T(8,128)} %collective-permute-done.1.refs_1_.refs_4_.refs_7_.refs_10_), channel_id=1, source_target_pairs={{0,1},{1,0},{2,3},{3,2},{4,5},{5,4},{6,7},{7,6},{8,9},{9,8},{10,11... | collective-permute-start | bytes 3145736 | tf_op jit(solution)/shard_map/ppermute | solution.py:332
  28.5 1.7 %all-to-all-done.chips_ref = f32[16,16,256]{2,1,0:T(8,128)S(1)} async-done(((f32[16,16,256]{2,1,0:T(8,128)}), f32[16,16,256]{2,1,0:T(8,128)S(1)}, u32[]{:S(2)}, u32[]{:S(2)}) %all-to-all-start) | async-done | bytes 262176 | tf_op jit(solution)/shard_map/all_to_all | solution.py:336
  30.2 0.0 copy-start
  30.2 2.2 %chip_scan.1 = f32[2,16,256]{2,1,0:T(8,128)} custom-call(s32[4]{0:T(128)} %pad_add_fusion.place_ref, f32[16,16,256]{2,1,0:T(8,128)S(1)} %all-to-all-done.chips_ref, f32[16,16,256]{2,1,0:T(8,128)} %get-tuple-element.7.own_ref, f32[16,256]{1,0:T(8,128)} %decay_ref.5), custom_call_target="tpu_custom_call" | custom-call | flops 199999995904 | bytes 200000000 | tf_op jit(solution)/shard_map/chip_scan/pallas_call | solution.py:177
  32.4 9.1 %all-gather = f32[8,16,256]{2,1,0:T(8,128)S(1)} all-gather(f32[2,16,256]{2,1,0:T(8,128)} %chip_scan.1), channel_id=2, replica_groups=mesh['xl'=2,'yh'=4,'yl'=2,'z'=8,'xh'=2,'core'=2] {'xl','core'}, dimensions={0}, use_global_device_ids=true | all-gather | bytes 163840 | tf_op jit(solution)/shard_map/all_gather | solution.py:342
  41.5 0.0 collective-permute-done.peer_ref
  41.5 0.0 copy-done
  41.5 3.1 %gated_both.1.gated_ref = bf16[256,512]{1,0:T(8,128)(2,1)} custom-call(s32[4]{0:T(128)} %pad_add_fusion.place_ref, f32[4,2,16,256]{3,2,1,0:T(8,128)S(1)} %bitcast.19, f32[544,256]{1,0:T(8,128)S(1)} %copy-done, f32[544,256]{1,0:T(8,128)} %collective-permute-done.peer_ref), custom_call_target="tpu_custom_call" | custom-call | tf_op jit(solution)/shard_map/gated_both/pallas_call | solution.py:239
  44.6 0.0 collective-permute-done.2.refs_2_.refs_5_.refs_8_.refs_11_
  44.6 2.8 %project_leaving.1 = f32[4,256,256]{2,1,0:T(8,128)S(1)} custom-call(s32[4]{0:T(128)} %pad_add_fusion.place_ref, bf16[256,512]{1,0:T(8,128)(2,1)} %gated_both.1.gated_ref, bf16[256,4096]{1,0:T(8,128)(2,1)} %refs_9_.3, f32[128,2048]{1,0:T(8,128)} %collective-permute-done.1.refs_1_.refs_4_.refs_7_.refs_10_, ...), custom_call_target="tpu_custom_call" | custom-call | tf_op jit(solution)/shard_map/project_leaving/pallas_call | solution.py:286
  47.4 5.1 %collective-permute-start.3 = (f32[4,256,256]{2,1,0:T(8,128)S(1)}, f32[4,256,256]{2,1,0:T(8,128)S(1)}, u32[]{:S(2)}, u32[]{:S(2)}) collective-permute-start(f32[4,256,256]{2,1,0:T(8,128)S(1)} %project_leaving.1), channel_id=1, source_target_pairs={{0,32},{1,225},{32,0},{33,65},{64,96},{65,33},{96,64},{97,129},{12... | collective-permute-start | bytes 3145736 | tf_op jit(solution)/shard_map/ppermute | solution.py:345
  52.5 2.8 %project_kept.1 = f32[4,256,256]{2,1,0:T(8,128)S(1)} custom-call(s32[4]{0:T(128)} %pad_add_fusion.place_ref, bf16[256,512]{1,0:T(8,128)(2,1)} %gated_both.1.gated_ref, bf16[256,4096]{1,0:T(8,128)(2,1)} %refs_9_.3, f32[128,2048]{1,0:T(8,128)} %collective-permute-done.1.refs_1_.refs_4_.refs_7_.refs_10_, ...), custom_call_target="tpu_custom_call" | custom-call | tf_op jit(solution)/shard_map/project_kept/pallas_call | solution.py:286
  55.3 9.4 %collective-permute-done.3 = f32[4,256,256]{2,1,0:T(8,128)S(1)} collective-permute-done((f32[4,256,256]{2,1,0:T(8,128)S(1)}, f32[4,256,256]{2,1,0:T(8,128)S(1)}, u32[]{:S(2)}, u32[]{:S(2)}) %collective-permute-start.3) | collective-permute-done | bytes 1048608 | tf_op jit(solution)/shard_map/ppermute | solution.py:345
  64.7 0.1 add.46
  64.8 0.1 dynamic-slice_bitcast_fusion.2
  64.9 7.0 %collective-permute-start.6 = (f32[256,256]{1,0:T(8,128)S(1)}, f32[256,256]{1,0:T(8,128)S(1)}, u32[]{:S(2)}, u32[]{:S(2)}) collective-permute-start(f32[256,256]{1,0:T(8,128)S(1)} %get-tuple-element.10), channel_id=1, source_target_pairs={{0,128},{64,192},{128,0},{192,64},{1,129},{65,193},{129,1},{193,65... | collective-permute-start | bytes 786440 | tf_op jit(solution)/shard_map/ppermute | solution.py:352
  71.8 1.9 %collective-permute-start.5 = (f32[256,256]{1,0:T(8,128)S(1)}, f32[256,256]{1,0:T(8,128)S(1)}, u32[]{:S(2)}, u32[]{:S(2)}) collective-permute-start(f32[256,256]{1,0:T(8,128)S(1)} %get-tuple-element.11), channel_id=1, source_target_pairs={{0,192},{64,0},{128,64},{192,128},{1,193},{65,1},{129,65},{193,129... | collective-permute-start | bytes 786440 | tf_op jit(solution)/shard_map/ppermute | solution.py:352
  73.8 4.3 %collective-permute-start.4 = (f32[256,256]{1,0:T(8,128)S(1)}, f32[256,256]{1,0:T(8,128)S(1)}, u32[]{:S(2)}, u32[]{:S(2)}) collective-permute-start(f32[256,256]{1,0:T(8,128)S(1)} %get-tuple-element.9), channel_id=1, source_target_pairs={{0,64},{64,128},{128,192},{192,0},{1,65},{65,129},{129,193},{193,1... | collective-permute-start | bytes 786440 | tf_op jit(solution)/shard_map/ppermute | solution.py:352
  78.0 6.3 %collective-permute-done.6 = f32[256,256]{1,0:T(8,128)S(1)} collective-permute-done((f32[256,256]{1,0:T(8,128)S(1)}, f32[256,256]{1,0:T(8,128)S(1)}, u32[]{:S(2)}, u32[]{:S(2)}) %collective-permute-start.6) | collective-permute-done | bytes 262176 | tf_op jit(solution)/shard_map/ppermute | solution.py:352
  84.3 11.1 %collective-permute-done.5 = f32[256,256]{1,0:T(8,128)S(1)} collective-permute-done((f32[256,256]{1,0:T(8,128)S(1)}, f32[256,256]{1,0:T(8,128)S(1)}, u32[]{:S(2)}, u32[]{:S(2)}) %collective-permute-start.5) | collective-permute-done | bytes 262176 | tf_op jit(solution)/shard_map/ppermute | solution.py:352
  95.4 0.0 collective-permute-done.4
  95.4 0.7 fusion.2
Async XLA Ops:
  1.1 23.6 %collective-permute-start.1 = (f32[128,2048]{1,0:T(8,128)S(1)}, f32[128,2048]{1,0:T(8,128)}, u32[]{:S(2)}, u32[]{:S(2)}) collective-permute-start(f32[128,2048]{1,0:T(8,128)S(1)} %dynamic-slice_convert_fusion), channel_id=1, source_target_pairs={{0,256},{1,259},{2,258},{3,257},{256,0},{257,3},{258,2},{259,1},{4... | collective-permute-start | bytes 3145736 | tf_op jit(solution)/shard_map/ppermute | solution.py:331
  8.5 21.6 %all-to-all-start = ((f32[16,16,256]{2,1,0:T(8,128)}), f32[16,16,256]{2,1,0:T(8,128)S(1)}, u32[]{:S(2)}, u32[]{:S(2)}) async-start(f32[16,16,256]{2,1,0:T(8,128)} %get-tuple-element.7.own_ref), calls=%async_computation | async-start | bytes 524288 | tf_op jit(solution)/shard_map/all_to_all | solution.py:336
  22.0 19.6 %collective-permute-start = (f32[544,256]{1,0:T(8,128)}, f32[544,256]{1,0:T(8,128)}, u32[]{:S(2)}, u32[]{:S(2)}) collective-permute-start(f32[544,256]{1,0:T(8,128)} %local_conv.1.own_ref), channel_id=1, source_target_pairs={{0,256},{256,0},{1,257},{257,1},{2,258},{258,2},{3,259},{259,3},{4... | collective-permute-start | bytes 1671176 | tf_op jit(solution)/shard_map/ppermute | solution.py:340
  24.7 19.9 %collective-permute-start.2 = (f32[128,2048]{1,0:T(8,128)}, f32[128,2048]{1,0:T(8,128)}, u32[]{:S(2)}, u32[]{:S(2)}) collective-permute-start(f32[128,2048]{1,0:T(8,128)} %collective-permute-done.1.refs_1_.refs_4_.refs_7_.refs_10_), channel_id=1, source_target_pairs={{0,1},{1,0},{2,3},{3,2},{4,5},{5,4},{6,7},{7,6},{8,9},{9,8},{10,11... | collective-permute-start | bytes 3145736 | tf_op jit(solution)/shard_map/ppermute | solution.py:332
  30.2 11.3 %copy-start = (f32[544,256]{1,0:T(8,128)S(1)}, f32[544,256]{1,0:T(8,128)}, u32[]{:S(2)}) copy-start(f32[544,256]{1,0:T(8,128)} %local_conv.1.own_ref) | copy-start | bytes 1671172
  47.4 17.3 %collective-permute-start.3 = (f32[4,256,256]{2,1,0:T(8,128)S(1)}, f32[4,256,256]{2,1,0:T(8,128)S(1)}, u32[]{:S(2)}, u32[]{:S(2)}) collective-permute-start(f32[4,256,256]{2,1,0:T(8,128)S(1)} %project_leaving.1), channel_id=1, source_target_pairs={{0,32},{1,225},{32,0},{33,65},{64,96},{65,33},{96,64},{97,129},{12... | collective-permute-start | bytes 3145736 | tf_op jit(solution)/shard_map/ppermute | solution.py:345
  64.9 19.4 %collective-permute-start.6 = (f32[256,256]{1,0:T(8,128)S(1)}, f32[256,256]{1,0:T(8,128)S(1)}, u32[]{:S(2)}, u32[]{:S(2)}) collective-permute-start(f32[256,256]{1,0:T(8,128)S(1)} %get-tuple-element.10), channel_id=1, source_target_pairs={{0,128},{64,192},{128,0},{192,64},{1,129},{65,193},{129,1},{193,65... | collective-permute-start | bytes 786440 | tf_op jit(solution)/shard_map/ppermute | solution.py:352
  71.8 23.6 %collective-permute-start.5 = (f32[256,256]{1,0:T(8,128)S(1)}, f32[256,256]{1,0:T(8,128)S(1)}, u32[]{:S(2)}, u32[]{:S(2)}) collective-permute-start(f32[256,256]{1,0:T(8,128)S(1)} %get-tuple-element.11), channel_id=1, source_target_pairs={{0,192},{64,0},{128,64},{192,128},{1,193},{65,1},{129,65},{193,129... | collective-permute-start | bytes 786440 | tf_op jit(solution)/shard_map/ppermute | solution.py:352
  73.8 21.6 %collective-permute-start.4 = (f32[256,256]{1,0:T(8,128)S(1)}, f32[256,256]{1,0:T(8,128)S(1)}, u32[]{:S(2)}, u32[]{:S(2)}) collective-permute-start(f32[256,256]{1,0:T(8,128)S(1)} %get-tuple-element.9), channel_id=1, source_target_pairs={{0,64},{64,128},{128,192},{192,0},{1,65},{65,129},{129,193},{193,1... | collective-permute-start | bytes 786440 | tf_op jit(solution)/shard_map/ppermute | solution.py:352

commit v8 on v7

--- a/solution.py
+++ b/solution.py
@@ -176,7 +176,7 @@
     shape = (2,) + decay.shape
     return pl.pallas_call(
         functools.partial(scan_kernel, rows=rows),
-        out_shape=jax.ShapeDtypeStruct(shape, jnp.float32),
+        out_shape=pltpu.VMEM(shape, jnp.float32),
         grid_spec=pltpu.PrefetchScalarGridSpec(
             num_scalar_prefetch=1,
             grid=(1,),
@@ -238,7 +238,7 @@
     args = (near_core(states), near_core(own), near_core(peer))
     return pl.pallas_call(
         gate_kernel,
-        out_shape=jax.ShapeDtypeStruct((rows, 2 * chans), jnp.bfloat16),
+        out_shape=pltpu.VMEM((rows, 2 * chans), jnp.bfloat16),
         grid_spec=pltpu.PrefetchScalarGridSpec(
             num_scalar_prefetch=1,
             grid=(1,),
@@ -295,7 +295,7 @@
             out_specs=whole((4, rows, chans)),
         ),
         name=name,
-    )(place, gated, *[weight, near, far] * 4)
+    )(place, near_core(gated), *[weight, near, far] * 4)
 
 
 def neighbour_routes(count):

time: 96.8 us -> 96 us (level)
  Pallas kernels: 16 us -> 14.6 us
    pallas_call x2, Pallas kernels: 5.31 us -> 3.99 us  [the longest x1 2.4 us: gated_both(): pl.pallas_call(gate_kernel, out_shape=pltpu.VMEM((rows, 2 * chans), jnp.b...]
  transfers between devices with their start and end apart: 8 -> 8, of which waited for: 4 -> 4; matrix products, arithmetic and copies ran while one was open for 1% -> 1% of each run, Pallas kernels for 14% -> 12%
where the time goes in v8:
time: 96 us; the launch traced here: 95.3 us
  starting transfers between devices  39.7 us (41%)
  waiting for transfers between devices  28.5 us (30%)
  Pallas kernels  14.6 us (15%)
  blocking collectives  9.74 us (10%)
  other arithmetic  2.57 us (3%)
    ppermute x3, waiting for transfers between devices, on_device(): result += lax.ppermute(block, 'yh', [(h, (h + d) % 4) for h in range(4)])  17.4 us
    ppermute x3, starting transfers between devices, on_device(): result += lax.ppermute(block, 'yh', [(h, (h + d) % 4) for h in range(4)])  13.1 us
    all_to_all x1, starting transfers between devices, on_device(): lax.all_to_all(copies, ('z', 'xh'), split_axis=0, concat_axis=0, tiled=True)  10.4 us
    all_gather x1, blocking collectives, on_device(): scanned = lax.all_gather(scanned, ('xl', 'core'), axis=0)  9.74 us
    ppermute x1, waiting for transfers between devices, on_device(): arrived = lax.ppermute(leaving, ('yh', 'yl', 'core'), neighbour_routes(8))  9.47 us
    pallas_call x2, Pallas kernels, project(): pl.pallas_call(project_kernel, out_shape=pltpu.VMEM((4, rows, chans), jnp...  5.38 us
    ppermute x1, starting transfers between devices, on_device(): near = lax.ppermute(sent, ('xl', 'xh', 'core'), weight_routes())  5.22 us
    ppermute x1, starting transfers between devices, on_device(): arrived = lax.ppermute(leaving, ('yh', 'yl', 'core'), neighbour_routes(8))  5.1 us
  transfers between devices with their start and end apart: 8, of which 4 were waited for; matrix products, arithmetic and copies ran while one was open for 1% of the time, Pallas kernels for 12%

profile of v8, /device:TPU:1, one launch (start us, length us, event | category | flops | bytes accessed | tf_op | source)
XLA Modules:
  0.0 95.3 jit_solution(13661113297809516066)
XLA Ops:
  0.0 1.1 %dynamic-slice_convert_fusion = f32[128,2048]{1,0:T(8,128)S(1)} fusion(bf16[256,4096]{1,0:T(8,128)(2,1)} %refs_9_.3, s32[]{:T(128)S(6)} %select_n.19, s32[]{:T(128)S(6)} %select_n.20), kind=kLoop, calls=%fused_computation | loop fusion | flops 262144 | bytes 1572872 | tf_op jit(solution)/shard_map/convert_element_type | solution.py:330
  1.1 5.2 %collective-permute-start.1 = (f32[128,2048]{1,0:T(8,128)S(1)}, f32[128,2048]{1,0:T(8,128)}, u32[]{:S(2)}, u32[]{:S(2)}) collective-permute-start(f32[128,2048]{1,0:T(8,128)S(1)} %dynamic-slice_convert_fusion), channel_id=1, source_target_pairs={{0,256},{1,259},{2,258},{3,257},{256,0},{257,3},{258,2},{259,1},{4... | collective-permute-start | bytes 3145736 | tf_op jit(solution)/shard_map/ppermute | solution.py:331
  6.4 2.2 %local_states.1 = (f32[4,16,256]{2,1,0:T(8,128)}, f32[16,16,256]{2,1,0:T(8,128)}) custom-call(bf16[256,256]{1,0:T(8,128)(2,1)} %key_ref.3, bf16[256,256]{1,0:T(8,128)(2,1)} %value_ref.3, f32[16,256]{1,0:T(8,128)} %decay_ref.5), custom_call_target="tpu_custom_call" | custom-call | tf_op jit(solution)/shard_map/local_states/pallas_call | solution.py:73
  8.5 10.4 %all-to-all-start = ((f32[16,16,256]{2,1,0:T(8,128)}), f32[16,16,256]{2,1,0:T(8,128)S(1)}, u32[]{:S(2)}, u32[]{:S(2)}) async-start(f32[16,16,256]{2,1,0:T(8,128)} %get-tuple-element.7.own_ref), calls=%async_computation | async-start | bytes 524288 | tf_op jit(solution)/shard_map/all_to_all | solution.py:336
  18.9 3.0 %local_conv.1.own_ref = f32[544,256]{1,0:T(8,128)} custom-call(f32[4,16,256]{2,1,0:T(8,128)} %get-tuple-element.8.blocks_ref, bf16[256,256]{1,0:T(8,128)(2,1)} %gate_ref.1, bf16[256,256]{1,0:T(8,128)(2,1)} %key_ref.3, bf16[256,256]{1,0:T(8,128)(2,1)} %value_ref.3, f32[16,256]{1,0:T(8,128)} %residues_ref.1, f32[16,256]{1,0:T(8,128)} %decay_ref.5), custom_call_target="tpu_custom_call" | custom-call | tf_op jit(solution)/shard_map/local_conv/pallas_call | solution.py:156
  21.9 2.2 %collective-permute-start = (f32[544,256]{1,0:T(8,128)}, f32[544,256]{1,0:T(8,128)}, u32[]{:S(2)}, u32[]{:S(2)}) collective-permute-start(f32[544,256]{1,0:T(8,128)} %local_conv.1.own_ref), channel_id=1, source_target_pairs={{0,256},{256,0},{1,257},{257,1},{2,258},{258,2},{3,259},{259,3},{4... | collective-permute-start | bytes 1671176 | tf_op jit(solution)/shard_map/ppermute | solution.py:340
  24.1 0.6 pad_add_fusion.place_ref
  24.7 0.0 collective-permute-done.1.refs_1_.refs_4_.refs_7_.refs_10_
  24.7 3.8 %collective-permute-start.2 = (f32[128,2048]{1,0:T(8,128)}, f32[128,2048]{1,0:T(8,128)}, u32[]{:S(2)}, u32[]{:S(2)}) collective-permute-start(f32[128,2048]{1,0:T(8,128)} %collective-permute-done.1.refs_1_.refs_4_.refs_7_.refs_10_), channel_id=1, source_target_pairs={{0,1},{1,0},{2,3},{3,2},{4,5},{5,4},{6,7},{7,6},{8,9},{9,8},{10,11... | collective-permute-start | bytes 3145736 | tf_op jit(solution)/shard_map/ppermute | solution.py:332
  28.5 1.7 %all-to-all-done.chips_ref = f32[16,16,256]{2,1,0:T(8,128)S(1)} async-done(((f32[16,16,256]{2,1,0:T(8,128)}), f32[16,16,256]{2,1,0:T(8,128)S(1)}, u32[]{:S(2)}, u32[]{:S(2)}) %all-to-all-start) | async-done | bytes 262176 | tf_op jit(solution)/shard_map/all_to_all | solution.py:336
  30.2 0.0 copy-start
  30.2 1.6 %chip_scan.1 = f32[2,16,256]{2,1,0:T(8,128)S(1)} custom-call(s32[4]{0:T(128)} %pad_add_fusion.place_ref, f32[16,16,256]{2,1,0:T(8,128)S(1)} %all-to-all-done.chips_ref, f32[16,16,256]{2,1,0:T(8,128)} %get-tuple-element.7.own_ref, f32[16,256]{1,0:T(8,128)} %decay_ref.5), custom_call_target="tpu_custom_call" | custom-call | flops 199999995904 | bytes 200000000 | tf_op jit(solution)/shard_map/chip_scan/pallas_call | solution.py:177
  31.8 9.7 %all-gather = f32[8,16,256]{2,1,0:T(8,128)S(1)} all-gather(f32[2,16,256]{2,1,0:T(8,128)S(1)} %chip_scan.1), channel_id=2, replica_groups=mesh['xl'=2,'yh'=4,'yl'=2,'z'=8,'xh'=2,'core'=2] {'xl','core'}, dimensions={0}, use_global_device_ids=true | all-gather | bytes 163840 | tf_op jit(solution)/shard_map/all_gather | solution.py:342
  41.5 0.0 collective-permute-done.peer_ref
  41.5 0.0 copy-done
  41.5 2.4 %gated_both.1.gated_ref = bf16[256,512]{1,0:T(8,128)(2,1)S(1)} custom-call(s32[4]{0:T(128)} %pad_add_fusion.place_ref, f32[4,2,16,256]{3,2,1,0:T(8,128)S(1)} %bitcast.19, f32[544,256]{1,0:T(8,128)S(1)} %copy-done, f32[544,256]{1,0:T(8,128)} %collective-permute-done.peer_ref), custom_call_target="tpu_custom_call" | custom-call | tf_op jit(solution)/shard_map/gated_both/pallas_call | solution.py:239
  43.9 0.0 collective-permute-done.2.refs_2_.refs_5_.refs_8_.refs_11_
  43.9 2.7 %project_leaving.1 = f32[4,256,256]{2,1,0:T(8,128)S(1)} custom-call(s32[4]{0:T(128)} %pad_add_fusion.place_ref, bf16[256,512]{1,0:T(8,128)(2,1)S(1)} %gated_both.1.gated_ref, bf16[256,4096]{1,0:T(8,128)(2,1)} %refs_9_.3, f32[128,2048]{1,0:T(8,128)} %collective-permute-done.1.refs_1_.refs_4_.refs_7_.refs_10_, ...), custom_call_target="tpu_custom_call" | custom-call | tf_op jit(solution)/shard_map/project_leaving/pallas_call | solution.py:286
  46.6 5.1 %collective-permute-start.3 = (f32[4,256,256]{2,1,0:T(8,128)S(1)}, f32[4,256,256]{2,1,0:T(8,128)S(1)}, u32[]{:S(2)}, u32[]{:S(2)}) collective-permute-start(f32[4,256,256]{2,1,0:T(8,128)S(1)} %project_leaving.1), channel_id=1, source_target_pairs={{0,32},{1,225},{32,0},{33,65},{64,96},{65,33},{96,64},{97,129},{12... | collective-permute-start | bytes 3145736 | tf_op jit(solution)/shard_map/ppermute | solution.py:345
  51.7 2.7 %project_kept.1 = f32[4,256,256]{2,1,0:T(8,128)S(1)} custom-call(s32[4]{0:T(128)} %pad_add_fusion.place_ref, bf16[256,512]{1,0:T(8,128)(2,1)S(1)} %gated_both.1.gated_ref, bf16[256,4096]{1,0:T(8,128)(2,1)} %refs_9_.3, f32[128,2048]{1,0:T(8,128)} %collective-permute-done.1.refs_1_.refs_4_.refs_7_.refs_10_, ...), custom_call_target="tpu_custom_call" | custom-call | tf_op jit(solution)/shard_map/project_kept/pallas_call | solution.py:286
  54.4 9.5 %collective-permute-done.3 = f32[4,256,256]{2,1,0:T(8,128)S(1)} collective-permute-done((f32[4,256,256]{2,1,0:T(8,128)S(1)}, f32[4,256,256]{2,1,0:T(8,128)S(1)}, u32[]{:S(2)}, u32[]{:S(2)}) %collective-permute-start.3) | collective-permute-done | bytes 1048608 | tf_op jit(solution)/shard_map/ppermute | solution.py:345
  63.9 0.1 add.46
  64.0 0.1 dynamic-slice_bitcast_fusion.2
  64.1 6.9 %collective-permute-start.6 = (f32[256,256]{1,0:T(8,128)S(1)}, f32[256,256]{1,0:T(8,128)S(1)}, u32[]{:S(2)}, u32[]{:S(2)}) collective-permute-start(f32[256,256]{1,0:T(8,128)S(1)} %get-tuple-element.10), channel_id=1, source_target_pairs={{0,128},{64,192},{128,0},{192,64},{1,129},{65,193},{129,1},{193,65... | collective-permute-start | bytes 786440 | tf_op jit(solution)/shard_map/ppermute | solution.py:352
  71.1 1.9 %collective-permute-start.5 = (f32[256,256]{1,0:T(8,128)S(1)}, f32[256,256]{1,0:T(8,128)S(1)}, u32[]{:S(2)}, u32[]{:S(2)}) collective-permute-start(f32[256,256]{1,0:T(8,128)S(1)} %get-tuple-element.11), channel_id=1, source_target_pairs={{0,192},{64,0},{128,64},{192,128},{1,193},{65,1},{129,65},{193,129... | collective-permute-start | bytes 786440 | tf_op jit(solution)/shard_map/ppermute | solution.py:352
  73.0 4.3 %collective-permute-start.4 = (f32[256,256]{1,0:T(8,128)S(1)}, f32[256,256]{1,0:T(8,128)S(1)}, u32[]{:S(2)}, u32[]{:S(2)}) collective-permute-start(f32[256,256]{1,0:T(8,128)S(1)} %get-tuple-element.9), channel_id=1, source_target_pairs={{0,64},{64,128},{128,192},{192,0},{1,65},{65,129},{129,193},{193,1... | collective-permute-start | bytes 786440 | tf_op jit(solution)/shard_map/ppermute | solution.py:352
  77.3 6.3 %collective-permute-done.6 = f32[256,256]{1,0:T(8,128)S(1)} collective-permute-done((f32[256,256]{1,0:T(8,128)S(1)}, f32[256,256]{1,0:T(8,128)S(1)}, u32[]{:S(2)}, u32[]{:S(2)}) %collective-permute-start.6) | collective-permute-done | bytes 262176 | tf_op jit(solution)/shard_map/ppermute | solution.py:352
  83.6 11.1 %collective-permute-done.5 = f32[256,256]{1,0:T(8,128)S(1)} collective-permute-done((f32[256,256]{1,0:T(8,128)S(1)}, f32[256,256]{1,0:T(8,128)S(1)}, u32[]{:S(2)}, u32[]{:S(2)}) %collective-permute-start.5) | collective-permute-done | bytes 262176 | tf_op jit(solution)/shard_map/ppermute | solution.py:352
  94.6 0.0 collective-permute-done.4
  94.6 0.7 fusion.2
Async XLA Ops:
  1.1 23.6 %collective-permute-start.1 = (f32[128,2048]{1,0:T(8,128)S(1)}, f32[128,2048]{1,0:T(8,128)}, u32[]{:S(2)}, u32[]{:S(2)}) collective-permute-start(f32[128,2048]{1,0:T(8,128)S(1)} %dynamic-slice_convert_fusion), channel_id=1, source_target_pairs={{0,256},{1,259},{2,258},{3,257},{256,0},{257,3},{258,2},{259,1},{4... | collective-permute-start | bytes 3145736 | tf_op jit(solution)/shard_map/ppermute | solution.py:331
  8.5 21.6 %all-to-all-start = ((f32[16,16,256]{2,1,0:T(8,128)}), f32[16,16,256]{2,1,0:T(8,128)S(1)}, u32[]{:S(2)}, u32[]{:S(2)}) async-start(f32[16,16,256]{2,1,0:T(8,128)} %get-tuple-element.7.own_ref), calls=%async_computation | async-start | bytes 524288 | tf_op jit(solution)/shard_map/all_to_all | solution.py:336
  21.9 19.6 %collective-permute-start = (f32[544,256]{1,0:T(8,128)}, f32[544,256]{1,0:T(8,128)}, u32[]{:S(2)}, u32[]{:S(2)}) collective-permute-start(f32[544,256]{1,0:T(8,128)} %local_conv.1.own_ref), channel_id=1, source_target_pairs={{0,256},{256,0},{1,257},{257,1},{2,258},{258,2},{3,259},{259,3},{4... | collective-permute-start | bytes 1671176 | tf_op jit(solution)/shard_map/ppermute | solution.py:340
  24.7 19.2 %collective-permute-start.2 = (f32[128,2048]{1,0:T(8,128)}, f32[128,2048]{1,0:T(8,128)}, u32[]{:S(2)}, u32[]{:S(2)}) collective-permute-start(f32[128,2048]{1,0:T(8,128)} %collective-permute-done.1.refs_1_.refs_4_.refs_7_.refs_10_), channel_id=1, source_target_pairs={{0,1},{1,0},{2,3},{3,2},{4,5},{5,4},{6,7},{7,6},{8,9},{9,8},{10,11... | collective-permute-start | bytes 3145736 | tf_op jit(solution)/shard_map/ppermute | solution.py:332
  30.2 11.3 %copy-start = (f32[544,256]{1,0:T(8,128)S(1)}, f32[544,256]{1,0:T(8,128)}, u32[]{:S(2)}) copy-start(f32[544,256]{1,0:T(8,128)} %local_conv.1.own_ref) | copy-start | bytes 1671172
  46.6 17.3 %collective-permute-start.3 = (f32[4,256,256]{2,1,0:T(8,128)S(1)}, f32[4,256,256]{2,1,0:T(8,128)S(1)}, u32[]{:S(2)}, u32[]{:S(2)}) collective-permute-start(f32[4,256,256]{2,1,0:T(8,128)S(1)} %project_leaving.1), channel_id=1, source_target_pairs={{0,32},{1,225},{32,0},{33,65},{64,96},{65,33},{96,64},{97,129},{12... | collective-permute-start | bytes 3145736 | tf_op jit(solution)/shard_map/ppermute | solution.py:345
  64.1 19.4 %collective-permute-start.6 = (f32[256,256]{1,0:T(8,128)S(1)}, f32[256,256]{1,0:T(8,128)S(1)}, u32[]{:S(2)}, u32[]{:S(2)}) collective-permute-start(f32[256,256]{1,0:T(8,128)S(1)} %get-tuple-element.10), channel_id=1, source_target_pairs={{0,128},{64,192},{128,0},{192,64},{1,129},{65,193},{129,1},{193,65... | collective-permute-start | bytes 786440 | tf_op jit(solution)/shard_map/ppermute | solution.py:352
  71.1 23.6 %collective-permute-start.5 = (f32[256,256]{1,0:T(8,128)S(1)}, f32[256,256]{1,0:T(8,128)S(1)}, u32[]{:S(2)}, u32[]{:S(2)}) collective-permute-start(f32[256,256]{1,0:T(8,128)S(1)} %get-tuple-element.11), channel_id=1, source_target_pairs={{0,192},{64,0},{128,64},{192,128},{1,193},{65,1},{129,65},{193,129... | collective-permute-start | bytes 786440 | tf_op jit(solution)/shard_map/ppermute | solution.py:352
  73.0 21.6 %collective-permute-start.4 = (f32[256,256]{1,0:T(8,128)S(1)}, f32[256,256]{1,0:T(8,128)S(1)}, u32[]{:S(2)}, u32[]{:S(2)}) collective-permute-start(f32[256,256]{1,0:T(8,128)S(1)} %get-tuple-element.9), channel_id=1, source_target_pairs={{0,64},{64,128},{128,192},{192,0},{1,65},{65,129},{129,193},{193,1... | collective-permute-start | bytes 786440 | tf_op jit(solution)/shard_map/ppermute | solution.py:352

commit v9 on v8

--- a/solution.py
+++ b/solution.py
@@ -25,6 +25,13 @@
     for k in (7.0, 6.0, 5.0, 4.0, 3.0, 2.0):
         series = 1.0 - x / k * series
     return jnp.where(x < 0.5, x * series, 1.0 - jnp.exp(-x))
+
+
+def tree_sum(terms):
+    while len(terms) > 1:
+        pairs = [a + b for a, b in zip(terms[::2], terms[1::2])]
+        terms = pairs + terms[len(terms) // 2 * 2 :]
+    return terms[0]
 
 
 def sub_iota():
@@ -99,7 +106,7 @@
         within = [jnp.exp(-decay[n : n + 1] * ahead) for n in range(modes)]
         kernel = [base[n : n + 1] * within[n] for n in range(modes)]
         for j in range(tiles):
-            taps_ref[pl.ds(j * SUB, SUB), :] = sum(kernel)
+            taps_ref[pl.ds(j * SUB, SUB), :] = tree_sum(kernel)
             if j + 1 < tiles:
                 kernel = [kernel[n] * step[n] for n in range(modes)]
         scale = base * jnp.exp(-decay)
@@ -121,7 +128,7 @@
                 if fade is None:
                     acc.append(jnp.zeros((SUB, LANES), jnp.float32))
                 else:
-                    acc.append(sum(fade))
+                    acc.append(tree_sum(fade))
                     fade = [fade[n] * step[n] for n in range(modes)]
                 mixed.append(
                     key_ref[at, lanes].astype(jnp.float32)
@@ -223,7 +230,7 @@
                 tiles = []
                 for row in (j, j + SUB):
                     gate = pack_ref[pl.ds(rows + row, SUB), lanes]
-                    tiles.append(pack_ref[pl.ds(row, SUB), lanes] + gate * sum(fade))
+                    tiles.append(pack_ref[pl.ds(row, SUB), lanes] + gate * tree_sum(fade))
                     fade = [fade[n] * step[n] for n in range(modes)]
                 out_ref[pl.ds(j, 2 * SUB), target] = jnp.concatenate(tiles).astype(
                     jnp.bfloat16

time: 96 us -> 96 us (level)
  no operation moved by 1% of the time
where the time goes in v9:
time: 96 us; the launch traced here: 95.3 us
  starting transfers between devices  39.7 us (41%)
  waiting for transfers between devices  28.5 us (30%)
  Pallas kernels  14.5 us (15%)
  blocking collectives  9.72 us (10%)
  other arithmetic  2.57 us (3%)
    ppermute x3, waiting for transfers between devices, on_device(): result += lax.ppermute(block, 'yh', [(h, (h + d) % 4) for h in range(4)])  17.4 us
    ppermute x3, starting transfers between devices, on_device(): result += lax.ppermute(block, 'yh', [(h, (h + d) % 4) for h in range(4)])  13.1 us
    all_to_all x1, starting transfers between devices, on_device(): lax.all_to_all(copies, ('z', 'xh'), split_axis=0, concat_axis=0, tiled=True)  10.4 us
    all_gather x1, blocking collectives, on_device(): scanned = lax.all_gather(scanned, ('xl', 'core'), axis=0)  9.72 us
    ppermute x1, waiting for transfers between devices, on_device(): arrived = lax.ppermute(leaving, ('yh', 'yl', 'core'), neighbour_routes(8))  9.47 us
    pallas_call x2, Pallas kernels, project(): pl.pallas_call(project_kernel, out_shape=pltpu.VMEM((4, rows, chans), jnp...  5.38 us
    ppermute x1, starting transfers between devices, on_device(): near = lax.ppermute(sent, ('xl', 'xh', 'core'), weight_routes())  5.22 us
    ppermute x1, starting transfers between devices, on_device(): arrived = lax.ppermute(leaving, ('yh', 'yl', 'core'), neighbour_routes(8))  5.1 us
  transfers between devices with their start and end apart: 8, of which 4 were waited for; matrix products, arithmetic and copies ran while one was open for 1% of the time, Pallas kernels for 12%

profile of v9, /device:TPU:1, one launch (start us, length us, event | category | flops | bytes accessed | tf_op | source)
XLA Modules:
  0.0 95.3 jit_solution(228865566322698790)
XLA Ops:
  0.0 1.1 %dynamic-slice_convert_fusion = f32[128,2048]{1,0:T(8,128)S(1)} fusion(bf16[256,4096]{1,0:T(8,128)(2,1)} %refs_9_.3, s32[]{:T(128)S(6)} %select_n.19, s32[]{:T(128)S(6)} %select_n.20), kind=kLoop, calls=%fused_computation | loop fusion | flops 262144 | bytes 1572872 | tf_op jit(solution)/shard_map/convert_element_type | solution.py:337
  1.1 5.2 %collective-permute-start.1 = (f32[128,2048]{1,0:T(8,128)S(1)}, f32[128,2048]{1,0:T(8,128)}, u32[]{:S(2)}, u32[]{:S(2)}) collective-permute-start(f32[128,2048]{1,0:T(8,128)S(1)} %dynamic-slice_convert_fusion), channel_id=1, source_target_pairs={{0,256},{1,259},{2,258},{3,257},{256,0},{257,3},{258,2},{259,1},{4... | collective-permute-start | bytes 3145736 | tf_op jit(solution)/shard_map/ppermute | solution.py:338
  6.4 2.2 %local_states.1 = (f32[4,16,256]{2,1,0:T(8,128)}, f32[16,16,256]{2,1,0:T(8,128)}) custom-call(bf16[256,256]{1,0:T(8,128)(2,1)} %key_ref.3, bf16[256,256]{1,0:T(8,128)(2,1)} %value_ref.3, f32[16,256]{1,0:T(8,128)} %decay_ref.5), custom_call_target="tpu_custom_call" | custom-call | tf_op jit(solution)/shard_map/local_states/pallas_call | solution.py:80
  8.5 10.4 %all-to-all-start = ((f32[16,16,256]{2,1,0:T(8,128)}), f32[16,16,256]{2,1,0:T(8,128)S(1)}, u32[]{:S(2)}, u32[]{:S(2)}) async-start(f32[16,16,256]{2,1,0:T(8,128)} %get-tuple-element.7.own_ref), calls=%async_computation | async-start | bytes 524288 | tf_op jit(solution)/shard_map/all_to_all | solution.py:343
  18.9 3.0 %local_conv.1.own_ref = f32[544,256]{1,0:T(8,128)} custom-call(f32[4,16,256]{2,1,0:T(8,128)} %get-tuple-element.8.blocks_ref, bf16[256,256]{1,0:T(8,128)(2,1)} %gate_ref.1, bf16[256,256]{1,0:T(8,128)(2,1)} %key_ref.3, bf16[256,256]{1,0:T(8,128)(2,1)} %value_ref.3, f32[16,256]{1,0:T(8,128)} %residues_ref.1, f32[16,256]{1,0:T(8,128)} %decay_ref.5), custom_call_target="tpu_custom_call" | custom-call | tf_op jit(solution)/shard_map/local_conv/pallas_call | solution.py:163
  21.9 2.2 %collective-permute-start = (f32[544,256]{1,0:T(8,128)}, f32[544,256]{1,0:T(8,128)}, u32[]{:S(2)}, u32[]{:S(2)}) collective-permute-start(f32[544,256]{1,0:T(8,128)} %local_conv.1.own_ref), channel_id=1, source_target_pairs={{0,256},{256,0},{1,257},{257,1},{2,258},{258,2},{3,259},{259,3},{4... | collective-permute-start | bytes 1671176 | tf_op jit(solution)/shard_map/ppermute | solution.py:347
  24.1 0.6 pad_add_fusion.place_ref
  24.7 0.0 collective-permute-done.1.refs_1_.refs_4_.refs_7_.refs_10_
  24.7 3.8 %collective-permute-start.2 = (f32[128,2048]{1,0:T(8,128)}, f32[128,2048]{1,0:T(8,128)}, u32[]{:S(2)}, u32[]{:S(2)}) collective-permute-start(f32[128,2048]{1,0:T(8,128)} %collective-permute-done.1.refs_1_.refs_4_.refs_7_.refs_10_), channel_id=1, source_target_pairs={{0,1},{1,0},{2,3},{3,2},{4,5},{5,4},{6,7},{7,6},{8,9},{9,8},{10,11... | collective-permute-start | bytes 3145736 | tf_op jit(solution)/shard_map/ppermute | solution.py:339
  28.5 1.7 %all-to-all-done.chips_ref = f32[16,16,256]{2,1,0:T(8,128)S(1)} async-done(((f32[16,16,256]{2,1,0:T(8,128)}), f32[16,16,256]{2,1,0:T(8,128)S(1)}, u32[]{:S(2)}, u32[]{:S(2)}) %all-to-all-start) | async-done | bytes 262176 | tf_op jit(solution)/shard_map/all_to_all | solution.py:343
  30.2 0.0 copy-start
  30.2 1.6 %chip_scan.1 = f32[2,16,256]{2,1,0:T(8,128)S(1)} custom-call(s32[4]{0:T(128)} %pad_add_fusion.place_ref, f32[16,16,256]{2,1,0:T(8,128)S(1)} %all-to-all-done.chips_ref, f32[16,16,256]{2,1,0:T(8,128)} %get-tuple-element.7.own_ref, f32[16,256]{1,0:T(8,128)} %decay_ref.5), custom_call_target="tpu_custom_call" | custom-call | flops 199999995904 | bytes 200000000 | tf_op jit(solution)/shard_map/chip_scan/pallas_call | solution.py:184
  31.8 9.7 %all-gather = f32[8,16,256]{2,1,0:T(8,128)S(1)} all-gather(f32[2,16,256]{2,1,0:T(8,128)S(1)} %chip_scan.1), channel_id=2, replica_groups=mesh['xl'=2,'yh'=4,'yl'=2,'z'=8,'xh'=2,'core'=2] {'xl','core'}, dimensions={0}, use_global_device_ids=true | all-gather | bytes 163840 | tf_op jit(solution)/shard_map/all_gather | solution.py:349
  41.5 0.0 collective-permute-done.peer_ref
  41.5 0.0 copy-done
  41.5 2.4 %gated_both.1.gated_ref = bf16[256,512]{1,0:T(8,128)(2,1)S(1)} custom-call(s32[4]{0:T(128)} %pad_add_fusion.place_ref, f32[4,2,16,256]{3,2,1,0:T(8,128)S(1)} %bitcast.19, f32[544,256]{1,0:T(8,128)S(1)} %copy-done, f32[544,256]{1,0:T(8,128)} %collective-permute-done.peer_ref), custom_call_target="tpu_custom_call" | custom-call | tf_op jit(solution)/shard_map/gated_both/pallas_call | solution.py:246
  43.9 0.0 collective-permute-done.2.refs_2_.refs_5_.refs_8_.refs_11_
  43.9 2.7 %project_leaving.1 = f32[4,256,256]{2,1,0:T(8,128)S(1)} custom-call(s32[4]{0:T(128)} %pad_add_fusion.place_ref, bf16[256,512]{1,0:T(8,128)(2,1)S(1)} %gated_both.1.gated_ref, bf16[256,4096]{1,0:T(8,128)(2,1)} %refs_9_.3, f32[128,2048]{1,0:T(8,128)} %collective-permute-done.1.refs_1_.refs_4_.refs_7_.refs_10_, ...), custom_call_target="tpu_custom_call" | custom-call | tf_op jit(solution)/shard_map/project_leaving/pallas_call | solution.py:293
  46.6 5.1 %collective-permute-start.3 = (f32[4,256,256]{2,1,0:T(8,128)S(1)}, f32[4,256,256]{2,1,0:T(8,128)S(1)}, u32[]{:S(2)}, u32[]{:S(2)}) collective-permute-start(f32[4,256,256]{2,1,0:T(8,128)S(1)} %project_leaving.1), channel_id=1, source_target_pairs={{0,32},{1,225},{32,0},{33,65},{64,96},{65,33},{96,64},{97,129},{12... | collective-permute-start | bytes 3145736 | tf_op jit(solution)/shard_map/ppermute | solution.py:352
  51.7 2.7 %project_kept.1 = f32[4,256,256]{2,1,0:T(8,128)S(1)} custom-call(s32[4]{0:T(128)} %pad_add_fusion.place_ref, bf16[256,512]{1,0:T(8,128)(2,1)S(1)} %gated_both.1.gated_ref, bf16[256,4096]{1,0:T(8,128)(2,1)} %refs_9_.3, f32[128,2048]{1,0:T(8,128)} %collective-permute-done.1.refs_1_.refs_4_.refs_7_.refs_10_, ...), custom_call_target="tpu_custom_call" | custom-call | tf_op jit(solution)/shard_map/project_kept/pallas_call | solution.py:293
  54.4 9.5 %collective-permute-done.3 = f32[4,256,256]{2,1,0:T(8,128)S(1)} collective-permute-done((f32[4,256,256]{2,1,0:T(8,128)S(1)}, f32[4,256,256]{2,1,0:T(8,128)S(1)}, u32[]{:S(2)}, u32[]{:S(2)}) %collective-permute-start.3) | collective-permute-done | bytes 1048608 | tf_op jit(solution)/shard_map/ppermute | solution.py:352
  63.9 0.1 add.46
  64.0 0.1 dynamic-slice_bitcast_fusion.2
  64.1 6.9 %collective-permute-start.6 = (f32[256,256]{1,0:T(8,128)S(1)}, f32[256,256]{1,0:T(8,128)S(1)}, u32[]{:S(2)}, u32[]{:S(2)}) collective-permute-start(f32[256,256]{1,0:T(8,128)S(1)} %get-tuple-element.10), channel_id=1, source_target_pairs={{0,128},{64,192},{128,0},{192,64},{1,129},{65,193},{129,1},{193,65... | collective-permute-start | bytes 786440 | tf_op jit(solution)/shard_map/ppermute | solution.py:359
  71.0 1.9 %collective-permute-start.5 = (f32[256,256]{1,0:T(8,128)S(1)}, f32[256,256]{1,0:T(8,128)S(1)}, u32[]{:S(2)}, u32[]{:S(2)}) collective-permute-start(f32[256,256]{1,0:T(8,128)S(1)} %get-tuple-element.11), channel_id=1, source_target_pairs={{0,192},{64,0},{128,64},{192,128},{1,193},{65,1},{129,65},{193,129... | collective-permute-start | bytes 786440 | tf_op jit(solution)/shard_map/ppermute | solution.py:359
  73.0 4.3 %collective-permute-start.4 = (f32[256,256]{1,0:T(8,128)S(1)}, f32[256,256]{1,0:T(8,128)S(1)}, u32[]{:S(2)}, u32[]{:S(2)}) collective-permute-start(f32[256,256]{1,0:T(8,128)S(1)} %get-tuple-element.9), channel_id=1, source_target_pairs={{0,64},{64,128},{128,192},{192,0},{1,65},{65,129},{129,193},{193,1... | collective-permute-start | bytes 786440 | tf_op jit(solution)/shard_map/ppermute | solution.py:359
  77.2 6.3 %collective-permute-done.6 = f32[256,256]{1,0:T(8,128)S(1)} collective-permute-done((f32[256,256]{1,0:T(8,128)S(1)}, f32[256,256]{1,0:T(8,128)S(1)}, u32[]{:S(2)}, u32[]{:S(2)}) %collective-permute-start.6) | collective-permute-done | bytes 262176 | tf_op jit(solution)/shard_map/ppermute | solution.py:359
  83.5 11.1 %collective-permute-done.5 = f32[256,256]{1,0:T(8,128)S(1)} collective-permute-done((f32[256,256]{1,0:T(8,128)S(1)}, f32[256,256]{1,0:T(8,128)S(1)}, u32[]{:S(2)}, u32[]{:S(2)}) %collective-permute-start.5) | collective-permute-done | bytes 262176 | tf_op jit(solution)/shard_map/ppermute | solution.py:359
  94.6 0.0 collective-permute-done.4
  94.6 0.7 fusion.2
Async XLA Ops:
  1.1 23.5 %collective-permute-start.1 = (f32[128,2048]{1,0:T(8,128)S(1)}, f32[128,2048]{1,0:T(8,128)}, u32[]{:S(2)}, u32[]{:S(2)}) collective-permute-start(f32[128,2048]{1,0:T(8,128)S(1)} %dynamic-slice_convert_fusion), channel_id=1, source_target_pairs={{0,256},{1,259},{2,258},{3,257},{256,0},{257,3},{258,2},{259,1},{4... | collective-permute-start | bytes 3145736 | tf_op jit(solution)/shard_map/ppermute | solution.py:338
  8.5 21.6 %all-to-all-start = ((f32[16,16,256]{2,1,0:T(8,128)}), f32[16,16,256]{2,1,0:T(8,128)S(1)}, u32[]{:S(2)}, u32[]{:S(2)}) async-start(f32[16,16,256]{2,1,0:T(8,128)} %get-tuple-element.7.own_ref), calls=%async_computation | async-start | bytes 524288 | tf_op jit(solution)/shard_map/all_to_all | solution.py:343
  21.9 19.6 %collective-permute-start = (f32[544,256]{1,0:T(8,128)}, f32[544,256]{1,0:T(8,128)}, u32[]{:S(2)}, u32[]{:S(2)}) collective-permute-start(f32[544,256]{1,0:T(8,128)} %local_conv.1.own_ref), channel_id=1, source_target_pairs={{0,256},{256,0},{1,257},{257,1},{2,258},{258,2},{3,259},{259,3},{4... | collective-permute-start | bytes 1671176 | tf_op jit(solution)/shard_map/ppermute | solution.py:347
  24.7 19.2 %collective-permute-start.2 = (f32[128,2048]{1,0:T(8,128)}, f32[128,2048]{1,0:T(8,128)}, u32[]{:S(2)}, u32[]{:S(2)}) collective-permute-start(f32[128,2048]{1,0:T(8,128)} %collective-permute-done.1.refs_1_.refs_4_.refs_7_.refs_10_), channel_id=1, source_target_pairs={{0,1},{1,0},{2,3},{3,2},{4,5},{5,4},{6,7},{7,6},{8,9},{9,8},{10,11... | collective-permute-start | bytes 3145736 | tf_op jit(solution)/shard_map/ppermute | solution.py:339
  30.2 11.3 %copy-start = (f32[544,256]{1,0:T(8,128)S(1)}, f32[544,256]{1,0:T(8,128)}, u32[]{:S(2)}) copy-start(f32[544,256]{1,0:T(8,128)} %local_conv.1.own_ref) | copy-start | bytes 1671172
  46.6 17.3 %collective-permute-start.3 = (f32[4,256,256]{2,1,0:T(8,128)S(1)}, f32[4,256,256]{2,1,0:T(8,128)S(1)}, u32[]{:S(2)}, u32[]{:S(2)}) collective-permute-start(f32[4,256,256]{2,1,0:T(8,128)S(1)} %project_leaving.1), channel_id=1, source_target_pairs={{0,32},{1,225},{32,0},{33,65},{64,96},{65,33},{96,64},{97,129},{12... | collective-permute-start | bytes 3145736 | tf_op jit(solution)/shard_map/ppermute | solution.py:352
  64.1 19.4 %collective-permute-start.6 = (f32[256,256]{1,0:T(8,128)S(1)}, f32[256,256]{1,0:T(8,128)S(1)}, u32[]{:S(2)}, u32[]{:S(2)}) collective-permute-start(f32[256,256]{1,0:T(8,128)S(1)} %get-tuple-element.10), channel_id=1, source_target_pairs={{0,128},{64,192},{128,0},{192,64},{1,129},{65,193},{129,1},{193,65... | collective-permute-start | bytes 786440 | tf_op jit(solution)/shard_map/ppermute | solution.py:359
  71.0 23.6 %collective-permute-start.5 = (f32[256,256]{1,0:T(8,128)S(1)}, f32[256,256]{1,0:T(8,128)S(1)}, u32[]{:S(2)}, u32[]{:S(2)}) collective-permute-start(f32[256,256]{1,0:T(8,128)S(1)} %get-tuple-element.11), channel_id=1, source_target_pairs={{0,192},{64,0},{128,64},{192,128},{1,193},{65,1},{129,65},{193,129... | collective-permute-start | bytes 786440 | tf_op jit(solution)/shard_map/ppermute | solution.py:359
  73.0 21.6 %collective-permute-start.4 = (f32[256,256]{1,0:T(8,128)S(1)}, f32[256,256]{1,0:T(8,128)S(1)}, u32[]{:S(2)}, u32[]{:S(2)}) collective-permute-start(f32[256,256]{1,0:T(8,128)S(1)} %get-tuple-element.9), channel_id=1, source_target_pairs={{0,64},{64,128},{128,192},{192,0},{1,65},{65,129},{129,193},{193,1... | collective-permute-start | bytes 786440 | tf_op jit(solution)/shard_map/ppermute | solution.py:359

commit v10 on v8

--- a/solution.py
+++ b/solution.py
@@ -74,7 +74,7 @@
         state_kernel,
         out_shape=(
             jax.ShapeDtypeStruct((rows // BLOCK, modes, chans), jnp.float32),
-            jax.ShapeDtypeStruct((chips, modes, chans), jnp.float32),
+            pltpu.VMEM((chips, modes, chans), jnp.float32),
         ),
         name="local_states",
     )(key_stream, value_stream, decay_rates)
@@ -187,7 +187,7 @@
             flops=2 * 10**11, transcendentals=0, bytes_accessed=2 * 10**8
         ),
         name="chip_scan",
-    )(place, near_core(chips), copies, decay)
+    )(place, near_core(chips), near_core(copies), decay)
 
 
 def gate_kernel(place_ref, states_ref, own_ref, peer_ref, out_ref):

time: 96 us -> 96 us (level)
  no operation moved by 1% of the time
where the time goes in v10:
time: 96 us; the launch traced here: 95.3 us
  starting transfers between devices  39.7 us (41%)
  waiting for transfers between devices  28.5 us (30%)
  Pallas kernels  14.6 us (15%)
  blocking collectives  9.74 us (10%)
  other arithmetic  2.57 us (3%)
    ppermute x3, waiting for transfers between devices, on_device(): result += lax.ppermute(block, 'yh', [(h, (h + d) % 4) for h in range(4)])  17.4 us
    ppermute x3, starting transfers between devices, on_device(): result += lax.ppermute(block, 'yh', [(h, (h + d) % 4) for h in range(4)])  13.1 us
    all_to_all x1, starting transfers between devices, on_device(): lax.all_to_all(copies, ('z', 'xh'), split_axis=0, concat_axis=0, tiled=True)  10.4 us
    all_gather x1, blocking collectives, on_device(): scanned = lax.all_gather(scanned, ('xl', 'core'), axis=0)  9.74 us
    ppermute x1, waiting for transfers between devices, on_device(): arrived = lax.ppermute(leaving, ('yh', 'yl', 'core'), neighbour_routes(8))  9.47 us
    pallas_call x2, Pallas kernels, project(): pl.pallas_call(project_kernel, out_shape=pltpu.VMEM((4, rows, chans), jnp...  5.38 us
    ppermute x1, starting transfers between devices, on_device(): near = lax.ppermute(sent, ('xl', 'xh', 'core'), weight_routes())  5.22 us
    ppermute x1, starting transfers between devices, on_device(): arrived = lax.ppermute(leaving, ('yh', 'yl', 'core'), neighbour_routes(8))  5.1 us
  transfers between devices with their start and end apart: 8, of which 4 were waited for; matrix products, arithmetic and copies ran while one was open for 1% of the time, Pallas kernels for 12%

profile of v10, /device:TPU:1, one launch (start us, length us, event | category | flops | bytes accessed | tf_op | source)
XLA Modules:
  0.0 95.3 jit_solution(15385696680996522025)
XLA Ops:
  0.0 1.1 %dynamic-slice_convert_fusion = f32[128,2048]{1,0:T(8,128)S(1)} fusion(bf16[256,4096]{1,0:T(8,128)(2,1)} %refs_9_.3, s32[]{:T(128)S(6)} %select_n.19, s32[]{:T(128)S(6)} %select_n.20), kind=kLoop, calls=%fused_computation | loop fusion | flops 262144 | bytes 1572872 | tf_op jit(solution)/shard_map/convert_element_type | solution.py:330
  1.1 5.2 %collective-permute-start.1 = (f32[128,2048]{1,0:T(8,128)S(1)}, f32[128,2048]{1,0:T(8,128)}, u32[]{:S(2)}, u32[]{:S(2)}) collective-permute-start(f32[128,2048]{1,0:T(8,128)S(1)} %dynamic-slice_convert_fusion), channel_id=1, source_target_pairs={{0,256},{1,259},{2,258},{3,257},{256,0},{257,3},{258,2},{259,1},{4... | collective-permute-start | bytes 3145736 | tf_op jit(solution)/shard_map/ppermute | solution.py:331
  6.4 2.2 %local_states.1 = (f32[4,16,256]{2,1,0:T(8,128)}, f32[16,16,256]{2,1,0:T(8,128)}) custom-call(bf16[256,256]{1,0:T(8,128)(2,1)} %key_ref.3, bf16[256,256]{1,0:T(8,128)(2,1)} %value_ref.3, f32[16,256]{1,0:T(8,128)} %decay_ref.5), custom_call_target="tpu_custom_call" | custom-call | tf_op jit(solution)/shard_map/local_states/pallas_call | solution.py:73
  8.5 10.4 %all-to-all-start = ((f32[16,16,256]{2,1,0:T(8,128)}), f32[16,16,256]{2,1,0:T(8,128)S(1)}, u32[]{:S(2)}, u32[]{:S(2)}) async-start(f32[16,16,256]{2,1,0:T(8,128)} %get-tuple-element.7.own_ref), calls=%async_computation | async-start | bytes 524288 | tf_op jit(solution)/shard_map/all_to_all | solution.py:336
  18.9 3.0 %local_conv.1.own_ref = f32[544,256]{1,0:T(8,128)} custom-call(f32[4,16,256]{2,1,0:T(8,128)} %get-tuple-element.8.blocks_ref, bf16[256,256]{1,0:T(8,128)(2,1)} %gate_ref.1, bf16[256,256]{1,0:T(8,128)(2,1)} %key_ref.3, bf16[256,256]{1,0:T(8,128)(2,1)} %value_ref.3, f32[16,256]{1,0:T(8,128)} %residues_ref.1, f32[16,256]{1,0:T(8,128)} %decay_ref.5), custom_call_target="tpu_custom_call" | custom-call | tf_op jit(solution)/shard_map/local_conv/pallas_call | solution.py:156
  21.9 2.2 %collective-permute-start = (f32[544,256]{1,0:T(8,128)}, f32[544,256]{1,0:T(8,128)}, u32[]{:S(2)}, u32[]{:S(2)}) collective-permute-start(f32[544,256]{1,0:T(8,128)} %local_conv.1.own_ref), channel_id=1, source_target_pairs={{0,256},{256,0},{1,257},{257,1},{2,258},{258,2},{3,259},{259,3},{4... | collective-permute-start | bytes 1671176 | tf_op jit(solution)/shard_map/ppermute | solution.py:340
  24.1 0.6 pad_add_fusion.place_ref
  24.7 0.0 collective-permute-done.1.refs_1_.refs_4_.refs_7_.refs_10_
  24.7 3.8 %collective-permute-start.2 = (f32[128,2048]{1,0:T(8,128)}, f32[128,2048]{1,0:T(8,128)}, u32[]{:S(2)}, u32[]{:S(2)}) collective-permute-start(f32[128,2048]{1,0:T(8,128)} %collective-permute-done.1.refs_1_.refs_4_.refs_7_.refs_10_), channel_id=1, source_target_pairs={{0,1},{1,0},{2,3},{3,2},{4,5},{5,4},{6,7},{7,6},{8,9},{9,8},{10,11... | collective-permute-start | bytes 3145736 | tf_op jit(solution)/shard_map/ppermute | solution.py:332
  28.5 1.7 %all-to-all-done.chips_ref = f32[16,16,256]{2,1,0:T(8,128)S(1)} async-done(((f32[16,16,256]{2,1,0:T(8,128)}), f32[16,16,256]{2,1,0:T(8,128)S(1)}, u32[]{:S(2)}, u32[]{:S(2)}) %all-to-all-start) | async-done | bytes 262176 | tf_op jit(solution)/shard_map/all_to_all | solution.py:336
  30.2 0.0 copy-start
  30.2 1.6 %chip_scan.1 = f32[2,16,256]{2,1,0:T(8,128)S(1)} custom-call(s32[4]{0:T(128)} %pad_add_fusion.place_ref, f32[16,16,256]{2,1,0:T(8,128)S(1)} %all-to-all-done.chips_ref, f32[16,16,256]{2,1,0:T(8,128)} %get-tuple-element.7.own_ref, f32[16,256]{1,0:T(8,128)} %decay_ref.5), custom_call_target="tpu_custom_call" | custom-call | flops 199999995904 | bytes 200000000 | tf_op jit(solution)/shard_map/chip_scan/pallas_call | solution.py:177
  31.8 9.7 %all-gather = f32[8,16,256]{2,1,0:T(8,128)S(1)} all-gather(f32[2,16,256]{2,1,0:T(8,128)S(1)} %chip_scan.1), channel_id=2, replica_groups=mesh['xl'=2,'yh'=4,'yl'=2,'z'=8,'xh'=2,'core'=2] {'xl','core'}, dimensions={0}, use_global_device_ids=true | all-gather | bytes 163840 | tf_op jit(solution)/shard_map/all_gather | solution.py:342
  41.5 0.0 collective-permute-done.peer_ref
  41.5 0.0 copy-done
  41.5 2.4 %gated_both.1.gated_ref = bf16[256,512]{1,0:T(8,128)(2,1)S(1)} custom-call(s32[4]{0:T(128)} %pad_add_fusion.place_ref, f32[4,2,16,256]{3,2,1,0:T(8,128)S(1)} %bitcast.19, f32[544,256]{1,0:T(8,128)S(1)} %copy-done, f32[544,256]{1,0:T(8,128)} %collective-permute-done.peer_ref), custom_call_target="tpu_custom_call" | custom-call | tf_op jit(solution)/shard_map/gated_both/pallas_call | solution.py:239
  43.9 0.0 collective-permute-done.2.refs_2_.refs_5_.refs_8_.refs_11_
  43.9 2.7 %project_leaving.1 = f32[4,256,256]{2,1,0:T(8,128)S(1)} custom-call(s32[4]{0:T(128)} %pad_add_fusion.place_ref, bf16[256,512]{1,0:T(8,128)(2,1)S(1)} %gated_both.1.gated_ref, bf16[256,4096]{1,0:T(8,128)(2,1)} %refs_9_.3, f32[128,2048]{1,0:T(8,128)} %collective-permute-done.1.refs_1_.refs_4_.refs_7_.refs_10_, ...), custom_call_target="tpu_custom_call" | custom-call | tf_op jit(solution)/shard_map/project_leaving/pallas_call | solution.py:286
  46.6 5.1 %collective-permute-start.3 = (f32[4,256,256]{2,1,0:T(8,128)S(1)}, f32[4,256,256]{2,1,0:T(8,128)S(1)}, u32[]{:S(2)}, u32[]{:S(2)}) collective-permute-start(f32[4,256,256]{2,1,0:T(8,128)S(1)} %project_leaving.1), channel_id=1, source_target_pairs={{0,32},{1,225},{32,0},{33,65},{64,96},{65,33},{96,64},{97,129},{12... | collective-permute-start | bytes 3145736 | tf_op jit(solution)/shard_map/ppermute | solution.py:345
  51.7 2.7 %project_kept.1 = f32[4,256,256]{2,1,0:T(8,128)S(1)} custom-call(s32[4]{0:T(128)} %pad_add_fusion.place_ref, bf16[256,512]{1,0:T(8,128)(2,1)S(1)} %gated_both.1.gated_ref, bf16[256,4096]{1,0:T(8,128)(2,1)} %refs_9_.3, f32[128,2048]{1,0:T(8,128)} %collective-permute-done.1.refs_1_.refs_4_.refs_7_.refs_10_, ...), custom_call_target="tpu_custom_call" | custom-call | tf_op jit(solution)/shard_map/project_kept/pallas_call | solution.py:286
  54.4 9.5 %collective-permute-done.3 = f32[4,256,256]{2,1,0:T(8,128)S(1)} collective-permute-done((f32[4,256,256]{2,1,0:T(8,128)S(1)}, f32[4,256,256]{2,1,0:T(8,128)S(1)}, u32[]{:S(2)}, u32[]{:S(2)}) %collective-permute-start.3) | collective-permute-done | bytes 1048608 | tf_op jit(solution)/shard_map/ppermute | solution.py:345
  63.9 0.1 add.46
  64.0 0.1 dynamic-slice_bitcast_fusion.2
  64.1 6.9 %collective-permute-start.6 = (f32[256,256]{1,0:T(8,128)S(1)}, f32[256,256]{1,0:T(8,128)S(1)}, u32[]{:S(2)}, u32[]{:S(2)}) collective-permute-start(f32[256,256]{1,0:T(8,128)S(1)} %get-tuple-element.10), channel_id=1, source_target_pairs={{0,128},{64,192},{128,0},{192,64},{1,129},{65,193},{129,1},{193,65... | collective-permute-start | bytes 786440 | tf_op jit(solution)/shard_map/ppermute | solution.py:352
  71.1 1.9 %collective-permute-start.5 = (f32[256,256]{1,0:T(8,128)S(1)}, f32[256,256]{1,0:T(8,128)S(1)}, u32[]{:S(2)}, u32[]{:S(2)}) collective-permute-start(f32[256,256]{1,0:T(8,128)S(1)} %get-tuple-element.11), channel_id=1, source_target_pairs={{0,192},{64,0},{128,64},{192,128},{1,193},{65,1},{129,65},{193,129... | collective-permute-start | bytes 786440 | tf_op jit(solution)/shard_map/ppermute | solution.py:352
  73.0 4.3 %collective-permute-start.4 = (f32[256,256]{1,0:T(8,128)S(1)}, f32[256,256]{1,0:T(8,128)S(1)}, u32[]{:S(2)}, u32[]{:S(2)}) collective-permute-start(f32[256,256]{1,0:T(8,128)S(1)} %get-tuple-element.9), channel_id=1, source_target_pairs={{0,64},{64,128},{128,192},{192,0},{1,65},{65,129},{129,193},{193,1... | collective-permute-start | bytes 786440 | tf_op jit(solution)/shard_map/ppermute | solution.py:352
  77.3 6.3 %collective-permute-done.6 = f32[256,256]{1,0:T(8,128)S(1)} collective-permute-done((f32[256,256]{1,0:T(8,128)S(1)}, f32[256,256]{1,0:T(8,128)S(1)}, u32[]{:S(2)}, u32[]{:S(2)}) %collective-permute-start.6) | collective-permute-done | bytes 262176 | tf_op jit(solution)/shard_map/ppermute | solution.py:352
  83.6 11.1 %collective-permute-done.5 = f32[256,256]{1,0:T(8,128)S(1)} collective-permute-done((f32[256,256]{1,0:T(8,128)S(1)}, f32[256,256]{1,0:T(8,128)S(1)}, u32[]{:S(2)}, u32[]{:S(2)}) %collective-permute-start.5) | collective-permute-done | bytes 262176 | tf_op jit(solution)/shard_map/ppermute | solution.py:352
  94.6 0.0 collective-permute-done.4
  94.6 0.7 fusion.2
Async XLA Ops:
  1.1 23.6 %collective-permute-start.1 = (f32[128,2048]{1,0:T(8,128)S(1)}, f32[128,2048]{1,0:T(8,128)}, u32[]{:S(2)}, u32[]{:S(2)}) collective-permute-start(f32[128,2048]{1,0:T(8,128)S(1)} %dynamic-slice_convert_fusion), channel_id=1, source_target_pairs={{0,256},{1,259},{2,258},{3,257},{256,0},{257,3},{258,2},{259,1},{4... | collective-permute-start | bytes 3145736 | tf_op jit(solution)/shard_map/ppermute | solution.py:331
  8.5 21.6 %all-to-all-start = ((f32[16,16,256]{2,1,0:T(8,128)}), f32[16,16,256]{2,1,0:T(8,128)S(1)}, u32[]{:S(2)}, u32[]{:S(2)}) async-start(f32[16,16,256]{2,1,0:T(8,128)} %get-tuple-element.7.own_ref), calls=%async_computation | async-start | bytes 524288 | tf_op jit(solution)/shard_map/all_to_all | solution.py:336
  21.9 19.6 %collective-permute-start = (f32[544,256]{1,0:T(8,128)}, f32[544,256]{1,0:T(8,128)}, u32[]{:S(2)}, u32[]{:S(2)}) collective-permute-start(f32[544,256]{1,0:T(8,128)} %local_conv.1.own_ref), channel_id=1, source_target_pairs={{0,256},{256,0},{1,257},{257,1},{2,258},{258,2},{3,259},{259,3},{4... | collective-permute-start | bytes 1671176 | tf_op jit(solution)/shard_map/ppermute | solution.py:340
  24.7 19.2 %collective-permute-start.2 = (f32[128,2048]{1,0:T(8,128)}, f32[128,2048]{1,0:T(8,128)}, u32[]{:S(2)}, u32[]{:S(2)}) collective-permute-start(f32[128,2048]{1,0:T(8,128)} %collective-permute-done.1.refs_1_.refs_4_.refs_7_.refs_10_), channel_id=1, source_target_pairs={{0,1},{1,0},{2,3},{3,2},{4,5},{5,4},{6,7},{7,6},{8,9},{9,8},{10,11... | collective-permute-start | bytes 3145736 | tf_op jit(solution)/shard_map/ppermute | solution.py:332
  30.2 11.3 %copy-start = (f32[544,256]{1,0:T(8,128)S(1)}, f32[544,256]{1,0:T(8,128)}, u32[]{:S(2)}) copy-start(f32[544,256]{1,0:T(8,128)} %local_conv.1.own_ref) | copy-start | bytes 1671172
  46.6 17.3 %collective-permute-start.3 = (f32[4,256,256]{2,1,0:T(8,128)S(1)}, f32[4,256,256]{2,1,0:T(8,128)S(1)}, u32[]{:S(2)}, u32[]{:S(2)}) collective-permute-start(f32[4,256,256]{2,1,0:T(8,128)S(1)} %project_leaving.1), channel_id=1, source_target_pairs={{0,32},{1,225},{32,0},{33,65},{64,96},{65,33},{96,64},{97,129},{12... | collective-permute-start | bytes 3145736 | tf_op jit(solution)/shard_map/ppermute | solution.py:345
  64.1 19.4 %collective-permute-start.6 = (f32[256,256]{1,0:T(8,128)S(1)}, f32[256,256]{1,0:T(8,128)S(1)}, u32[]{:S(2)}, u32[]{:S(2)}) collective-permute-start(f32[256,256]{1,0:T(8,128)S(1)} %get-tuple-element.10), channel_id=1, source_target_pairs={{0,128},{64,192},{128,0},{192,64},{1,129},{65,193},{129,1},{193,65... | collective-permute-start | bytes 786440 | tf_op jit(solution)/shard_map/ppermute | solution.py:352
  71.1 23.6 %collective-permute-start.5 = (f32[256,256]{1,0:T(8,128)S(1)}, f32[256,256]{1,0:T(8,128)S(1)}, u32[]{:S(2)}, u32[]{:S(2)}) collective-permute-start(f32[256,256]{1,0:T(8,128)S(1)} %get-tuple-element.11), channel_id=1, source_target_pairs={{0,192},{64,0},{128,64},{192,128},{1,193},{65,1},{129,65},{193,129... | collective-permute-start | bytes 786440 | tf_op jit(solution)/shard_map/ppermute | solution.py:352
  73.0 21.6 %collective-permute-start.4 = (f32[256,256]{1,0:T(8,128)S(1)}, f32[256,256]{1,0:T(8,128)S(1)}, u32[]{:S(2)}, u32[]{:S(2)}) collective-permute-start(f32[256,256]{1,0:T(8,128)S(1)} %get-tuple-element.9), channel_id=1, source_target_pairs={{0,64},{64,128},{128,192},{192,0},{1,65},{65,129},{129,193},{193,1... | collective-permute-start | bytes 786440 | tf_op jit(solution)/shard_map/ppermute | solution.py:352
